TPU v7x, 512 devices: a whole 4x8x8 slice. The times are simulated.
512 devices in a mesh: group: 16 (over x_hi, y), shard: 32 (over x_lo, z, core).
Axes of the slice: x: 4 (x_hi: 2, x_lo: 2; x = x_hi * 2 + x_lo), y: 8, z: 8, core: 2. Of those that a mesh axis runs over, the one named last changes fastest.
Arguments:
- factors: bfloat16 [128, 6144, 1024], P('group', 'shard'), may hold values from -0.15625 to 0.15625
- amplitudes: bfloat16 [64, 32, 1024], P('group'), may hold values from -6 to 6
- factor_route: int32 [16, 16], P('group'), may hold values from 0 to 7
- amp_route: int32 [16, 16], P('group'), may hold values from 0 to 3
- task_list: int32 [16, 3, 4], P('group'), may hold values from 0 to 15
- target_tile: int32 [16, 16], P('group'), may hold values from 0 to 1
Outputs:
- residual: float32 [32, 32, 1024], P('group', None, 'shard')
Inputs may be any that keep to these rules, and one draw needn't show every extreme that they name: task_list[h, k] names the group that owns the residual tile and the groups that send the two factor blocks and the amplitude tile used by task k of helper group h.
All inputs are finite; a program needn't handle non-finite values.
Results may differ from a plain program's by a relative error of at most 0.0025.
Values may be sent and summed in bfloat16 or wider, within the bound.
No kernel may reach another device: no remote copies, remote signals or barrier semaphores. Data moves between devices by JAX's collectives and lax.ppermute only.
A program may use at most 128 MiB of HBM per device.

v0:
```python
import jax
import jax.numpy as jnp
from jax import lax
from jax.sharding import PartitionSpec as P

VB = 32
TPG = 2


def in_blocks(shard, dim, peers):
    shape = shard.shape
    pieces = shard.reshape(*shape[:dim], peers, shape[dim] // peers, *shape[dim + 1 :])
    return jnp.moveaxis(pieces, dim, 0)


def summed_on_arrival(shard, axis, dim):
    peers = lax.axis_size(axis)
    pieces = lax.all_to_all(in_blocks(shard, dim, peers), axis, 0, 0, tiled=True)
    return jnp.sum(pieces, axis=0)


def body(factors, amplitudes, factor_route, amp_route, task_list, target_tile):
    groups = lax.axis_size("group")
    width = factors.shape[2]
    occupied = amplitudes.shape[1]
    factor_send = jnp.take(factors, factor_route[0], axis=0)
    amp_send = jnp.take(amplitudes, amp_route[0], axis=0)
    factor_recv, amp_recv = (
        lax.all_to_all(factor_send, "group", split_axis=0, concat_axis=0, tiled=True),
        lax.all_to_all(amp_send, "group", split_axis=0, concat_axis=0, tiled=True),
    )

    def ladder_task(step_index, returns):
        record = task_list[0, step_index]
        left_block = factor_recv[record[1]]
        right_block = factor_recv[record[2]]
        amplitude = amp_recv[record[3]]
        products = lax.dot_general(
            left_block, right_block, (((0,), (0,)), ((), ())), preferred_element_type=jnp.float32
        )
        integral = products.reshape(VB, VB, VB, VB).transpose(0, 2, 1, 3).reshape(width, width)
        integral = integral.astype(jnp.bfloat16)
        contribution = lax.dot_general(
            amplitude, integral, (((1,), (1,)), ((), ())), preferred_element_type=jnp.float32
        )
        return returns.at[record[0]].add(contribution)

    returns = jnp.zeros((groups, occupied, width), jnp.float32)
    returns = lax.fori_loop(0, task_list.shape[1], ladder_task, returns)
    selector = (target_tile[0][None, :] == jnp.arange(TPG, dtype=jnp.int32)[:, None]).astype(
        jnp.float32
    )
    arrived = lax.all_to_all(returns, "group", split_axis=0, concat_axis=0, tiled=True)
    owned = jnp.einsum("th,hor->tor", selector, arrived, precision=lax.Precision.HIGHEST)
    return summed_on_arrival(owned, "shard", 2)


def solution(mesh):
    return jax.shard_map(
        body,
        mesh=mesh,
        in_specs=(
            P("group", "shard", None),
            P("group", None, None),
            P("group", None),
            P("group", None),
            P("group", None, None),
            P("group", None),
        ),
        out_specs=P("group", None, "shard"),
        check_vma=False,
    )
```

profile of v0, /device:TPU:1, one launch (start us, length us, event | category | flops | bytes accessed | tf_op | source)
XLA Modules:
  0.0 391.1 jit_solution(6985798561303161442)
XLA Ops:
  0.0 0.0 copy-start
  0.0 0.8 fusion.12
  0.8 0.8 compare_and_fusion
  1.6 0.3 copy-done
  1.9 3.6 gather_fusion.1
  5.5 6.1 %broadcast_select_fusion = bf16[16,192,1024]{2,1,0:T(8,128)(2,1)} fusion(bf16[16,192,1024]{2,1,0:T(8,128)(2,1)} %gather_fusion.1, pred[16]{0:T(512)(128)(4,1)S(1)} %compare_and_fusion), kind=kLoop, calls=%fused_computation.14 | loop fusion | flops 3145728 | bytes 12582928 | tf_op jit(solution)/shard_map/jit(_take)/select_n | solution.py:26
  11.6 10.4 %all-to-all-start.1 = ((bf16[16,192,1024]{2,1,0:T(8,128)(2,1)}), bf16[16,192,1024]{2,1,0:T(8,128)(2,1)}, u32[]{:S(2)}, u32[]{:S(2)}) async-start(bf16[16,192,1024]{2,1,0:T(8,128)(2,1)} %broadcast_select_fusion), calls=%async_computation.1 | async-start | bytes 12582912 | tf_op jit(solution)/shard_map/all_to_all | solution.py:29
  22.0 1.6 gather_fusion
  23.6 2.4 broadcast_select_fusion.1
  26.0 137.2 %all-to-all-done.1 = bf16[16,192,1024]{2,1,0:T(8,128)(2,1)} async-done(((bf16[16,192,1024]{2,1,0:T(8,128)(2,1)}), bf16[16,192,1024]{2,1,0:T(8,128)(2,1)}, u32[]{:S(2)}, u32[]{:S(2)}) %all-to-all-start.1) | async-done | bytes 6291488 | tf_op jit(solution)/shard_map/all_to_all | solution.py:29
  163.2 9.6 %all-to-all-start = ((bf16[16,32,1024]{2,1,0:T(8,128)(2,1)}), bf16[16,32,1024]{2,1,0:T(8,128)(2,1)}, u32[]{:S(2)}, u32[]{:S(2)}) async-start(bf16[16,32,1024]{2,1,0:T(8,128)(2,1)} %broadcast_select_fusion.1), calls=%async_computation | async-start | bytes 2097152 | tf_op jit(solution)/shard_map/all_to_all | solution.py:30
  172.8 0.0 copy-start.2
  172.9 11.1 %copy.10 = bf16[16,192,1024]{1,2,0:T(8,128)(2,1)} copy(bf16[16,192,1024]{2,1,0:T(8,128)(2,1)} %all-to-all-done.1) | data formatting | bytes 12582912 | tf_op jit(solution)/shard_map/while | solution.py:49
  183.9 16.1 %all-to-all-done = bf16[16,32,1024]{2,1,0:T(8,128)(2,1)} async-done(((bf16[16,32,1024]{2,1,0:T(8,128)(2,1)}), bf16[16,32,1024]{2,1,0:T(8,128)(2,1)}, u32[]{:S(2)}, u32[]{:S(2)}) %all-to-all-start) | async-done | bytes 1048608 | tf_op jit(solution)/shard_map/all_to_all | solution.py:30
  200.0 1.6 broadcast_in_dim.27
  201.5 94.1 %while.14 = (s32[]{:T(128)}, f32[16,32,1024]{2,1,0:T(8,128)}, s32[1,3,4]{2,0,1:T(1,128)}, bf16[16,32,1024]{2,1,0:T(8,128)(2,1)}, bf16[16,192,1024]{1,2,0:T(8,128...) while((s32[]{:T(128)}, f32[16,32,1024]{2,1,0:T(8,128)}, ...), condition=%wide.region_2.3_spmd, body=%wide.region_0.0_spmd.sunk | while | flops 470876192 | bytes 11076946 | solution.py:49
  201.5 0.7 constant_dynamic-slice_fusion.5
  202.2 0.7 fusion.29
  206.5 1.3 constant_dynamic-slice_fusion.6
  207.8 4.6 %convert_bitcast_fusion.2 = bf16[32,32,32,32]{3,2,1,0:T(8,128)(2,1)} fusion(bf16[32,32,192,1]{2,1,3,0:T(8,128)(2,1)S(1)} %bitcast.94, bf16[32,32,192,1]{2,1,0,3:T(8,128)(2,1)S(1)} %bitcast.93), kind=kOutput, calls=%fused_computation.2.clone.1 | convolution fusion | flops 403701760 | bytes 2883584 | tf_op jit(solution)/shard_map/while/body/eval_jaxpr/dot_general | solution.py:38
  212.4 12.4 %convert_element_type.18 = bf16[1024,1024]{1,0:T(8,128)(2,1)} reshape(bf16[32,32,32,32]{3,2,1,0:T(8,128)(2,1)} %convert_bitcast_fusion.2) | data formatting | bytes 4194304 | tf_op jit(solution)/shard_map/while/body/eval_jaxpr/convert_element_type | solution.py:42
  226.6 0.8 and_reduce_fusion.2
  229.3 3.6 fusion.30
  232.9 0.7 constant_dynamic-slice_fusion.5
  233.6 0.7 fusion.29
  237.9 1.3 constant_dynamic-slice_fusion.6
  239.2 4.6 %convert_bitcast_fusion.2 = bf16[32,32,32,32]{3,2,1,0:T(8,128)(2,1)} fusion(bf16[32,32,192,1]{2,1,3,0:T(8,128)(2,1)S(1)} %bitcast.94, bf16[32,32,192,1]{2,1,0,3:T(8,128)(2,1)S(1)} %bitcast.93), kind=kOutput, calls=%fused_computation.2.clone.1 | convolution fusion | flops 403701760 | bytes 2883584 | tf_op jit(solution)/shard_map/while/body/eval_jaxpr/dot_general | solution.py:38
  243.8 12.4 %convert_element_type.18 = bf16[1024,1024]{1,0:T(8,128)(2,1)} reshape(bf16[32,32,32,32]{3,2,1,0:T(8,128)(2,1)} %convert_bitcast_fusion.2) | data formatting | bytes 4194304 | tf_op jit(solution)/shard_map/while/body/eval_jaxpr/convert_element_type | solution.py:42
  258.0 0.8 and_reduce_fusion.2
  260.6 3.7 fusion.30
  264.3 0.7 constant_dynamic-slice_fusion.5
  264.9 0.7 fusion.29
  269.2 1.3 constant_dynamic-slice_fusion.6
  270.5 4.6 %convert_bitcast_fusion.2 = bf16[32,32,32,32]{3,2,1,0:T(8,128)(2,1)} fusion(bf16[32,32,192,1]{2,1,3,0:T(8,128)(2,1)S(1)} %bitcast.94, bf16[32,32,192,1]{2,1,0,3:T(8,128)(2,1)S(1)} %bitcast.93), kind=kOutput, calls=%fused_computation.2.clone.1 | convolution fusion | flops 403701760 | bytes 2883584 | tf_op jit(solution)/shard_map/while/body/eval_jaxpr/dot_general | solution.py:38
  275.1 12.4 %convert_element_type.18 = bf16[1024,1024]{1,0:T(8,128)(2,1)} reshape(bf16[32,32,32,32]{3,2,1,0:T(8,128)(2,1)} %convert_bitcast_fusion.2) | data formatting | bytes 4194304 | tf_op jit(solution)/shard_map/while/body/eval_jaxpr/convert_element_type | solution.py:42
  289.3 0.8 and_reduce_fusion.2
  292.0 3.7 fusion.30
  295.6 55.0 %all_to_all.20 = f32[16,32,1024]{2,1,0:T(8,128)S(1)} all-to-all(f32[16,32,1024]{2,1,0:T(8,128)} %get-tuple-element.121), channel_id=1, replica_groups=mesh['group'=16,'shard'=32] {'group'}, dimensions={0} | all-to-all | bytes 4194304 | tf_op jit(solution)/shard_map/all_to_all | solution.py:53
  350.6 2.0 fusion.6
  352.6 1.4 reshape.154
  354.1 3.0 copy.22
  357.1 2.3 reshape.174
  359.4 24.9 %all_to_all.21 = f32[32,1,2048]{2,1,0:T(1,128)} all-to-all(f32[32,1,2048]{2,1,0:T(1,128)S(1)} %reshape.174), channel_id=1, replica_groups=mesh['group'=16,'shard'=32] {'shard'}, dimensions={0} | all-to-all | bytes 524288 | tf_op jit(solution)/shard_map/all_to_all | solution.py:18
  384.3 0.5 broadcast.103
  384.8 2.2 reduce.11
  387.0 1.9 reshape.175
  388.9 1.6 bitcast_reduce_fusion
  390.5 0.6 copy.14
  (11 shorter events, 0.0 us)
Async XLA Ops:
  0.0 1.9 copy-start
  11.6 10.4 %copy-start.4 = (s32[1,16]{1,0:T(1,128)S(1)}, s32[1,16]{1,0:T(1,128)}, u32[]{:S(2)}) copy-start(s32[1,16]{1,0:T(1,128)} %param.13) | copy-start | bytes 196
  11.6 10.4 %copy-start.1 = (bf16[4,32,1024]{2,1,0:T(8,128)(2,1)S(1)}, bf16[4,32,1024]{2,1,0:T(8,128)(2,1)}, u32[]{:S(2)}) copy-start(bf16[4,32,1024]{2,1,0:T(8,128)(2,1)} %param.11) | copy-start | bytes 786436
  11.6 151.6 %all-to-all-start.1 = ((bf16[16,192,1024]{2,1,0:T(8,128)(2,1)}), bf16[16,192,1024]{2,1,0:T(8,128)(2,1)}, u32[]{:S(2)}, u32[]{:S(2)}) async-start(bf16[16,192,1024]{2,1,0:T(8,128)(2,1)} %broadcast_select_fusion), calls=%async_computation.1 | async-start | bytes 12582912 | tf_op jit(solution)/shard_map/all_to_all | solution.py:29
  163.2 36.8 %all-to-all-start = ((bf16[16,32,1024]{2,1,0:T(8,128)(2,1)}), bf16[16,32,1024]{2,1,0:T(8,128)(2,1)}, u32[]{:S(2)}, u32[]{:S(2)}) async-start(bf16[16,32,1024]{2,1,0:T(8,128)(2,1)} %broadcast_select_fusion.1), calls=%async_computation | async-start | bytes 2097152 | tf_op jit(solution)/shard_map/all_to_all | solution.py:30
  172.8 28.7 %copy-start.2 = (s32[3]{0:T(128)S(1)}, s32[3]{0:T(128)}, u32[]{:S(2)}) copy-start(s32[3]{0:T(128)} %constant.95.clone.1) | copy-start | bytes 40
  295.6 55.0 %copy-start.3 = (s32[1,16]{1,0:T(1,128)S(1)}, s32[1,16]{1,0:T(1,128)}, u32[]{:S(2)}) copy-start(s32[1,16]{1,0:T(1,128)} %param.15) | copy-start | bytes 196
where the time goes:
time: 393 us; the launch traced here: 391 us
  waiting for transfers between devices  153 us (39%)
  blocking collectives  79.9 us (20%)
  local copies, waits for them, and re-layouts  72.8 us (19%)
  matrix products  26.8 us (7%)
  loops' own time  22.1 us (6%)
  starting transfers between devices  20 us (5%)
  other arithmetic  16.3 us (4%)
    all_to_all x1, waiting for transfers between devices, body(): lax.all_to_all(factor_send, 'group', split_axis=0, concat_axis=0, tiled=T...  137 us
    all_to_all x1, blocking collectives, body(): lax.all_to_all(returns, 'group', split_axis=0, concat_axis=0, tiled=True)  55 us
    convert_element_type x3, local copies, waits for them, and re-layouts, ladder_task(): integral = integral.astype(jnp.bfloat16)  37.1 us
    all_to_all x1, blocking collectives, summed_on_arrival(): lax.all_to_all(in_blocks(shard, dim, peers), axis, 0, 0, tiled=True)  24.9 us
    another operation x1, loops' own time, body(): returns = lax.fori_loop(0, task_list.shape[1], ladder_task, returns)  22.1 us
    all_to_all x1, waiting for transfers between devices, body(): lax.all_to_all(amp_send, 'group', split_axis=0, concat_axis=0, tiled=True)  16.1 us
    dot_general x3, matrix products, ladder_task(): lax.dot_general(left_block, right_block, (((0,), (0,)), ((), ())), prefer...  13.8 us
    while x1, local copies, waits for them, and re-layouts, body(): returns = lax.fori_loop(0, task_list.shape[1], ladder_task, returns)  11.1 us
  transfers between devices with their start and end apart: 2, of which 2 were waited for; matrix products, arithmetic and copies ran while one was open for 4% of the time, Pallas kernels for 0%

commit v1 on v0

v1 whole, which is shorter than its diff:
```python
import functools

import jax
import jax.numpy as jnp
from jax import lax
from jax.experimental import pallas as pl
from jax.experimental.pallas import tpu as pltpu
from jax.sharding import PartitionSpec as P

VB = 32
TPG = 2
LANES = 128
FOLD = LANES // VB


def swap_lane_blocks(tiles):
    lane = lax.broadcasted_iota(jnp.int32, tiles[0].shape, 1)
    x0, x1, x2, x3 = tiles
    low = lane < 2 * VB
    y0 = jnp.where(low, x0, pltpu.roll(x2, 2 * VB, 1))
    y2 = jnp.where(low, pltpu.roll(x0, 2 * VB, 1), x2)
    y1 = jnp.where(low, x1, pltpu.roll(x3, 2 * VB, 1))
    y3 = jnp.where(low, pltpu.roll(x1, 2 * VB, 1), x3)
    even = lane % (2 * VB) < VB
    z0 = jnp.where(even, y0, pltpu.roll(y1, VB, 1))
    z1 = jnp.where(even, pltpu.roll(y0, LANES - VB, 1), y1)
    z2 = jnp.where(even, y2, pltpu.roll(y3, VB, 1))
    z3 = jnp.where(even, pltpu.roll(y2, LANES - VB, 1), y3)
    return z0, z1, z2, z3


def ladder_kernel(record, left, right, amp, swap, out, folded, result):
    width = left.shape[2]
    occupied = amp.shape[1]
    per_pass = 2 * FOLD
    span = per_pass * VB
    right_t = jnp.dot(right[0], swap[...], preferred_element_type=jnp.float32).astype(jnp.bfloat16)
    amp_t = jnp.dot(amp[0], swap[...], preferred_element_type=jnp.float32).astype(jnp.bfloat16)
    for step in range(VB // per_pass):
        columns = slice(step * span, (step + 1) * span)
        integral = lax.dot_general(
            left[0, :, columns], right_t, (((0,), (0,)), ((), ())), preferred_element_type=jnp.float32
        )
        for half in range(2):
            for part in range(width // LANES):
                lanes = slice(part * LANES, (part + 1) * LANES)
                rows = half * FOLD * VB
                tiles = [integral[rows + a * VB : rows + (a + 1) * VB, lanes] for a in range(FOLD)]
                for d, tile in enumerate(swap_lane_blocks(tiles)):
                    base = (part * FOLD + d) * VB
                    folded[base : base + VB, half * LANES : (half + 1) * LANES] = tile.astype(jnp.bfloat16)
        result[:, columns] = jnp.dot(amp_t, folded[...], preferred_element_type=jnp.float32)
    band = occupied // FOLD
    for group in range(width // LANES):
        lanes = slice(group * LANES, (group + 1) * LANES)
        tiles = [result[i * band : (i + 1) * band, lanes] for i in range(FOLD)]
        for a, tile in enumerate(swap_lane_blocks(tiles)):
            out[group * FOLD + a, 0] = tile


def ladder(records, factors, amps):
    tasks = records.shape[0]
    rows, width = factors.shape[1:]
    occupied = amps.shape[1]
    index = jnp.arange(width, dtype=jnp.int32)
    swap = (
        (index[:, None] // VB == index[None, :] % VB) & (index[:, None] % VB == index[None, :] // VB)
    ).astype(jnp.bfloat16)
    band = occupied // FOLD
    return pl.pallas_call(
        ladder_kernel,
        grid_spec=pltpu.PrefetchScalarGridSpec(
            num_scalar_prefetch=1,
            grid=(tasks,),
            in_specs=[
                pl.BlockSpec((1, rows, width), lambda k, rec: (rec[k, 1], 0, 0)),
                pl.BlockSpec((1, rows, width), lambda k, rec: (rec[k, 2], 0, 0)),
                pl.BlockSpec((1, occupied, width), lambda k, rec: (rec[k, 3], 0, 0)),
                pl.BlockSpec((width, width), lambda k, rec: (0, 0)),
            ],
            out_specs=pl.BlockSpec((VB, 1, band, LANES), lambda k, rec: (0, k, 0, 0)),
            scratch_shapes=[
                pltpu.VMEM((width, 2 * LANES), jnp.bfloat16),
                pltpu.VMEM((occupied, width), jnp.float32),
            ],
        ),
        out_shape=jax.ShapeDtypeStruct((VB, tasks, band, LANES), jnp.float32),
        compiler_params=pltpu.CompilerParams(dimension_semantics=("arbitrary",)),
        name="ladder",
    )(records, factors, factors, amps, swap)


def combine_kernel(record, pieces, out):
    tasks = record.shape[0]
    total = jnp.sum(pieces[...], axis=0)
    out[...] = jnp.zeros_like(out)
    for k in range(tasks):
        owner = record[k, 0]
        out[owner] += total[k]


def combine(records, pieces, groups):
    return pl.pallas_call(
        combine_kernel,
        in_specs=[pl.BlockSpec(memory_space=pltpu.SMEM), pl.BlockSpec(memory_space=pltpu.VMEM)],
        out_specs=pl.BlockSpec(memory_space=pltpu.VMEM),
        out_shape=jax.ShapeDtypeStruct((groups, *pieces.shape[2:]), jnp.float32),
        name="combine",
    )(records, pieces)


def owned_kernel(tile, arrived, out, total):
    groups, band, lanes = arrived.shape
    total[...] = jnp.zeros_like(total)
    for h in range(groups):
        total[tile[h]] += arrived[h]
    for t in range(TPG):
        for i in range(FOLD):
            out[t, i * band : (i + 1) * band, :] = total[t][:, i * VB : (i + 1) * VB]


def owned(tile, arrived):
    groups, band, lanes = arrived.shape
    return pl.pallas_call(
        owned_kernel,
        in_specs=[pl.BlockSpec(memory_space=pltpu.SMEM), pl.BlockSpec(memory_space=pltpu.VMEM)],
        out_specs=pl.BlockSpec(memory_space=pltpu.VMEM),
        out_shape=jax.ShapeDtypeStruct((TPG, band * FOLD, VB), jnp.float32),
        scratch_shapes=[pltpu.VMEM((TPG, band, lanes), jnp.float32)],
        name="owned",
    )(tile, arrived)


def body(factors, amplitudes, factor_route, amp_route, task_list, target_tile):
    groups = lax.axis_size("group")
    records = task_list[0]
    factor_send = factors.at[factor_route[0]].get(mode="promise_in_bounds")
    amp_send = amplitudes.at[amp_route[0]].get(mode="promise_in_bounds")
    amp_recv = lax.all_to_all(amp_send, "group", split_axis=0, concat_axis=0, tiled=True)
    factor_recv = lax.all_to_all(factor_send, "group", split_axis=0, concat_axis=0, tiled=True)
    parts = ladder(records, factor_recv, amp_recv)
    pieces = lax.all_to_all(parts, "shard", split_axis=0, concat_axis=0, tiled=True)
    returns = combine(records, pieces, groups)
    arrived = lax.all_to_all(returns, "group", split_axis=0, concat_axis=0, tiled=True)
    return owned(target_tile[0], arrived)


def solution(mesh):
    return jax.shard_map(
        body,
        mesh=mesh,
        in_specs=(
            P("group", "shard", None),
            P("group", None, None),
            P("group", None),
            P("group", None),
            P("group", None, None),
            P("group", None),
        ),
        out_specs=P("group", None, "shard"),
        check_vma=False,
    )
```

time: 393 us -> 259 us (0.66)
  the two profiles are of different devices: /device:TPU:1 before, /device:TPU:8 now
where the time goes in v1:
time: 259 us; the launch traced here: 258 us
  waiting for transfers between devices  163 us (63%)
  blocking collectives  46.4 us (18%)
  Pallas kernels  24.1 us (9%)
  starting transfers between devices  15.4 us (6%)
  local copies, waits for them, and re-layouts  6.92 us (3%)
  other arithmetic  2.79 us (1%)
    all_to_all x1, waiting for transfers between devices, body(): lax.all_to_all(factor_send, 'group', split_axis=0, concat_axis=0, tiled=T...  138 us
    all_to_all x1, blocking collectives, body(): lax.all_to_all(parts, 'shard', split_axis=0, concat_axis=0, tiled=True)  26.7 us
    all_to_all x1, waiting for transfers between devices, body(): lax.all_to_all(amp_send, 'group', split_axis=0, concat_axis=0, tiled=True)  24.2 us
    pallas_call x1, Pallas kernels, ladder(): pl.pallas_call(ladder_kernel, grid_spec=pltpu.PrefetchScalarGridSpec(num_...  20.8 us
    all_to_all x1, blocking collectives, body(): lax.all_to_all(returns, 'group', split_axis=0, concat_axis=0, tiled=True)  19.8 us
    all_to_all x1, starting transfers between devices, body(): lax.all_to_all(amp_send, 'group', split_axis=0, concat_axis=0, tiled=True)  10 us
    all_to_all x1, starting transfers between devices, body(): lax.all_to_all(factor_send, 'group', split_axis=0, concat_axis=0, tiled=T...  5.4 us
  transfers between devices with their start and end apart: 2, of which 2 were waited for; matrix products, arithmetic and copies ran while one was open for 2% of the time, Pallas kernels for 0%

profile of v1, /device:TPU:8, one launch (start us, length us, event | category | flops | bytes accessed | tf_op | source)
XLA Modules:
  0.0 258.3 jit_solution(4061011692592841932)
XLA Ops:
  0.0 0.0 copy-start
  0.0 0.0 copy-start.2
  0.0 0.8 fusion.8
  0.8 2.7 %gather_fusion.1 = bf16[16,32,1024]{2,1,0:T(8,128)(2,1)} fusion(bf16[4,32,1024]{2,1,0:T(8,128)(2,1)} %param.7, s32[1024]{0:T(1024)S(1)} %pad_clamp_fusion), kind=kCustom, calls=%fused_computation.1 | custom fusion | bytes 2097216 | tf_op jit(solution)/shard_map/gather | solution.py:138
  3.6 10.0 %all-to-all-start.1 = ((bf16[16,32,1024]{2,1,0:T(8,128)(2,1)}), bf16[16,32,1024]{2,1,0:T(8,128)(2,1)}, u32[]{:S(2)}, u32[]{:S(2)}) async-start(bf16[16,32,1024]{2,1,0:T(8,128)(2,1)} %gather_fusion.1), calls=%async_computation.1 | async-start | bytes 2097152 | tf_op jit(solution)/shard_map/all_to_all | solution.py:139
  13.6 0.0 copy-done.2
  13.6 0.0 copy-done
  13.6 3.6 %gather_fusion = bf16[16,192,1024]{2,1,0:T(8,128)(2,1)} fusion(bf16[8,192,1024]{2,1,0:T(8,128)(2,1)S(1)} %copy-done, s32[1024]{0:T(1024)S(1)} %pad_clamp_fusion.1), kind=kCustom, calls=%fused_computation | custom fusion | bytes 12582976 | tf_op jit(solution)/shard_map/gather | solution.py:137
  17.2 0.0 copy-start.1
  17.2 24.2 %all-to-all-done.1.amp = bf16[16,32,1024]{2,1,0:T(8,128)(2,1)} async-done(((bf16[16,32,1024]{2,1,0:T(8,128)(2,1)}), bf16[16,32,1024]{2,1,0:T(8,128)(2,1)}, u32[]{:S(2)}, u32[]{:S(2)}) %all-to-all-start.1) | async-done | bytes 1048608 | tf_op jit(solution)/shard_map/all_to_all | solution.py:139
  41.4 5.4 %all-to-all-start = ((bf16[16,192,1024]{2,1,0:T(8,128)(2,1)}), bf16[16,192,1024]{2,1,0:T(8,128)(2,1)}, u32[]{:S(2)}, u32[]{:S(2)}) async-start(bf16[16,192,1024]{2,1,0:T(8,128)(2,1)} %gather_fusion), calls=%async_computation | async-start | bytes 12582912 | tf_op jit(solution)/shard_map/all_to_all | solution.py:140
  46.8 0.0 copy-done.1
  46.8 0.6 copy.9
  47.4 1.9 and_convert_fusion.swap
  49.3 138.4 %all-to-all-done.left.right = bf16[16,192,1024]{2,1,0:T(8,128)(2,1)} async-done(((bf16[16,192,1024]{2,1,0:T(8,128)(2,1)}), bf16[16,192,1024]{2,1,0:T(8,128)(2,1)}, u32[]{:S(2)}, u32[]{:S(2)}) %all-to-all-start) | async-done | bytes 6291488 | tf_op jit(solution)/shard_map/all_to_all | solution.py:140
  187.8 20.8 %ladder.1 = f32[32,3,8,128]{3,2,1,0:T(8,128)} custom-call(s32[3,4]{1,0:T(4,128)} %bitcast.12, bf16[16,192,1024]{2,1,0:T(8,128)(2,1)} %all-to-all-done.left.right, bf16[16,192,1024]{2,1,0:T(8,128)(2,1)} %all-to-all-done.left.right, bf16[16,32,1024]{2,1,0:T(8,128)(2,1)} %all-to-all-done.1.amp, bf16[1024,1024]{1,0:T(8,128)(2,1)} %and_convert_fusion.swap), custom_call_target="tpu_custom_call" | custom-call | tf_op jit(solution)/shard_map/ladder/pallas_call | solution.py:70
  208.5 26.7 %all_to_all.20.pieces = f32[32,3,8,128]{3,2,1,0:T(8,128)} all-to-all(f32[32,3,8,128]{3,2,1,0:T(8,128)} %ladder.1), channel_id=1, replica_groups=mesh['group'=16,'shard'=32] {'shard'}, dimensions={0} | all-to-all | bytes 786432 | tf_op jit(solution)/shard_map/all_to_all | solution.py:142
  235.2 1.7 combine.1
  236.9 19.8 %all_to_all.21.arrived = f32[16,8,128]{2,1,0:T(8,128)} all-to-all(f32[16,8,128]{2,1,0:T(8,128)} %combine.1), channel_id=1, replica_groups=mesh['group'=16,'shard'=32] {'group'}, dimensions={0} | all-to-all | bytes 131072 | tf_op jit(solution)/shard_map/all_to_all | solution.py:144
  256.6 1.6 owned.1
  (4 shorter events, 0.0 us)
Async XLA Ops:
  0.0 13.6 %copy-start = (bf16[8,192,1024]{2,1,0:T(8,128)(2,1)S(1)}, bf16[8,192,1024]{2,1,0:T(8,128)(2,1)}, u32[]{:S(2)}) copy-start(bf16[8,192,1024]{2,1,0:T(8,128)(2,1)} %param.6) | copy-start | bytes 9437188
  0.0 13.6 %copy-start.2 = (s32[1,16]{1,0:T(1,128)S(1)}, s32[1,16]{1,0:T(1,128)}, u32[]{:S(2)}) copy-start(s32[1,16]{1,0:T(1,128)} %param.8) | copy-start | bytes 196
  3.6 37.8 %all-to-all-start.1 = ((bf16[16,32,1024]{2,1,0:T(8,128)(2,1)}), bf16[16,32,1024]{2,1,0:T(8,128)(2,1)}, u32[]{:S(2)}, u32[]{:S(2)}) async-start(bf16[16,32,1024]{2,1,0:T(8,128)(2,1)} %gather_fusion.1), calls=%async_computation.1 | async-start | bytes 2097152 | tf_op jit(solution)/shard_map/all_to_all | solution.py:139
  17.2 29.6 %copy-start.1 = (s32[1,3,4]{2,0,1:T(1,128)S(1)}, s32[1,3,4]{2,0,1:T(1,128)}, u32[]{:S(2)}) copy-start(s32[1,3,4]{2,0,1:T(1,128)} %param.10) | copy-start | bytes 148
  41.4 146.4 %all-to-all-start = ((bf16[16,192,1024]{2,1,0:T(8,128)(2,1)}), bf16[16,192,1024]{2,1,0:T(8,128)(2,1)}, u32[]{:S(2)}, u32[]{:S(2)}) async-start(bf16[16,192,1024]{2,1,0:T(8,128)(2,1)} %gather_fusion), calls=%async_computation | async-start | bytes 12582912 | tf_op jit(solution)/shard_map/all_to_all | solution.py:140

commit v2 on v1

--- a/solution.py
+++ b/solution.py
@@ -75,7 +75,7 @@
             in_specs=[
                 pl.BlockSpec((1, rows, width), lambda k, rec: (rec[k, 1], 0, 0)),
                 pl.BlockSpec((1, rows, width), lambda k, rec: (rec[k, 2], 0, 0)),
-                pl.BlockSpec((1, occupied, width), lambda k, rec: (rec[k, 3], 0, 0)),
+                pl.BlockSpec((1, occupied, width), lambda k, rec: (k, 0, 0)),
                 pl.BlockSpec((width, width), lambda k, rec: (0, 0)),
             ],
             out_specs=pl.BlockSpec((VB, 1, band, LANES), lambda k, rec: (0, k, 0, 0)),
@@ -131,14 +131,45 @@
     )(tile, arrived)
 
 
+def spread(block, axis):
+    members = lax.axis_size(axis)
+    me = lax.axis_index(axis)
+    held = block[None]
+    bit = 1
+    while bit < members:
+        other = lax.ppermute(held, axis, [(i, i ^ bit) for i in range(members)])
+        mine_first = (me & bit) == 0
+        held = jnp.where(
+            mine_first, jnp.concatenate([held, other]), jnp.concatenate([other, held])
+        )
+        bit *= 2
+    return held
+
+
+def amplitude_tiles(records, amplitudes, amp_route):
+    group, shard = lax.axis_index("group"), lax.axis_index("shard")
+    tiles, _, width = amplitudes.shape
+    tasks = records.shape[0]
+    rows = lax.dynamic_index_in_dim(amplitudes, shard, 1, keepdims=False)
+    route = jnp.pad(amp_route[0], (0, width - amp_route.shape[1])).astype(rows.dtype)
+    block = jnp.concatenate([rows, route[None], jnp.zeros((8 - tiles - 1, width), rows.dtype)])
+    held = spread(block, "group")
+    source = records[:, 3]
+    routes = held[:, tiles, : amp_route.shape[1]].astype(jnp.int32)[:, group]
+    picked = [
+        lax.dynamic_slice(held, (source[k], routes[source[k]], 0), (1, 1, width))[0, 0] for k in range(tasks)
+    ]
+    whole = spread(jnp.stack(picked), "shard")
+    return whole.transpose(1, 0, 2)
+
+
 def body(factors, amplitudes, factor_route, amp_route, task_list, target_tile):
     groups = lax.axis_size("group")
     records = task_list[0]
     factor_send = factors.at[factor_route[0]].get(mode="promise_in_bounds")
-    amp_send = amplitudes.at[amp_route[0]].get(mode="promise_in_bounds")
-    amp_recv = lax.all_to_all(amp_send, "group", split_axis=0, concat_axis=0, tiled=True)
+    amps = amplitude_tiles(records, amplitudes, amp_route)
     factor_recv = lax.all_to_all(factor_send, "group", split_axis=0, concat_axis=0, tiled=True)
-    parts = ladder(records, factor_recv, amp_recv)
+    parts = ladder(records, factor_recv, amps)
     pieces = lax.all_to_all(parts, "shard", split_axis=0, concat_axis=0, tiled=True)
     returns = combine(records, pieces, groups)
     arrived = lax.all_to_all(returns, "group", split_axis=0, concat_axis=0, tiled=True)

time: 259 us -> 295 us (1.14)
  starting transfers between devices: 15.4 us -> 54.5 us
  waiting for transfers between devices: 163 us -> 151 us
  between operations: 0.04 us -> 11.5 us
  blocking collectives: 46.4 us -> 41.5 us
    ppermute x0 -> x9, waiting for transfers between devices: none -> 151 us  [spread(): other = lax.ppermute(held, axis, [(i, i ^ bit) for i in range(members)])]
    all_to_all x1, waiting for transfers between devices: 138 us -> 0.01 us  [body(): lax.all_to_all(factor_send, 'group', split_axis=0, concat_axis=0, tiled=T...]
    ppermute x0 -> x9, starting transfers between devices: none -> 44.2 us  [spread(): other = lax.ppermute(held, axis, [(i, i ^ bit) for i in range(members)])]
    all_to_all x1 -> x0, waiting for transfers between devices: 24.2 us -> none  [body(): lax.all_to_all(amp_send, 'group', split_axis=0, concat_axis=0, tiled=True)]
    all_to_all x1 -> x0, starting transfers between devices: 10 us -> none  [body(): lax.all_to_all(amp_send, 'group', split_axis=0, concat_axis=0, tiled=True)]
    all_to_all x1, starting transfers between devices: 5.4 us -> 10.3 us  [body(): lax.all_to_all(factor_send, 'group', split_axis=0, concat_axis=0, tiled=T...]
  transfers between devices with their start and end apart: 2 -> 10, of which waited for: 2 -> 8; matrix products, arithmetic and copies ran while one was open for 2% -> 2% of each run, Pallas kernels for 0% -> 0%
where the time goes in v2:
time: 295 us; the launch traced here: 294 us
  waiting for transfers between devices  151 us (51%)
  starting transfers between devices  54.5 us (18%)
  blocking collectives  41.5 us (14%)
  Pallas kernels  24 us (8%)
  between operations  11.5 us (4%)
  local copies, waits for them, and re-layouts  7.01 us (2%)
  other arithmetic  4.86 us (2%)
    ppermute x9, waiting for transfers between devices, spread(): other = lax.ppermute(held, axis, [(i, i ^ bit) for i in range(members)])  151 us
    ppermute x9, starting transfers between devices, spread(): other = lax.ppermute(held, axis, [(i, i ^ bit) for i in range(members)])  44.2 us
    all_to_all x1, blocking collectives, body(): lax.all_to_all(parts, 'shard', split_axis=0, concat_axis=0, tiled=True)  24.1 us
    pallas_call x1, Pallas kernels, ladder(): pl.pallas_call(ladder_kernel, grid_spec=pltpu.PrefetchScalarGridSpec(num_...  20.7 us
    all_to_all x1, blocking collectives, body(): lax.all_to_all(returns, 'group', split_axis=0, concat_axis=0, tiled=True)  17.5 us
    all_to_all x1, starting transfers between devices, body(): lax.all_to_all(factor_send, 'group', split_axis=0, concat_axis=0, tiled=T...  10.3 us
  transfers between devices with their start and end apart: 10, of which 8 were waited for; matrix products, arithmetic and copies ran while one was open for 2% of the time, Pallas kernels for 0%

profile of v2, /device:TPU:8, one launch (start us, length us, event | category | flops | bytes accessed | tf_op | source)
XLA Modules:
  0.0 294.0 jit_solution(3773070457442173909)
XLA Ops:
  0.0 0.0 copy-start
  0.0 0.8 fusion.8
  0.8 1.1 copy-done
  1.9 3.6 %gather_fusion = bf16[16,192,1024]{2,1,0:T(8,128)(2,1)} fusion(bf16[8,192,1024]{2,1,0:T(8,128)(2,1)S(1)} %copy-done, s32[1024]{0:T(1024)S(1)} %pad_clamp_fusion), kind=kCustom, calls=%fused_computation | custom fusion | bytes 12582976 | tf_op jit(solution)/shard_map/gather | solution.py:169
  5.5 0.0 copy-start.3
  5.5 0.0 copy-start.2
  5.5 10.3 %all-to-all-start = ((bf16[16,192,1024]{2,1,0:T(8,128)(2,1)}), bf16[16,192,1024]{2,1,0:T(8,128)(2,1)}, u32[]{:S(2)}, u32[]{:S(2)}) async-start(bf16[16,192,1024]{2,1,0:T(8,128)(2,1)} %gather_fusion), calls=%async_computation | async-start | bytes 12582912 | tf_op jit(solution)/shard_map/all_to_all | solution.py:171
  15.8 0.0 copy-done.3
  15.8 0.9 constant_dynamic-slice_fusion.3
  16.7 0.1 pad.47.clone
  16.8 0.1 maximum_bitcast_fusion
  16.9 2.2 collective-permute-start
  19.1 136.2 %collective-permute-done = bf16[1,8,1024]{2,1,0:T(8,128)(2,1)S(1)} collective-permute-done((bf16[1,8,1024]{2,1,0:T(8,128)(2,1)S(1)}, bf16[1,8,1024]{2,1,0:T(8,128)(2,1)S(1)}, u32[]{:S(2)}, u32[]{:S(2)}) %collective-permute-start) | collective-permute-done | bytes 16416 | tf_op jit(solution)/shard_map/ppermute | solution.py:140
  155.3 5.7 %collective-permute-start.1 = (bf16[2,8,1024]{2,1,0:T(8,128)(2,1)S(1)}, bf16[2,8,1024]{2,1,0:T(8,128)(2,1)S(1)}, u32[]{:S(2)}, u32[]{:S(2)}) collective-permute-start(bf16[2,8,1024]{2,1,0:T(8,128)(2,1)S(1)} %maximum_select_fusion.6), channel_id=1, source_target_pairs={{0,64},{32,96},{64,0},{96,32},{128,192},{160,224},{192,128},{224,1... | collective-permute-start | bytes 98312 | tf_op jit(solution)/shard_map/ppermute | solution.py:140
  160.9 1.9 collective-permute-done.1
  162.8 7.1 %collective-permute-start.2 = (bf16[4,8,1024]{2,1,0:T(8,128)(2,1)S(1)}, bf16[4,8,1024]{2,1,0:T(8,128)(2,1)S(1)}, u32[]{:S(2)}, u32[]{:S(2)}) collective-permute-start(bf16[4,8,1024]{2,1,0:T(8,128)(2,1)S(1)} %maximum_select_fusion.4), channel_id=1, source_target_pairs={{0,128},{32,160},{64,192},{96,224},{128,0},{160,32},{192,64},{224,... | collective-permute-start | bytes 196616 | tf_op jit(solution)/shard_map/ppermute | solution.py:140
  169.9 3.7 %collective-permute-done.2 = bf16[4,8,1024]{2,1,0:T(8,128)(2,1)S(1)} collective-permute-done((bf16[4,8,1024]{2,1,0:T(8,128)(2,1)S(1)}, bf16[4,8,1024]{2,1,0:T(8,128)(2,1)S(1)}, u32[]{:S(2)}, u32[]{:S(2)}) %collective-permute-start.2) | collective-permute-done | bytes 65568 | tf_op jit(solution)/shard_map/ppermute | solution.py:140
  173.6 5.1 %collective-permute-start.3 = (bf16[8,8,1024]{2,1,0:T(8,128)(2,1)S(1)}, bf16[8,8,1024]{2,1,0:T(8,128)(2,1)}, u32[]{:S(2)}, u32[]{:S(2)}) collective-permute-start(bf16[8,8,1024]{2,1,0:T(8,128)(2,1)S(1)} %maximum_select_fusion.2), channel_id=1, source_target_pairs={{0,256},{32,288},{64,320},{96,352},{128,384},{160,416},{192,448},{... | collective-permute-start | bytes 393224 | tf_op jit(solution)/shard_map/ppermute | solution.py:140
  178.7 0.0 copy-done.2
  178.7 0.0 copy-start.1
  178.7 0.7 fusion.9
  185.0 0.0 collective-permute-done.3
  185.0 1.0 maximum_select_fusion
  186.1 0.7 constant_dynamic-slice_fusion.2
  192.5 1.9 collective-permute-start.4
  194.4 1.1 collective-permute-done.4
  195.6 0.1 broadcast_select_fusion
  195.6 4.5 %collective-permute-start.5 = (bf16[2,3,1024]{2,0,1:T(2,128)(2,1)S(1)}, bf16[2,3,1024]{2,0,1:T(2,128)(2,1)S(1)}, u32[]{:S(2)}, u32[]{:S(2)}) collective-permute-start(bf16[2,3,1024]{2,0,1:T(2,128)(2,1)S(1)} %broadcast_select_fusion), channel_id=1, source_target_pairs={{0,2},{1,3},{2,0},{3,1},{4,6},{5,7},{6,4},{7,5},{8,10},{9,11},{10,... | collective-permute-start | bytes 36872 | tf_op jit(solution)/shard_map/ppermute | solution.py:140
  200.1 1.7 collective-permute-done.5
  201.8 0.1 maximum_select_fusion.7
  201.8 6.1 %collective-permute-start.6 = (bf16[4,3,1024]{2,0,1:T(4,128)(2,1)S(1)}, bf16[4,3,1024]{2,0,1:T(4,128)(2,1)S(1)}, u32[]{:S(2)}, u32[]{:S(2)}) collective-permute-start(bf16[4,3,1024]{2,0,1:T(4,128)(2,1)S(1)} %maximum_select_fusion.7), channel_id=1, source_target_pairs={{0,4},{1,5},{2,6},{3,7},{4,0},{5,1},{6,2},{7,3},{8,12},{9,13},{10,... | collective-permute-start | bytes 73736 | tf_op jit(solution)/shard_map/ppermute | solution.py:140
  207.9 1.8 collective-permute-done.6
  209.8 9.3 %collective-permute-start.7 = (bf16[8,3,1024]{2,0,1:T(8,128)(2,1)S(1)}, bf16[8,3,1024]{2,0,1:T(8,128)(2,1)S(1)}, u32[]{:S(2)}, u32[]{:S(2)}) collective-permute-start(bf16[8,3,1024]{2,0,1:T(8,128)(2,1)S(1)} %maximum_select_fusion.5), channel_id=1, source_target_pairs={{0,8},{1,9},{2,10},{3,11},{4,12},{5,13},{6,14},{7,15},{8,0},{9,1},... | collective-permute-start | bytes 147464 | tf_op jit(solution)/shard_map/ppermute | solution.py:140
  219.1 2.1 collective-permute-done.7
  221.2 2.5 collective-permute-start.8
  223.7 1.9 and_convert_fusion.swap
  225.6 2.1 collective-permute-done.8
  227.7 0.7 fusion.amp
  228.4 0.0 all-to-all-done.left.right
  228.4 0.0 copy-done.1
  228.4 20.7 %ladder.1 = f32[32,3,8,128]{3,2,1,0:T(8,128)} custom-call(s32[3,4]{1,0:T(4,128)} %bitcast.33, bf16[16,192,1024]{2,1,0:T(8,128)(2,1)} %all-to-all-done.left.right, bf16[16,192,1024]{2,1,0:T(8,128)(2,1)} %all-to-all-done.left.right, bf16[3,32,1024]{2,1,0:T(8,128)(2,1)} %fusion.amp, bf16[1024,1024]{1,0:T(8,128)(2,1)} %and_convert_fusion.swap), custom_call_target="tpu_custom_call" | custom-call | tf_op jit(solution)/shard_map/ladder/pallas_call | solution.py:70
  249.2 24.1 %all_to_all.15.pieces = f32[32,3,8,128]{3,2,1,0:T(8,128)} all-to-all(f32[32,3,8,128]{3,2,1,0:T(8,128)} %ladder.1), channel_id=1, replica_groups=mesh['group'=16,'shard'=32] {'shard'}, dimensions={0} | all-to-all | bytes 786432 | tf_op jit(solution)/shard_map/all_to_all | solution.py:173
  273.2 1.7 combine.1
  274.9 17.5 %all_to_all.16.arrived = f32[16,8,128]{2,1,0:T(8,128)} all-to-all(f32[16,8,128]{2,1,0:T(8,128)} %combine.1), channel_id=1, replica_groups=mesh['group'=16,'shard'=32] {'group'}, dimensions={0} | all-to-all | bytes 131072 | tf_op jit(solution)/shard_map/all_to_all | solution.py:175
  292.4 1.6 owned.1
  (17 shorter events, 0.2 us)
Async XLA Ops:
  0.0 1.9 copy-start
  5.5 10.3 %copy-start.3 = (s32[1,16]{1,0:T(1,128)S(1)}, s32[1,16]{1,0:T(1,128)}, u32[]{:S(2)}) copy-start(s32[1,16]{1,0:T(1,128)} %param.9) | copy-start | bytes 196
  5.5 173.2 %copy-start.2 = (s32[1,3,4]{2,0,1:T(1,128)S(1)}, s32[1,3,4]{2,0,1:T(1,128)}, u32[]{:S(2)}) copy-start(s32[1,3,4]{2,0,1:T(1,128)} %param.10) | copy-start | bytes 148
  5.5 222.9 %all-to-all-start = ((bf16[16,192,1024]{2,1,0:T(8,128)(2,1)}), bf16[16,192,1024]{2,1,0:T(8,128)(2,1)}, u32[]{:S(2)}, u32[]{:S(2)}) async-start(bf16[16,192,1024]{2,1,0:T(8,128)(2,1)} %gather_fusion), calls=%async_computation | async-start | bytes 12582912 | tf_op jit(solution)/shard_map/all_to_all | solution.py:171
  16.9 138.4 %collective-permute-start = (bf16[1,8,1024]{2,1,0:T(8,128)(2,1)S(1)}, bf16[1,8,1024]{2,1,0:T(8,128)(2,1)S(1)}, u32[]{:S(2)}, u32[]{:S(2)}) collective-permute-start(bf16[1,8,1024]{2,1,0:T(8,128)(2,1)S(1)} %maximum_bitcast_fusion), channel_id=1, source_target_pairs={{0,32},{32,0},{64,96},{96,64},{128,160},{160,128},{192,224},{224,1... | collective-permute-start | bytes 49160 | tf_op jit(solution)/shard_map/ppermute | solution.py:140
  155.3 7.5 %collective-permute-start.1 = (bf16[2,8,1024]{2,1,0:T(8,128)(2,1)S(1)}, bf16[2,8,1024]{2,1,0:T(8,128)(2,1)S(1)}, u32[]{:S(2)}, u32[]{:S(2)}) collective-permute-start(bf16[2,8,1024]{2,1,0:T(8,128)(2,1)S(1)} %maximum_select_fusion.6), channel_id=1, source_target_pairs={{0,64},{32,96},{64,0},{96,32},{128,192},{160,224},{192,128},{224,1... | collective-permute-start | bytes 98312 | tf_op jit(solution)/shard_map/ppermute | solution.py:140
  162.8 10.8 %collective-permute-start.2 = (bf16[4,8,1024]{2,1,0:T(8,128)(2,1)S(1)}, bf16[4,8,1024]{2,1,0:T(8,128)(2,1)S(1)}, u32[]{:S(2)}, u32[]{:S(2)}) collective-permute-start(bf16[4,8,1024]{2,1,0:T(8,128)(2,1)S(1)} %maximum_select_fusion.4), channel_id=1, source_target_pairs={{0,128},{32,160},{64,192},{96,224},{128,0},{160,32},{192,64},{224,... | collective-permute-start | bytes 196616 | tf_op jit(solution)/shard_map/ppermute | solution.py:140
  173.6 11.4 %collective-permute-start.3 = (bf16[8,8,1024]{2,1,0:T(8,128)(2,1)S(1)}, bf16[8,8,1024]{2,1,0:T(8,128)(2,1)}, u32[]{:S(2)}, u32[]{:S(2)}) collective-permute-start(bf16[8,8,1024]{2,1,0:T(8,128)(2,1)S(1)} %maximum_select_fusion.2), channel_id=1, source_target_pairs={{0,256},{32,288},{64,320},{96,352},{128,384},{160,416},{192,448},{... | collective-permute-start | bytes 393224 | tf_op jit(solution)/shard_map/ppermute | solution.py:140
  178.7 49.7 %copy-start.1 = (s32[1,3,4]{2,1,0:T(4,128)}, s32[1,3,4]{2,1,0:T(4,128)S(1)}, u32[]{:S(2)}) copy-start(s32[1,3,4]{2,1,0:T(4,128)S(1)} %copy.15) | copy-start | bytes 148
  192.5 3.1 %collective-permute-start.4 = (bf16[1,3,1024]{2,0,1:T(2,128)(2,1)S(1)}, bf16[1,3,1024]{2,0,1:T(2,128)(2,1)S(1)}, u32[]{:S(2)}, u32[]{:S(2)}) collective-permute-start(bf16[1,3,1024]{2,0,1:T(2,128)(2,1)S(1)} %copy.8), channel_id=1, source_target_pairs={{0,1},{1,0},{2,3},{3,2},{4,5},{5,4},{6,7},{7,6},{8,9},{9,8},{10,11... | collective-permute-start | bytes 18440 | tf_op jit(solution)/shard_map/ppermute | solution.py:140
  195.6 6.1 %collective-permute-start.5 = (bf16[2,3,1024]{2,0,1:T(2,128)(2,1)S(1)}, bf16[2,3,1024]{2,0,1:T(2,128)(2,1)S(1)}, u32[]{:S(2)}, u32[]{:S(2)}) collective-permute-start(bf16[2,3,1024]{2,0,1:T(2,128)(2,1)S(1)} %broadcast_select_fusion), channel_id=1, source_target_pairs={{0,2},{1,3},{2,0},{3,1},{4,6},{5,7},{6,4},{7,5},{8,10},{9,11},{10,... | collective-permute-start | bytes 36872 | tf_op jit(solution)/shard_map/ppermute | solution.py:140
  201.8 7.9 %collective-permute-start.6 = (bf16[4,3,1024]{2,0,1:T(4,128)(2,1)S(1)}, bf16[4,3,1024]{2,0,1:T(4,128)(2,1)S(1)}, u32[]{:S(2)}, u32[]{:S(2)}) collective-permute-start(bf16[4,3,1024]{2,0,1:T(4,128)(2,1)S(1)} %maximum_select_fusion.7), channel_id=1, source_target_pairs={{0,4},{1,5},{2,6},{3,7},{4,0},{5,1},{6,2},{7,3},{8,12},{9,13},{10,... | collective-permute-start | bytes 73736 | tf_op jit(solution)/shard_map/ppermute | solution.py:140
  209.8 11.4 %collective-permute-start.7 = (bf16[8,3,1024]{2,0,1:T(8,128)(2,1)S(1)}, bf16[8,3,1024]{2,0,1:T(8,128)(2,1)S(1)}, u32[]{:S(2)}, u32[]{:S(2)}) collective-permute-start(bf16[8,3,1024]{2,0,1:T(8,128)(2,1)S(1)} %maximum_select_fusion.5), channel_id=1, source_target_pairs={{0,8},{1,9},{2,10},{3,11},{4,12},{5,13},{6,14},{7,15},{8,0},{9,1},... | collective-permute-start | bytes 147464 | tf_op jit(solution)/shard_map/ppermute | solution.py:140
  221.2 6.5 %collective-permute-start.8 = (bf16[16,3,1024]{2,0,1:T(8,128)(2,1)S(1)}, bf16[16,3,1024]{2,0,1:T(8,128)(2,1)S(1)}, u32[]{:S(2)}, u32[]{:S(2)}) collective-permute-start(bf16[16,3,1024]{2,0,1:T(8,128)(2,1)S(1)} %maximum_select_fusion.3), channel_id=1, source_target_pairs={{0,16},{1,17},{2,18},{3,19},{4,20},{5,21},{6,22},{7,23},{8,24},{9,... | collective-permute-start | bytes 294920 | tf_op jit(solution)/shard_map/ppermute | solution.py:140

commit v3 on v2

--- a/solution.py
+++ b/solution.py
@@ -15,13 +15,13 @@
 
 def swap_lane_blocks(tiles):
     lane = lax.broadcasted_iota(jnp.int32, tiles[0].shape, 1)
+    low = lane.astype(tiles[0].dtype) < 2 * VB
+    even = (lane % (2 * VB)).astype(tiles[0].dtype) < VB
     x0, x1, x2, x3 = tiles
-    low = lane < 2 * VB
     y0 = jnp.where(low, x0, pltpu.roll(x2, 2 * VB, 1))
     y2 = jnp.where(low, pltpu.roll(x0, 2 * VB, 1), x2)
     y1 = jnp.where(low, x1, pltpu.roll(x3, 2 * VB, 1))
     y3 = jnp.where(low, pltpu.roll(x1, 2 * VB, 1), x3)
-    even = lane % (2 * VB) < VB
     z0 = jnp.where(even, y0, pltpu.roll(y1, VB, 1))
     z1 = jnp.where(even, pltpu.roll(y0, LANES - VB, 1), y1)
     z2 = jnp.where(even, y2, pltpu.roll(y3, VB, 1))
@@ -29,27 +29,39 @@
     return z0, z1, z2, z3
 
 
-def ladder_kernel(record, left, right, amp, swap, out, folded, result):
+def ladder_kernel(record, left, right, amp, swap, out, right_t, amp_t, integral, folded, result):
     width = left.shape[2]
     occupied = amp.shape[1]
     per_pass = 2 * FOLD
     span = per_pass * VB
-    right_t = jnp.dot(right[0], swap[...], preferred_element_type=jnp.float32).astype(jnp.bfloat16)
-    amp_t = jnp.dot(amp[0], swap[...], preferred_element_type=jnp.float32).astype(jnp.bfloat16)
-    for step in range(VB // per_pass):
-        columns = slice(step * span, (step + 1) * span)
-        integral = lax.dot_general(
-            left[0, :, columns], right_t, (((0,), (0,)), ((), ())), preferred_element_type=jnp.float32
-        )
-        for half in range(2):
-            for part in range(width // LANES):
-                lanes = slice(part * LANES, (part + 1) * LANES)
+    right_t[...] = jnp.dot(right[0], swap[...], preferred_element_type=jnp.float32).astype(jnp.bfloat16)
+    amp_t[...] = jnp.dot(amp[0], swap[...], preferred_element_type=jnp.float32).astype(jnp.bfloat16)
+
+    def products(step, _):
+        columns = pl.ds(pl.multiple_of(step * 2 * span, 2 * span), 2 * span)
+        integral[columns, :] = lax.dot_general(
+            left[0, :, columns], right_t[...], (((0,), (0,)), ((), ())), preferred_element_type=jnp.float32
+        ).astype(jnp.bfloat16)
+        return 0
+
+    lax.fori_loop(0, VB // per_pass // 2, products, 0)
+
+    def one_pass(step, _):
+        columns = pl.ds(pl.multiple_of(step * span, span), span)
+        for part in range(width // LANES):
+            lanes = slice(part * LANES, (part + 1) * LANES)
+            for half in range(2):
                 rows = half * FOLD * VB
-                tiles = [integral[rows + a * VB : rows + (a + 1) * VB, lanes] for a in range(FOLD)]
+                tiles = [
+                    integral[pl.ds(pl.multiple_of(step * span + rows + a * VB, VB), VB), lanes] for a in range(FOLD)
+                ]
                 for d, tile in enumerate(swap_lane_blocks(tiles)):
                     base = (part * FOLD + d) * VB
-                    folded[base : base + VB, half * LANES : (half + 1) * LANES] = tile.astype(jnp.bfloat16)
-        result[:, columns] = jnp.dot(amp_t, folded[...], preferred_element_type=jnp.float32)
+                    folded[base : base + VB, half * LANES : (half + 1) * LANES] = tile
+        result[:, columns] = jnp.dot(amp_t[...], folded[...], preferred_element_type=jnp.float32)
+        return 0
+
+    lax.fori_loop(0, VB // per_pass, one_pass, 0)
     band = occupied // FOLD
     for group in range(width // LANES):
         lanes = slice(group * LANES, (group + 1) * LANES)
@@ -80,6 +92,9 @@
             ],
             out_specs=pl.BlockSpec((VB, 1, band, LANES), lambda k, rec: (0, k, 0, 0)),
             scratch_shapes=[
+                pltpu.VMEM((rows, width), jnp.bfloat16),
+                pltpu.VMEM((occupied, width), jnp.bfloat16),
+                pltpu.VMEM((width, width), jnp.bfloat16),
                 pltpu.VMEM((width, 2 * LANES), jnp.bfloat16),
                 pltpu.VMEM((occupied, width), jnp.float32),
             ],
@@ -147,28 +162,22 @@
 
 
 def amplitude_tiles(records, amplitudes, amp_route):
-    group, shard = lax.axis_index("group"), lax.axis_index("shard")
-    tiles, _, width = amplitudes.shape
-    tasks = records.shape[0]
+    shard = lax.axis_index("shard")
+    width = amplitudes.shape[2]
     rows = lax.dynamic_index_in_dim(amplitudes, shard, 1, keepdims=False)
-    route = jnp.pad(amp_route[0], (0, width - amp_route.shape[1])).astype(rows.dtype)
-    block = jnp.concatenate([rows, route[None], jnp.zeros((8 - tiles - 1, width), rows.dtype)])
-    held = spread(block, "group")
-    source = records[:, 3]
-    routes = held[:, tiles, : amp_route.shape[1]].astype(jnp.int32)[:, group]
-    picked = [
-        lax.dynamic_slice(held, (source[k], routes[source[k]], 0), (1, 1, width))[0, 0] for k in range(tasks)
-    ]
-    whole = spread(jnp.stack(picked), "shard")
-    return whole.transpose(1, 0, 2)
+    send = rows.at[amp_route[0]].get(mode="promise_in_bounds").reshape(-1, width // LANES, LANES)
+    arrived = lax.all_to_all(send, "group", split_axis=0, concat_axis=0, tiled=True)
+    return arrived.at[records[:, 3]].get(mode="promise_in_bounds")
 
 
 def body(factors, amplitudes, factor_route, amp_route, task_list, target_tile):
     groups = lax.axis_size("group")
     records = task_list[0]
     factor_send = factors.at[factor_route[0]].get(mode="promise_in_bounds")
-    amps = amplitude_tiles(records, amplitudes, amp_route)
+    picked = amplitude_tiles(records, amplitudes, amp_route)
+    factor_send, picked = lax.optimization_barrier((factor_send, picked))
     factor_recv = lax.all_to_all(factor_send, "group", split_axis=0, concat_axis=0, tiled=True)
+    amps = spread(picked, "shard").reshape(-1, records.shape[0], factors.shape[2]).transpose(1, 0, 2)
     parts = ladder(records, factor_recv, amps)
     pieces = lax.all_to_all(parts, "shard", split_axis=0, concat_axis=0, tiled=True)
     returns = combine(records, pieces, groups)

time: 295 us -> 235 us (0.80)
  waiting for transfers between devices: 151 us -> 116 us
  starting transfers between devices: 54.5 us -> 39.7 us
  between operations: 11.5 us -> 0.14 us
  blocking collectives: 41.5 us -> 47.1 us
  Pallas kernels: 24 us -> 19.3 us
    ppermute x9 -> x5, waiting for transfers between devices: 151 us -> 10.4 us  [spread(): other = lax.ppermute(held, axis, [(i, i ^ bit) for i in range(members)])]
    all_to_all x1, waiting for transfers between devices: 0.01 us -> 102 us  [body(): lax.all_to_all(factor_send, 'group', split_axis=0, concat_axis=0, tiled=T...]
    ppermute x9 -> x5, starting transfers between devices: 44.2 us -> 23.6 us  [spread(): other = lax.ppermute(held, axis, [(i, i ^ bit) for i in range(members)])]
    all_to_all x0 -> x1, starting transfers between devices: none -> 10 us  [amplitude_tiles(): lax.all_to_all(send, 'group', split_axis=0, concat_axis=0, tiled=True)]
    pallas_call x1, Pallas kernels: 20.7 us -> 16 us  [ladder(): pl.pallas_call(ladder_kernel, grid_spec=pltpu.PrefetchScalarGridSpec(num_...]
    all_to_all x1, starting transfers between devices: 10.3 us -> 6.05 us  [body(): lax.all_to_all(factor_send, 'group', split_axis=0, concat_axis=0, tiled=T...]
    all_to_all x0 -> x1, waiting for transfers between devices: none -> 3.61 us  [amplitude_tiles(): lax.all_to_all(send, 'group', split_axis=0, concat_axis=0, tiled=True)]
  transfers between devices with their start and end apart: 10 -> 7, of which waited for: 8 -> 6; matrix products, arithmetic and copies ran while one was open for 2% -> 3% of each run, Pallas kernels for 0% -> 0%
where the time goes in v3:
time: 235 us; the launch traced here: 234 us
  waiting for transfers between devices  116 us (49%)
  blocking collectives  47.1 us (20%)
  starting transfers between devices  39.7 us (17%)
  Pallas kernels  19.3 us (8%)
  local copies, waits for them, and re-layouts  7.18 us (3%)
  other arithmetic  4.39 us (2%)
    all_to_all x1, waiting for transfers between devices, body(): lax.all_to_all(factor_send, 'group', split_axis=0, concat_axis=0, tiled=T...  102 us
    all_to_all x1, blocking collectives, body(): lax.all_to_all(parts, 'shard', split_axis=0, concat_axis=0, tiled=True)  26.8 us
    ppermute x5, starting transfers between devices, spread(): other = lax.ppermute(held, axis, [(i, i ^ bit) for i in range(members)])  23.6 us
    all_to_all x1, blocking collectives, body(): lax.all_to_all(returns, 'group', split_axis=0, concat_axis=0, tiled=True)  20.4 us
    pallas_call x1, Pallas kernels, ladder(): pl.pallas_call(ladder_kernel, grid_spec=pltpu.PrefetchScalarGridSpec(num_...  16 us
    ppermute x5, waiting for transfers between devices, spread(): other = lax.ppermute(held, axis, [(i, i ^ bit) for i in range(members)])  10.4 us
    all_to_all x1, starting transfers between devices, amplitude_tiles(): lax.all_to_all(send, 'group', split_axis=0, concat_axis=0, tiled=True)  10 us
    all_to_all x1, starting transfers between devices, body(): lax.all_to_all(factor_send, 'group', split_axis=0, concat_axis=0, tiled=T...  6.05 us
  transfers between devices with their start and end apart: 7, of which 6 were waited for; matrix products, arithmetic and copies ran while one was open for 3% of the time, Pallas kernels for 0%

profile of v3, /device:TPU:8, one launch (start us, length us, event | category | flops | bytes accessed | tf_op | source)
XLA Modules:
  0.0 234.0 jit_solution(2802156103840947263)
XLA Ops:
  0.0 0.0 copy-start
  0.0 1.0 constant_dynamic-slice_fusion
  1.0 0.7 fusion.10
  1.7 0.6 gather_fusion.1
  2.3 0.6 copy.9
  2.9 10.0 %all-to-all-start = ((bf16[16,8,128]{2,1,0:T(8,128)(2,1)}), bf16[16,8,128]{2,1,0:T(8,128)(2,1)S(1)}, u32[]{:S(2)}, u32[]{:S(2)}) async-start(bf16[16,8,128]{2,1,0:T(8,128)(2,1)} %bitcast.10), calls=%async_computation | async-start | bytes 65536 | tf_op jit(solution)/shard_map/all_to_all | solution.py:169
  12.9 0.7 copy.13
  13.6 0.0 copy-start.1
  13.6 0.7 fusion.9
  14.3 0.2 fusion.8
  14.5 0.0 copy-done
  14.5 3.6 %gather_fusion = bf16[16,192,1024]{2,1,0:T(8,128)(2,1)} fusion(bf16[8,192,1024]{2,1,0:T(8,128)(2,1)S(1)} %copy-done, s32[1024]{0:T(1024)S(1)} %pad_clamp_fusion.2), kind=kCustom, calls=%fused_computation | custom fusion | bytes 12582976 | tf_op jit(solution)/shard_map/gather | solution.py:176
  18.1 0.0 copy-done.1
  18.1 3.6 %all-to-all-done = bf16[16,8,128]{2,1,0:T(8,128)(2,1)S(1)} async-done(((bf16[16,8,128]{2,1,0:T(8,128)(2,1)}), bf16[16,8,128]{2,1,0:T(8,128)(2,1)S(1)}, u32[]{:S(2)}, u32[]{:S(2)}) %all-to-all-start) | async-done | bytes 32800 | tf_op jit(solution)/shard_map/all_to_all | solution.py:169
  21.7 0.6 gather_fusion.2
  22.2 6.0 %all-to-all-start.1 = ((bf16[16,192,1024]{2,1,0:T(8,128)(2,1)}), bf16[16,192,1024]{2,1,0:T(8,128)(2,1)}, u32[]{:S(2)}, u32[]{:S(2)}) async-start(bf16[16,192,1024]{2,1,0:T(8,128)(2,1)} %gather_fusion), calls=%async_computation.1 | async-start | bytes 12582912 | tf_op jit(solution)/shard_map/all_to_all | solution.py:179
  28.3 1.9 collective-permute-start
  30.2 1.1 collective-permute-done
  31.4 4.3 %collective-permute-start.1 = (bf16[2,3,8,128]{3,2,0,1:T(8,128)(2,1)S(1)}, bf16[2,3,8,128]{3,2,0,1:T(8,128)(2,1)S(1)}, u32[]{:S(2)}, u32[]{:S(2)}) collective-permute-start(bf16[2,3,8,128]{3,2,0,1:T(8,128)(2,1)S(1)} %maximum_select_fusion.7), channel_id=1, source_target_pairs={{0,2},{1,3},{2,0},{3,1},{4,6},{5,7},{6,4},{7,5},{8,10},{9,11},{10,... | collective-permute-start | bytes 36872 | tf_op jit(solution)/shard_map/ppermute | solution.py:155
  35.6 2.0 and_convert_fusion.swap
  37.6 0.0 collective-permute-done.1
  37.6 6.1 %collective-permute-start.2 = (bf16[4,3,8,128]{3,2,0,1:T(8,128)(2,1)S(1)}, bf16[4,3,8,128]{3,2,0,1:T(8,128)(2,1)S(1)}, u32[]{:S(2)}, u32[]{:S(2)}) collective-permute-start(bf16[4,3,8,128]{3,2,0,1:T(8,128)(2,1)S(1)} %maximum_select_fusion.6), channel_id=1, source_target_pairs={{0,4},{1,5},{2,6},{3,7},{4,0},{5,1},{6,2},{7,3},{8,12},{9,13},{10,... | collective-permute-start | bytes 73736 | tf_op jit(solution)/shard_map/ppermute | solution.py:155
  43.8 0.1 maximum_select_fusion.5
  43.8 1.8 collective-permute-done.2
  45.6 8.9 %collective-permute-start.3 = (bf16[8,3,8,128]{3,2,0,1:T(8,128)(2,1)S(1)}, bf16[8,3,8,128]{3,2,0,1:T(8,128)(2,1)S(1)}, u32[]{:S(2)}, u32[]{:S(2)}) collective-permute-start(bf16[8,3,8,128]{3,2,0,1:T(8,128)(2,1)S(1)} %maximum_select_fusion.4), channel_id=1, source_target_pairs={{0,8},{1,9},{2,10},{3,11},{4,12},{5,13},{6,14},{7,15},{8,0},{9,1},... | collective-permute-start | bytes 147464 | tf_op jit(solution)/shard_map/ppermute | solution.py:155
  54.5 0.1 maximum_select_fusion.3
  54.6 2.0 collective-permute-done.3
  56.6 2.5 %collective-permute-start.4 = (bf16[16,3,8,128]{3,2,0,1:T(8,128)(2,1)S(1)}, bf16[16,3,8,128]{3,2,0,1:T(8,128)(2,1)S(1)}, u32[]{:S(2)}, u32[]{:S(2)}) collective-permute-start(bf16[16,3,8,128]{3,2,0,1:T(8,128)(2,1)S(1)} %maximum_select_fusion.2), channel_id=1, source_target_pairs={{0,16},{1,17},{2,18},{3,19},{4,20},{5,21},{6,22},{7,23},{8,24},{9,... | collective-permute-start | bytes 294920 | tf_op jit(solution)/shard_map/ppermute | solution.py:155
  59.2 5.5 %collective-permute-done.4 = bf16[16,3,8,128]{3,2,0,1:T(8,128)(2,1)S(1)} collective-permute-done((bf16[16,3,8,128]{3,2,0,1:T(8,128)(2,1)S(1)}, bf16[16,3,8,128]{3,2,0,1:T(8,128)(2,1)S(1)}, u32[]{:S(2)}, u32[]{:S(2)}) %collective-permute-start.4) | collective-permute-done | bytes 98336 | tf_op jit(solution)/shard_map/ppermute | solution.py:155
  64.7 0.7 fusion.amp
  65.4 102.2 %all-to-all-done.1.left.right = bf16[16,192,1024]{2,1,0:T(8,128)(2,1)} async-done(((bf16[16,192,1024]{2,1,0:T(8,128)(2,1)}), bf16[16,192,1024]{2,1,0:T(8,128)(2,1)}, u32[]{:S(2)}, u32[]{:S(2)}) %all-to-all-start.1) | async-done | bytes 6291488 | tf_op jit(solution)/shard_map/all_to_all | solution.py:179
  167.6 16.0 %ladder.1 = f32[32,3,8,128]{3,2,1,0:T(8,128)} custom-call(s32[3,4]{1,0:T(4,128)} %bitcast.43, bf16[16,192,1024]{2,1,0:T(8,128)(2,1)} %all-to-all-done.1.left.right, bf16[16,192,1024]{2,1,0:T(8,128)(2,1)} %all-to-all-done.1.left.right, bf16[3,32,1024]{2,1,0:T(8,128)(2,1)} %fusion.amp, bf16[1024,1024]{1,0:T(8,128)(2,1)} %and_convert_fusion.swap), custom_call_target="tpu_custom_call" | custom-call | tf_op jit(solution)/shard_map/ladder/pallas_call | solution.py:82
  183.6 26.8 %all_to_all.20.pieces = f32[32,3,8,128]{3,2,1,0:T(8,128)} all-to-all(f32[32,3,8,128]{3,2,1,0:T(8,128)} %ladder.1), channel_id=1, replica_groups=mesh['group'=16,'shard'=32] {'shard'}, dimensions={0} | all-to-all | bytes 786432 | tf_op jit(solution)/shard_map/all_to_all | solution.py:182
  210.4 1.7 combine.1
  212.0 20.4 %all_to_all.21.arrived = f32[16,8,128]{2,1,0:T(8,128)} all-to-all(f32[16,8,128]{2,1,0:T(8,128)} %combine.1), channel_id=1, replica_groups=mesh['group'=16,'shard'=32] {'group'}, dimensions={0} | all-to-all | bytes 131072 | tf_op jit(solution)/shard_map/all_to_all | solution.py:184
  232.4 1.6 owned.1
  (15 shorter events, 0.2 us)
Async XLA Ops:
  0.0 14.5 %copy-start = (bf16[8,192,1024]{2,1,0:T(8,128)(2,1)S(1)}, bf16[8,192,1024]{2,1,0:T(8,128)(2,1)}, u32[]{:S(2)}) copy-start(bf16[8,192,1024]{2,1,0:T(8,128)(2,1)} %param.6) | copy-start | bytes 9437188
  2.9 18.8 %all-to-all-start = ((bf16[16,8,128]{2,1,0:T(8,128)(2,1)}), bf16[16,8,128]{2,1,0:T(8,128)(2,1)S(1)}, u32[]{:S(2)}, u32[]{:S(2)}) async-start(bf16[16,8,128]{2,1,0:T(8,128)(2,1)} %bitcast.10), calls=%async_computation | async-start | bytes 65536 | tf_op jit(solution)/shard_map/all_to_all | solution.py:169
  13.6 4.5 %copy-start.1 = (s32[1,3,4]{2,1,0:T(4,128)}, s32[1,3,4]{2,1,0:T(4,128)S(1)}, u32[]{:S(2)}) copy-start(s32[1,3,4]{2,1,0:T(4,128)S(1)} %copy.13) | copy-start | bytes 148
  22.2 145.4 %all-to-all-start.1 = ((bf16[16,192,1024]{2,1,0:T(8,128)(2,1)}), bf16[16,192,1024]{2,1,0:T(8,128)(2,1)}, u32[]{:S(2)}, u32[]{:S(2)}) async-start(bf16[16,192,1024]{2,1,0:T(8,128)(2,1)} %gather_fusion), calls=%async_computation.1 | async-start | bytes 12582912 | tf_op jit(solution)/shard_map/all_to_all | solution.py:179
  28.3 3.1 %collective-permute-start = (bf16[1,3,8,128]{3,2,0,1:T(8,128)(2,1)S(1)}, bf16[1,3,8,128]{3,2,0,1:T(8,128)(2,1)S(1)}, u32[]{:S(2)}, u32[]{:S(2)}) collective-permute-start(bf16[1,3,8,128]{3,2,0,1:T(8,128)(2,1)S(1)} %bitcast.45), channel_id=1, source_target_pairs={{0,1},{1,0},{2,3},{3,2},{4,5},{5,4},{6,7},{7,6},{8,9},{9,8},{10,11... | collective-permute-start | bytes 18440 | tf_op jit(solution)/shard_map/ppermute | solution.py:155
  31.4 6.3 %collective-permute-start.1 = (bf16[2,3,8,128]{3,2,0,1:T(8,128)(2,1)S(1)}, bf16[2,3,8,128]{3,2,0,1:T(8,128)(2,1)S(1)}, u32[]{:S(2)}, u32[]{:S(2)}) collective-permute-start(bf16[2,3,8,128]{3,2,0,1:T(8,128)(2,1)S(1)} %maximum_select_fusion.7), channel_id=1, source_target_pairs={{0,2},{1,3},{2,0},{3,1},{4,6},{5,7},{6,4},{7,5},{8,10},{9,11},{10,... | collective-permute-start | bytes 36872 | tf_op jit(solution)/shard_map/ppermute | solution.py:155
  37.6 8.0 %collective-permute-start.2 = (bf16[4,3,8,128]{3,2,0,1:T(8,128)(2,1)S(1)}, bf16[4,3,8,128]{3,2,0,1:T(8,128)(2,1)S(1)}, u32[]{:S(2)}, u32[]{:S(2)}) collective-permute-start(bf16[4,3,8,128]{3,2,0,1:T(8,128)(2,1)S(1)} %maximum_select_fusion.6), channel_id=1, source_target_pairs={{0,4},{1,5},{2,6},{3,7},{4,0},{5,1},{6,2},{7,3},{8,12},{9,13},{10,... | collective-permute-start | bytes 73736 | tf_op jit(solution)/shard_map/ppermute | solution.py:155
  45.6 11.0 %collective-permute-start.3 = (bf16[8,3,8,128]{3,2,0,1:T(8,128)(2,1)S(1)}, bf16[8,3,8,128]{3,2,0,1:T(8,128)(2,1)S(1)}, u32[]{:S(2)}, u32[]{:S(2)}) collective-permute-start(bf16[8,3,8,128]{3,2,0,1:T(8,128)(2,1)S(1)} %maximum_select_fusion.4), channel_id=1, source_target_pairs={{0,8},{1,9},{2,10},{3,11},{4,12},{5,13},{6,14},{7,15},{8,0},{9,1},... | collective-permute-start | bytes 147464 | tf_op jit(solution)/shard_map/ppermute | solution.py:155
  56.6 8.0 %collective-permute-start.4 = (bf16[16,3,8,128]{3,2,0,1:T(8,128)(2,1)S(1)}, bf16[16,3,8,128]{3,2,0,1:T(8,128)(2,1)S(1)}, u32[]{:S(2)}, u32[]{:S(2)}) collective-permute-start(bf16[16,3,8,128]{3,2,0,1:T(8,128)(2,1)S(1)} %maximum_select_fusion.2), channel_id=1, source_target_pairs={{0,16},{1,17},{2,18},{3,19},{4,20},{5,21},{6,22},{7,23},{8,24},{9,... | collective-permute-start | bytes 294920 | tf_op jit(solution)/shard_map/ppermute | solution.py:155

commit v4 on v3

v4 whole, which is shorter than its diff:
```python
import functools

import jax
import jax.numpy as jnp
from jax import lax
from jax.experimental import pallas as pl
from jax.experimental.pallas import tpu as pltpu
from jax.sharding import PartitionSpec as P

VB = 32
FPG = 8
APG = 4
TPG = 2
TASKS = 3
LANES = 128
FAST = 4
SWEEPS = 12
FACTOR_ROUTE, TARGET, RECORDS = 16, 32, 48
FOLD = LANES // VB


def swap_lane_blocks(tiles):
    lane = lax.broadcasted_iota(jnp.int32, tiles[0].shape, 1)
    low = lane.astype(tiles[0].dtype) < 2 * VB
    even = (lane % (2 * VB)).astype(tiles[0].dtype) < VB
    x0, x1, x2, x3 = tiles
    y0 = jnp.where(low, x0, pltpu.roll(x2, 2 * VB, 1))
    y2 = jnp.where(low, pltpu.roll(x0, 2 * VB, 1), x2)
    y1 = jnp.where(low, x1, pltpu.roll(x3, 2 * VB, 1))
    y3 = jnp.where(low, pltpu.roll(x1, 2 * VB, 1), x3)
    z0 = jnp.where(even, y0, pltpu.roll(y1, VB, 1))
    z1 = jnp.where(even, pltpu.roll(y0, LANES - VB, 1), y1)
    z2 = jnp.where(even, y2, pltpu.roll(y3, VB, 1))
    z3 = jnp.where(even, pltpu.roll(y2, LANES - VB, 1), y3)
    return z0, z1, z2, z3


def assemble(select, whole, cut, out):
    @pl.when(select < FPG)
    def _():
        out[...] = whole[0]

    @pl.when(select >= FPG)
    def _():
        rows = cut.shape[2]
        for piece in range(cut.shape[0]):
            half, part = divmod(piece, out.shape[1] // LANES)
            out[half * rows : (half + 1) * rows, part * LANES : (part + 1) * LANES] = cut[piece, 0]


def ladder_kernel(
    plan, left_whole, left_cut, right_whole, right_cut, amp, swap, out,
    left, right, right_t, amp_t, integral, folded, result,
):
    task = pl.program_id(0)

    @pl.when(plan[task, 3] < 0)
    def _():
        out[...] = jnp.zeros_like(out)

    @pl.when(plan[task, 3] >= 0)
    def _():
        assemble(plan[task, 0], left_whole, left_cut, left)
        assemble(plan[task, 1], right_whole, right_cut, right)
        ladder_task(left, right, amp, swap, out, right_t, amp_t, integral, folded, result)


def ladder_task(left, right, amp, swap, out, right_t, amp_t, integral, folded, result):
    width = left.shape[1]
    occupied = amp.shape[1]
    per_pass = 2 * FOLD
    span = per_pass * VB
    right_t[...] = jnp.dot(right[...], swap[...], preferred_element_type=jnp.float32).astype(jnp.bfloat16)
    amp_t[...] = jnp.dot(amp[0], swap[...], preferred_element_type=jnp.float32).astype(jnp.bfloat16)

    def products(step, _):
        columns = pl.ds(pl.multiple_of(step * 2 * span, 2 * span), 2 * span)
        integral[columns, :] = lax.dot_general(
            left[:, columns], right_t[...], (((0,), (0,)), ((), ())), preferred_element_type=jnp.float32
        ).astype(jnp.bfloat16)
        return 0

    lax.fori_loop(0, VB // per_pass // 2, products, 0)

    def one_pass(step, _):
        columns = pl.ds(pl.multiple_of(step * span, span), span)
        for part in range(width // LANES):
            lanes = slice(part * LANES, (part + 1) * LANES)
            for half in range(2):
                rows = half * FOLD * VB
                tiles = [
                    integral[pl.ds(pl.multiple_of(step * span + rows + a * VB, VB), VB), lanes] for a in range(FOLD)
                ]
                for d, tile in enumerate(swap_lane_blocks(tiles)):
                    base = (part * FOLD + d) * VB
                    folded[base : base + VB, half * LANES : (half + 1) * LANES] = tile
        result[:, columns] = jnp.dot(amp_t[...], folded[...], preferred_element_type=jnp.float32)
        return 0

    lax.fori_loop(0, VB // per_pass, one_pass, 0)
    band = occupied // FOLD
    for group in range(width // LANES):
        lanes = slice(group * LANES, (group + 1) * LANES)
        tiles = [result[i * band : (i + 1) * band, lanes] for i in range(FOLD)]
        for a, tile in enumerate(swap_lane_blocks(tiles)):
            out[group * FOLD + a, 0] = tile


def ladder(plan, factors, arrived, amps):
    rows, width = factors.shape[1:]
    tasks, occupied = amps.shape[:2]
    index = jnp.arange(width, dtype=jnp.int32)
    swap = (
        (index[:, None] // VB == index[None, :] % VB) & (index[:, None] % VB == index[None, :] // VB)
    ).astype(jnp.bfloat16)
    band = occupied // FOLD
    pieces, _, piece_rows, _ = arrived.shape

    def whole(side):
        def place(k, plan):
            return jnp.where(plan[k, side] < FPG, plan[k, side], 0), 0, 0

        return pl.BlockSpec((1, rows, width), place)

    def cut(side):
        def place(k, plan):
            return 0, jnp.where(plan[k, side] < FPG, 0, plan[k, side] - FPG), 0, 0

        return pl.BlockSpec((pieces, 1, piece_rows, LANES), place)

    return pl.pallas_call(
        ladder_kernel,
        grid_spec=pltpu.PrefetchScalarGridSpec(
            num_scalar_prefetch=1,
            grid=(tasks,),
            in_specs=[
                whole(0),
                cut(0),
                whole(1),
                cut(1),
                pl.BlockSpec((1, occupied, width), lambda k, plan: (k, 0, 0)),
                pl.BlockSpec((width, width), lambda k, plan: (0, 0)),
            ],
            out_specs=pl.BlockSpec((VB, 1, band, LANES), lambda k, plan: (0, k, 0, 0)),
            scratch_shapes=[
                pltpu.VMEM((rows, width), jnp.bfloat16),
                pltpu.VMEM((rows, width), jnp.bfloat16),
                pltpu.VMEM((rows, width), jnp.bfloat16),
                pltpu.VMEM((occupied, width), jnp.bfloat16),
                pltpu.VMEM((width, width), jnp.bfloat16),
                pltpu.VMEM((width, 2 * LANES), jnp.bfloat16),
                pltpu.VMEM((occupied, width), jnp.float32),
            ],
        ),
        out_shape=jax.ShapeDtypeStruct((VB, tasks, band, LANES), jnp.float32),
        compiler_params=pltpu.CompilerParams(dimension_semantics=("arbitrary",)),
        name="ladder",
    )(plan, factors, arrived, factors, arrived, amps, swap)


def combine_kernel(plan, pieces, out):
    total = jnp.sum(pieces[...], axis=0)
    out[...] = jnp.zeros_like(out)
    for k in range(pieces.shape[1]):
        target = plan[k, 3]

        @pl.when(target >= 0)
        def _():
            out[target] += total[k]


def combine(plan, pieces, tiles):
    return pl.pallas_call(
        combine_kernel,
        in_specs=[pl.BlockSpec(memory_space=pltpu.SMEM), pl.BlockSpec(memory_space=pltpu.VMEM)],
        out_specs=pl.BlockSpec(memory_space=pltpu.VMEM),
        out_shape=jax.ShapeDtypeStruct((tiles, *pieces.shape[2:]), jnp.float32),
        name="combine",
    )(plan, pieces)


def owned_kernel(arrived, out):
    groups, tiles, band, lanes = arrived.shape
    for t in range(tiles):
        total = jnp.sum(arrived[:, t], axis=0)
        for i in range(FOLD):
            out[t, i * band : (i + 1) * band, :] = total[:, i * VB : (i + 1) * VB]


def owned(arrived):
    groups, tiles, band, lanes = arrived.shape
    return pl.pallas_call(
        owned_kernel,
        in_specs=[pl.BlockSpec(memory_space=pltpu.VMEM)],
        out_specs=pl.BlockSpec(memory_space=pltpu.VMEM),
        out_shape=jax.ShapeDtypeStruct((tiles, band * FOLD, VB), jnp.float32),
        name="owned",
    )(arrived)


def assign_kernel(
    me, table, send, pick, plan, balanced,
    compute, other, compute_block, other_block, load, sent, uses, filled, slots, where_sent,
):
    groups = table.shape[0]
    mine = me[0]
    for g in range(groups):
        load[g] = 0
        sent[g] = 0
        filled[g] = 0
        slots[g] = 0

    def clear(i, _):
        uses[i] = 0
        where_sent[i] = -1
        pick[i] = 0
        return 0

    lax.fori_loop(0, groups * FPG, clear, 0)
    for i in range(send.shape[0]):
        send[i] = 0
    for k in range(plan.shape[0]):
        for j in range(3):
            plan[k, j] = 0
        plan[k, 3] = -1

    def first_choice(h, _):
        for k in range(TASKS):
            s1, s2 = table[h, RECORDS + 4 * k + 1], table[h, RECORDS + 4 * k + 2]
            b1, b2 = table[s1, FACTOR_ROUTE + h], table[s2, FACTOR_ROUTE + h]
            n1, n2 = uses[s1 * FPG + b1], uses[s2 * FPG + b2]
            at_first = 2 * load[s1] - jnp.where(n2 > 0, 0, FAST - sent[s2])
            at_second = 2 * load[s2] - jnp.where(n1 > 0, 0, FAST - sent[s1])
            second = at_first > at_second
            c, o = jnp.where(second, s2, s1), jnp.where(second, s1, s2)
            y, x = jnp.where(second, b2, b1), jnp.where(second, b1, b2)
            n = jnp.where(second, n1, n2)
            moved = jnp.where(c != o, 1, 0)
            i = h * TASKS + k
            compute[i], other[i], compute_block[i], other_block[i] = c, o, y, x
            load[c] += 1
            sent[o] += jnp.where(n == 0, moved, 0)
            uses[o * FPG + x] = n + moved
        return 0

    lax.fori_loop(0, groups, first_choice, 0)
    over = lambda n: jnp.maximum(n - FAST, 0)

    def excess():
        total = 0
        for g in range(groups):
            total += over(load[g]) + over(sent[g])
        return total

    def sweep(state):
        def visit(i, bad):
            c, o = compute[i], other[i]
            wanted = (c != o) & ((load[c] > FAST) | (sent[o] > FAST))

            def flip(bad):
                y, x = compute_block[i], other_block[i]
                nc, no = uses[c * FPG + y], uses[o * FPG + x]
                less, more = jnp.where(no == 1, 1, 0), jnp.where(nc == 0, 1, 0)
                lc, lo, sc, so = load[c], load[o], sent[c], sent[o]
                change = over(lc - 1) - over(lc) + over(lo + 1) - over(lo)
                change += over(sc + more) - over(sc) + over(so - less) - over(so)

                def take(bad):
                    compute[i], other[i], compute_block[i], other_block[i] = o, c, x, y
                    load[c], load[o] = lc - 1, lo + 1
                    sent[c], sent[o] = sc + more, so - less
                    uses[c * FPG + y], uses[o * FPG + x] = nc + 1, no - 1
                    return bad + change

                return lax.cond(change <= 0, take, lambda bad: bad, bad)

            return lax.cond(wanted, flip, lambda bad: bad, bad)

        return state[0] + 1, lax.fori_loop(0, groups * TASKS, visit, state[1])

    _, bad = lax.while_loop(lambda s: (s[0] < SWEEPS) & (s[1] > 0), sweep, (jnp.int32(0), excess()))
    good = bad == 0
    balanced[0] = jnp.where(good, 1, 0)
    stride = jnp.where(good, FAST, FPG)

    def fetch(source, block, c):
        remote = source != c
        known = where_sent[source * FPG + block]
        fresh = remote & (known < 0)
        count = filled[source]
        at = jnp.where(fresh, count, known)
        filled[source] = count + jnp.where(fresh, 1, 0)
        where_sent[source * FPG + block] = at
        send[jnp.where(fresh & (source == mine), at, FPG)] = block
        slot = slots[c]
        slots[c] = slot + jnp.where(remote, 1, 0)
        pick[jnp.where(remote, c * FPG + slot, groups * FPG)] = source * stride + at
        return jnp.where(remote, FPG + slot, block)

    def deal(h, _):
        for k in range(TASKS):
            o, s1, s2, s3 = [table[h, RECORDS + 4 * k + j] for j in range(4)]
            c = jnp.where(good, compute[h * TASKS + k], h)
            left = fetch(s1, table[s1, FACTOR_ROUTE + h], c)
            right = fetch(s2, table[s2, FACTOR_ROUTE + h], c)
            t = load[c]
            load[c] = t + 1
            row = jnp.where(c == mine, t, FAST)
            plan[row, 0] = left
            plan[row, 1] = right
            plan[row, 2] = s3 * APG + table[s3, h]
            plan[row, 3] = o * TPG + table[o, TARGET + h]
        return 0

    for g in range(groups):
        load[g] = 0
    lax.fori_loop(0, groups, deal, 0)


def assign(me, table):
    groups = table.shape[0]
    smem = pl.BlockSpec(memory_space=pltpu.SMEM)
    one = lambda n: pltpu.SMEM((n,), jnp.int32)
    tasks = groups * TASKS
    return pl.pallas_call(
        assign_kernel,
        in_specs=[smem, smem],
        out_specs=[smem] * 4,
        out_shape=[
            jax.ShapeDtypeStruct((2 * FPG,), jnp.int32),
            jax.ShapeDtypeStruct(((groups + 1) * FPG,), jnp.int32),
            jax.ShapeDtypeStruct((2 * FAST, 4), jnp.int32),
            jax.ShapeDtypeStruct((1,), jnp.int32),
        ],
        scratch_shapes=[one(tasks)] * 4 + [one(groups)] * 2 + [one(groups * FPG)] + [one(groups)] * 2 + [one(groups * FPG)],
        name="assign",
    )(me, table)


def cut_kernel(send, block, out):
    rows = out.shape[2]
    for piece in range(out.shape[0]):
        half, part = divmod(piece, block.shape[2] // LANES)
        out[piece, 0] = block[0, half * rows : (half + 1) * rows, part * LANES : (part + 1) * LANES]


def cut_blocks(send, factors, count, pieces):
    _, rows, width = factors.shape
    piece_rows = rows * width // LANES // pieces
    return pl.pallas_call(
        cut_kernel,
        grid_spec=pltpu.PrefetchScalarGridSpec(
            num_scalar_prefetch=1,
            grid=(count,),
            in_specs=[pl.BlockSpec((1, rows, width), lambda i, send: (send[i], 0, 0))],
            out_specs=pl.BlockSpec((pieces, 1, piece_rows, LANES), lambda i, send: (0, i, 0, 0)),
        ),
        out_shape=jax.ShapeDtypeStruct((pieces, count, piece_rows, LANES), factors.dtype),
        compiler_params=pltpu.CompilerParams(dimension_semantics=("arbitrary",)),
        name="cut_blocks",
    )(send, factors)


def spread(block, axis):
    members = lax.axis_size(axis)
    me = lax.axis_index(axis)
    held = block[None]
    bit = 1
    while bit < members:
        other = lax.ppermute(held, axis, [(i, i ^ bit) for i in range(members)])
        mine_first = (me & bit) == 0
        held = jnp.where(
            mine_first, jnp.concatenate([held, other]), jnp.concatenate([other, held])
        )
        bit *= 2
    return held


def group_blocks(amplitudes, factor_route, amp_route, task_list, target_tile):
    groups = lax.axis_size("group")
    tiles, _, width = amplitudes.shape
    rows = lax.dynamic_index_in_dim(amplitudes, lax.axis_index("shard"), 1, keepdims=False)
    facts = jnp.concatenate([amp_route[0], factor_route[0], target_tile[0], task_list[0].reshape(-1)])
    facts = jnp.pad(facts, (0, width - facts.shape[0])).astype(rows.dtype)
    block = jnp.concatenate([rows, facts[None], jnp.zeros((8 - tiles - 1, width), rows.dtype)])
    held = lax.all_to_all(
        jnp.broadcast_to(block[None], (groups, *block.shape)), "group", split_axis=0, concat_axis=0, tiled=True
    )
    return held[:, :tiles].reshape(groups * tiles, width), held[:, tiles, :LANES].astype(jnp.int32)


def contributions(blocks_sent, slots, factors, amp_rows, send, pick, plan):
    groups = lax.axis_size("group")
    width = factors.shape[2]
    cut = cut_blocks(send, factors, blocks_sent, groups)
    held = lax.all_to_all(cut, "group", split_axis=0, concat_axis=0, tiled=True)
    chosen = amp_rows.at[plan[:FAST, 2]].get(mode="promise_in_bounds")
    amps = spread(chosen.reshape(FAST, width // LANES, LANES), "shard")
    amps = amps.reshape(-1, FAST, width).transpose(1, 0, 2)
    wanted = pick[: groups * FPG].reshape(groups, FPG)[:, :slots].reshape(-1)
    dealt = held.reshape(groups * blocks_sent, *held.shape[2:]).at[wanted].get(mode="promise_in_bounds")
    dealt = dealt.reshape(groups, slots, *held.shape[2:])
    arrived = lax.all_to_all(dealt, "group", split_axis=0, concat_axis=0, tiled=True)
    return ladder(plan, factors, arrived, amps)


def body(factors, amplitudes, factor_route, amp_route, task_list, target_tile):
    groups = lax.axis_size("group")
    amp_rows, table = group_blocks(amplitudes, factor_route, amp_route, task_list, target_tile)
    me = lax.axis_index("group").astype(jnp.int32).reshape(1)
    send, pick, plan, balanced = assign(me, table)
    operands = (factors, amp_rows, send, pick, plan)
    parts = lax.cond(
        balanced[0] == 1,
        functools.partial(contributions, FAST, FAST),
        functools.partial(contributions, FPG, 2 * TASKS),
        *operands,
    )
    pieces = lax.all_to_all(parts, "shard", split_axis=0, concat_axis=0, tiled=True)
    returns = combine(plan, pieces, groups * TPG)
    arrived = lax.all_to_all(returns, "group", split_axis=0, concat_axis=0, tiled=True)
    return owned(arrived.reshape(groups, TPG, *arrived.shape[1:]))


def solution(mesh):
    return jax.shard_map(
        body,
        mesh=mesh,
        in_specs=(
            P("group", "shard", None),
            P("group", None, None),
            P("group", None),
            P("group", None),
            P("group", None, None),
            P("group", None),
        ),
        out_specs=P("group", None, "shard"),
        check_vma=False,
    )
```

time: 235 us -> 200 us (0.85)
  waiting for transfers between devices: 116 us -> 53.2 us
  Pallas kernels: 19.3 us -> 29.2 us
  other arithmetic: 4.39 us -> 12.3 us
  starting transfers between devices: 39.7 us -> 43.6 us
    all_to_all x2 -> x3, waiting for transfers between devices: 106 us -> 48.9 us  [the longest x1 37.5 us: contributions(): held = lax.all_to_all(cut, 'group', split_axis=0, concat_axis=0, tiled=True)]
    pallas_call x1 -> x3, Pallas kernels: 1.62 us -> 11.1 us  [the longest x1 5.23 us: assign(): pl.pallas_call(assign_kernel, in_specs=[smem, smem], out_specs=[smem] * 4...]
    ppermute x5, waiting for transfers between devices: 10.4 us -> 4.32 us  [spread(): other = lax.ppermute(held, axis, [(i, i ^ bit) for i in range(members)])]
    select_n x7, other arithmetic: 0.16 us -> 5.54 us  [spread(): jnp.where(mine_first, jnp.concatenate([held, other]), jnp.concatenate([ot...]
    concatenate x5, local copies, waits for them, and re-layouts: 0.11 us -> 4.87 us  [spread(): jnp.concatenate([held, other])]
    all_to_all x2 -> x3, starting transfers between devices: 16.1 us -> 19.9 us  [the longest x1 10 us: group_blocks(): lax.all_to_all(jnp.broadcast_to(block[None], (groups, *block.shape)), 'gr...]
    gather x3 -> x2, local copies, waits for them, and re-layouts: 4.74 us -> 2.5 us  [the longest x1 1.93 us: contributions(): held.reshape(groups * blocks_sent, *held.shape[2:]).at[wanted]]
  transfers between devices with their start and end apart: 7 -> 8, of which waited for: 6 -> 5; matrix products, arithmetic and copies ran while one was open for 3% -> 8% of each run, Pallas kernels for 0% -> 0%
where the time goes in v4:
time: 200 us; the launch traced here: 197 us
  waiting for transfers between devices  53.2 us (27%)
  blocking collectives  48.9 us (24%)
  starting transfers between devices  43.6 us (22%)
  Pallas kernels  29.2 us (15%)
  other arithmetic  12.3 us (6%)
  local copies, waits for them, and re-layouts  9.22 us (5%)
    all_to_all x1, waiting for transfers between devices, contributions(): held = lax.all_to_all(cut, 'group', split_axis=0, concat_axis=0, tiled=True)  37.5 us
    all_to_all x1, blocking collectives, body(): lax.all_to_all(parts, 'shard', split_axis=0, concat_axis=0, tiled=True)  26.8 us
    ppermute x5, starting transfers between devices, spread(): other = lax.ppermute(held, axis, [(i, i ^ bit) for i in range(members)])  23.7 us
    all_to_all x1, blocking collectives, body(): lax.all_to_all(returns, 'group', split_axis=0, concat_axis=0, tiled=True)  22.2 us
    pallas_call x1, Pallas kernels, ladder(): pl.pallas_call(ladder_kernel, grid_spec=pltpu.PrefetchScalarGridSpec(num_...  16.4 us
    all_to_all x1, waiting for transfers between devices, group_blocks(): lax.all_to_all(jnp.broadcast_to(block[None], (groups, *block.shape)), 'gr...  11.5 us
    all_to_all x1, starting transfers between devices, group_blocks(): lax.all_to_all(jnp.broadcast_to(block[None], (groups, *block.shape)), 'gr...  10 us
    select_n x7, other arithmetic, spread(): jnp.where(mine_first, jnp.concatenate([held, other]), jnp.concatenate([ot...  5.54 us
  transfers between devices with their start and end apart: 8, of which 5 were waited for; matrix products, arithmetic and copies ran while one was open for 8% of the time, Pallas kernels for 0%

profile of v4, /device:TPU:8, one launch (start us, length us, event | category | flops | bytes accessed | tf_op | source)
XLA Modules:
  0.0 197.3 jit_solution(2968074800041969112)
XLA Ops:
  0.0 0.7 convert_reduce_fusion
  0.7 0.1 reshape_squeeze.4
  0.8 0.7 convert_bitcast_fusion.2
  1.5 0.7 convert_bitcast_fusion
  2.2 0.1 fusion.27
  2.3 0.1 pad.72.clone
  2.4 0.1 maximum_maximum_fusion
  2.5 0.7 broadcast_in_dim.8
  3.2 10.0 %all-to-all-start.4 = ((bf16[16,8,1024]{2,1,0:T(8,128)(2,1)}), bf16[16,8,1024]{2,1,0:T(8,128)(2,1)S(1)}, u32[]{:S(2)}, u32[]{:S(2)}) async-start(bf16[16,8,1024]{2,1,0:T(8,128)(2,1)} %broadcast_in_dim.8), calls=%async_computation.4 | async-start | bytes 524288 | tf_op jit(solution)/shard_map/all_to_all | solution.py:386
  13.2 11.5 %all-to-all-done.4 = bf16[16,8,1024]{2,1,0:T(8,128)(2,1)S(1)} async-done(((bf16[16,8,1024]{2,1,0:T(8,128)(2,1)}), bf16[16,8,1024]{2,1,0:T(8,128)(2,1)S(1)}, u32[]{:S(2)}, u32[]{:S(2)}) %all-to-all-start.4) | async-done | bytes 262176 | tf_op jit(solution)/shard_map/all_to_all | solution.py:386
  24.7 0.6 fusion.24.table
  25.3 5.2 %assign.1 = (s32[16]{0:T(128)S(1)}, s32[136]{0:T(256)S(1)}, s32[8,4]{1,0:T(8,128)S(1)}, s32[1]{0:T(128)}) custom-call(s32[1]{0:T(128)} %bitcast.10.me, s32[16,128]{1,0:T(8,128)} %fusion.24.table), custom_call_target="tpu_custom_call" | custom-call | tf_op jit(solution)/shard_map/assign/pallas_call | solution.py:325
  31.3 113.8 %conditional.1 = (f32[32,4,8,128]{3,2,1,0:T(8,128)}) conditional(s32[]{:T(128)} %bitcast.15, (s32[16]{0:T(128)S(1)}, bf16[8,192,1024]{2,1,0:T(8,128)(2,1)}, s32[136]{0:T(256)S(1)}, s32[8,4]{1,0:T(8,128)S(1)}, bf16[64,1024]{1,0:T(8,128)(2,1)S(1)}) %tuple.11, (s32[16]{0:T(128)S(1)}, bf16[8,192,1024]{2,1,0:T(8,128)(2,1)}, s32[136]{0:T(256)S(1)}, ...), branch_computations={%region_0.1_spmd, %region_1.2_spmd} | conditional | flops 6789432 | bytes 39252764 | solution.py:413
  31.3 4.3 %cut_blocks.3 = bf16[16,4,96,128]{3,2,1,0:T(8,128)(2,1)} custom-call(s32[16]{0:T(128)S(1)} %get-tuple-element.35.send, bf16[8,192,1024]{2,1,0:T(8,128)(2,1)} %get-tuple-element.34.block.left_whole.right_whole), custom_call_target="tpu_custom_call" | custom-call | tf_op jit(solution)/shard_map/cond/branch_1_fun/cut_blocks/pallas_call | solution.py:350
  35.6 4.7 %all-to-all-start.2 = ((bf16[16,4,96,128]{3,2,1,0:T(8,128)(2,1)}), bf16[16,4,96,128]{3,2,1,0:T(8,128)(2,1)S(1)}, u32[]{:S(2)}, u32[]{:S(2)}) async-start(bf16[16,4,96,128]{3,2,1,0:T(8,128)(2,1)} %cut_blocks.3), calls=%async_computation.2 | async-start | bytes 3145728 | tf_op jit(solution)/shard_map/cond/branch_1_fun/all_to_all | solution.py:396
  40.2 0.1 reshape.353
  40.3 0.1 reshape.354
  40.5 37.5 %all-to-all-done.2 = bf16[16,4,96,128]{3,2,1,0:T(8,128)(2,1)S(1)} async-done(((bf16[16,4,96,128]{3,2,1,0:T(8,128)(2,1)}), bf16[16,4,96,128]{3,2,1,0:T(8,128)(2,1)S(1)}, u32[]{:S(2)}, u32[]{:S(2)}) %all-to-all-start.2) | async-done | bytes 1572896 | tf_op jit(solution)/shard_map/cond/branch_1_fun/all_to_all | solution.py:396
  77.9 1.9 gather_fusion.2
  79.8 5.2 %all-to-all-start.3 = ((bf16[16,4,96,128]{3,2,1,0:T(8,128)(2,1)}), bf16[16,4,96,128]{3,2,1,0:T(8,128)(2,1)}, u32[]{:S(2)}, u32[]{:S(2)}) async-start(bf16[16,4,96,128]{3,2,1,0:T(8,128)(2,1)} %bitcast.7), calls=%async_computation.3 | async-start | bytes 3145728 | tf_op jit(solution)/shard_map/cond/branch_1_fun/all_to_all | solution.py:403
  85.1 0.2 fusion.18
  85.3 0.6 gather_fusion.3
  85.9 2.1 %collective-permute-start.5 = (bf16[1,4,8,128]{3,2,0,1:T(8,128)(2,1)S(1)}, bf16[1,4,8,128]{3,2,0,1:T(8,128)(2,1)S(1)}, u32[]{:S(2)}, u32[]{:S(2)}) collective-permute-start(bf16[1,4,8,128]{3,2,0,1:T(8,128)(2,1)S(1)} %bitcast.98), channel_id=1, source_target_pairs={{0,1},{1,0},{2,3},{3,2},{4,5},{5,4},{6,7},{7,6},{8,9},{9,8},{10,11... | collective-permute-start | bytes 24584 | tf_op jit(solution)/shard_map/cond/branch_1_fun/ppermute | solution.py:370
  87.9 1.1 collective-permute-done.5
  89.1 4.3 %collective-permute-start.6 = (bf16[2,4,8,128]{3,2,0,1:T(8,128)(2,1)S(1)}, bf16[2,4,8,128]{3,2,0,1:T(8,128)(2,1)S(1)}, u32[]{:S(2)}, u32[]{:S(2)}) collective-permute-start(bf16[2,4,8,128]{3,2,0,1:T(8,128)(2,1)S(1)} %maximum_select_fusion.15), channel_id=1, source_target_pairs={{0,2},{1,3},{2,0},{3,1},{4,6},{5,7},{6,4},{7,5},{8,10},{9,11},{10,... | collective-permute-start | bytes 49160 | tf_op jit(solution)/shard_map/cond/branch_1_fun/ppermute | solution.py:370
  93.4 1.7 collective-permute-done.6
  95.1 6.1 %collective-permute-start.7 = (bf16[4,4,8,128]{3,2,0,1:T(8,128)(2,1)S(1)}, bf16[4,4,8,128]{3,2,0,1:T(8,128)(2,1)S(1)}, u32[]{:S(2)}, u32[]{:S(2)}) collective-permute-start(bf16[4,4,8,128]{3,2,0,1:T(8,128)(2,1)S(1)} %maximum_select_fusion.14), channel_id=1, source_target_pairs={{0,4},{1,5},{2,6},{3,7},{4,0},{5,1},{6,2},{7,3},{8,12},{9,13},{10,... | collective-permute-start | bytes 98312 | tf_op jit(solution)/shard_map/cond/branch_1_fun/ppermute | solution.py:370
  101.2 1.9 and_convert_fusion.1.swap
  103.1 0.6 concatenate.106
  103.7 0.6 concatenate.107
  104.4 0.6 copy-done.4
  105.0 0.8 maximum_select_fusion.12
  105.8 8.8 %collective-permute-start.8 = (bf16[8,4,8,128]{3,2,0,1:T(8,128)(2,1)S(1)}, bf16[8,4,8,128]{3,2,0,1:T(8,128)(2,1)S(1)}, u32[]{:S(2)}, u32[]{:S(2)}) collective-permute-start(bf16[8,4,8,128]{3,2,0,1:T(8,128)(2,1)S(1)} %maximum_select_fusion.12), channel_id=1, source_target_pairs={{0,8},{1,9},{2,10},{3,11},{4,12},{5,13},{6,14},{7,15},{8,0},{9,1},... | collective-permute-start | bytes 196616 | tf_op jit(solution)/shard_map/cond/branch_1_fun/ppermute | solution.py:370
  114.6 1.5 maximum_select_fusion.13
  116.1 1.4 concatenate.112
  117.5 0.7 maximum_select_fusion.10
  118.1 2.5 %collective-permute-start.9 = (bf16[16,4,8,128]{3,2,0,1:T(8,128)(2,1)}, bf16[16,4,8,128]{3,2,0,1:T(8,128)(2,1)}, u32[]{:S(2)}, u32[]{:S(2)}) collective-permute-start(bf16[16,4,8,128]{3,2,0,1:T(8,128)(2,1)} %maximum_select_fusion.10), channel_id=1, source_target_pairs={{0,16},{1,17},{2,18},{3,19},{4,20},{5,21},{6,22},{7,23},{8,24},{9,... | collective-permute-start | bytes 393224 | tf_op jit(solution)/shard_map/cond/branch_1_fun/ppermute | solution.py:370
  120.6 1.5 maximum_select_fusion.11
  122.2 0.7 concatenate.117
  122.8 1.0 maximum_select_fusion.9
  123.8 1.5 collective-permute-done.9
  125.3 1.6 concatenate.122
  126.9 1.8 fusion.10.amp
  128.7 16.4 %ladder.3 = f32[32,4,8,128]{3,2,1,0:T(8,128)} custom-call(s32[8,4]{1,0:T(8,128)S(1)} %get-tuple-element.33.plan, bf16[8,192,1024]{2,1,0:T(8,128)(2,1)S(1)} %copy-done.2, bf16[16,4,96,128]{3,2,1,0:T(8,128)(2,1)} %all-to-all-done.3.left_cut.right_cut, bf16[8,192,1024]{2,1,0:T(8,128)(2,1)S(1)} %copy-done.2, ...), custom_call_target="tpu_custom_call" | custom-call | tf_op jit(solution)/shard_map/cond/branch_1_fun/ladder/pallas_call | solution.py:131
  145.0 26.8 %all_to_all.31.pieces = f32[32,4,8,128]{3,2,1,0:T(8,128)} all-to-all(f32[32,4,8,128]{3,2,1,0:T(8,128)} %get-tuple-element.52), channel_id=1, replica_groups=mesh['group'=16,'shard'=32] {'shard'}, dimensions={0} | all-to-all | bytes 1048576 | tf_op jit(solution)/shard_map/all_to_all | solution.py:419
  171.8 1.8 combine.1
  173.6 22.2 %all_to_all.32 = f32[32,8,128]{2,1,0:T(8,128)} all-to-all(f32[32,8,128]{2,1,0:T(8,128)} %combine.1), channel_id=1, replica_groups=mesh['group'=16,'shard'=32] {'group'}, dimensions={0} | all-to-all | bytes 262144 | tf_op jit(solution)/shard_map/all_to_all | solution.py:421
  195.7 1.6 owned.1
  (25 shorter events, 0.2 us)
Async XLA Ops:
  0.0 2.3 %copy-start = (bf16[4,32,1024]{2,1,0:T(8,128)(2,1)S(1)}, bf16[4,32,1024]{2,1,0:T(8,128)(2,1)}, u32[]{:S(2)}) copy-start(bf16[4,32,1024]{2,1,0:T(8,128)(2,1)} %param.9) | copy-start | bytes 786436
  3.2 21.5 %all-to-all-start.4 = ((bf16[16,8,1024]{2,1,0:T(8,128)(2,1)}), bf16[16,8,1024]{2,1,0:T(8,128)(2,1)S(1)}, u32[]{:S(2)}, u32[]{:S(2)}) async-start(bf16[16,8,1024]{2,1,0:T(8,128)(2,1)} %broadcast_in_dim.8), calls=%async_computation.4 | async-start | bytes 524288 | tf_op jit(solution)/shard_map/all_to_all | solution.py:386
  35.6 42.3 %all-to-all-start.2 = ((bf16[16,4,96,128]{3,2,1,0:T(8,128)(2,1)}), bf16[16,4,96,128]{3,2,1,0:T(8,128)(2,1)S(1)}, u32[]{:S(2)}, u32[]{:S(2)}) async-start(bf16[16,4,96,128]{3,2,1,0:T(8,128)(2,1)} %cut_blocks.3), calls=%async_computation.2 | async-start | bytes 3145728 | tf_op jit(solution)/shard_map/cond/branch_1_fun/all_to_all | solution.py:396
  79.8 48.8 %all-to-all-start.3 = ((bf16[16,4,96,128]{3,2,1,0:T(8,128)(2,1)}), bf16[16,4,96,128]{3,2,1,0:T(8,128)(2,1)}, u32[]{:S(2)}, u32[]{:S(2)}) async-start(bf16[16,4,96,128]{3,2,1,0:T(8,128)(2,1)} %bitcast.7), calls=%async_computation.3 | async-start | bytes 3145728 | tf_op jit(solution)/shard_map/cond/branch_1_fun/all_to_all | solution.py:403
  85.1 43.6 %copy-start.2 = (bf16[8,192,1024]{2,1,0:T(8,128)(2,1)S(1)}, bf16[8,192,1024]{2,1,0:T(8,128)(2,1)}, u32[]{:S(2)}) copy-start(bf16[8,192,1024]{2,1,0:T(8,128)(2,1)} %get-tuple-element.34.block.left_whole.right_whole) | copy-start | bytes 9437188 | tf_op jit(solution)/shard_map/cond
  85.9 3.2 %collective-permute-start.5 = (bf16[1,4,8,128]{3,2,0,1:T(8,128)(2,1)S(1)}, bf16[1,4,8,128]{3,2,0,1:T(8,128)(2,1)S(1)}, u32[]{:S(2)}, u32[]{:S(2)}) collective-permute-start(bf16[1,4,8,128]{3,2,0,1:T(8,128)(2,1)S(1)} %bitcast.98), channel_id=1, source_target_pairs={{0,1},{1,0},{2,3},{3,2},{4,5},{5,4},{6,7},{7,6},{8,9},{9,8},{10,11... | collective-permute-start | bytes 24584 | tf_op jit(solution)/shard_map/cond/branch_1_fun/ppermute | solution.py:370
  89.1 6.0 %collective-permute-start.6 = (bf16[2,4,8,128]{3,2,0,1:T(8,128)(2,1)S(1)}, bf16[2,4,8,128]{3,2,0,1:T(8,128)(2,1)S(1)}, u32[]{:S(2)}, u32[]{:S(2)}) collective-permute-start(bf16[2,4,8,128]{3,2,0,1:T(8,128)(2,1)S(1)} %maximum_select_fusion.15), channel_id=1, source_target_pairs={{0,2},{1,3},{2,0},{3,1},{4,6},{5,7},{6,4},{7,5},{8,10},{9,11},{10,... | collective-permute-start | bytes 49160 | tf_op jit(solution)/shard_map/cond/branch_1_fun/ppermute | solution.py:370
  95.1 9.3 %copy-start.6 = (bf16[4,4,8,128]{3,2,0,1:T(8,128)(2,1)}, bf16[4,4,8,128]{3,2,0,1:T(8,128)(2,1)S(1)}, u32[]{:S(2)}) copy-start(bf16[4,4,8,128]{3,2,0,1:T(8,128)(2,1)S(1)} %maximum_select_fusion.14) | copy-start | bytes 98308 | tf_op jit(solution)/shard_map/cond
  95.1 9.3 %collective-permute-start.7 = (bf16[4,4,8,128]{3,2,0,1:T(8,128)(2,1)S(1)}, bf16[4,4,8,128]{3,2,0,1:T(8,128)(2,1)S(1)}, u32[]{:S(2)}, u32[]{:S(2)}) collective-permute-start(bf16[4,4,8,128]{3,2,0,1:T(8,128)(2,1)S(1)} %maximum_select_fusion.14), channel_id=1, source_target_pairs={{0,4},{1,5},{2,6},{3,7},{4,0},{5,1},{6,2},{7,3},{8,12},{9,13},{10,... | collective-permute-start | bytes 98312 | tf_op jit(solution)/shard_map/cond/branch_1_fun/ppermute | solution.py:370
  104.3 0.6 copy-start.4
  105.8 11.6 %collective-permute-start.8 = (bf16[8,4,8,128]{3,2,0,1:T(8,128)(2,1)S(1)}, bf16[8,4,8,128]{3,2,0,1:T(8,128)(2,1)S(1)}, u32[]{:S(2)}, u32[]{:S(2)}) collective-permute-start(bf16[8,4,8,128]{3,2,0,1:T(8,128)(2,1)S(1)} %maximum_select_fusion.12), channel_id=1, source_target_pairs={{0,8},{1,9},{2,10},{3,11},{4,12},{5,13},{6,14},{7,15},{8,0},{9,1},... | collective-permute-start | bytes 196616 | tf_op jit(solution)/shard_map/cond/branch_1_fun/ppermute | solution.py:370
  118.1 7.2 %collective-permute-start.9 = (bf16[16,4,8,128]{3,2,0,1:T(8,128)(2,1)}, bf16[16,4,8,128]{3,2,0,1:T(8,128)(2,1)}, u32[]{:S(2)}, u32[]{:S(2)}) collective-permute-start(bf16[16,4,8,128]{3,2,0,1:T(8,128)(2,1)} %maximum_select_fusion.10), channel_id=1, source_target_pairs={{0,16},{1,17},{2,18},{3,19},{4,20},{5,21},{6,22},{7,23},{8,24},{9,... | collective-permute-start | bytes 393224 | tf_op jit(solution)/shard_map/cond/branch_1_fun/ppermute | solution.py:370

commit v5 on v4

--- a/solution.py
+++ b/solution.py
@@ -103,7 +103,7 @@
         lanes = slice(group * LANES, (group + 1) * LANES)
         tiles = [result[i * band : (i + 1) * band, lanes] for i in range(FOLD)]
         for a, tile in enumerate(swap_lane_blocks(tiles)):
-            out[group * FOLD + a, 0] = tile
+            out[group * FOLD + a, 0] = tile.astype(out.dtype)
 
 
 def ladder(plan, factors, arrived, amps):
@@ -152,14 +152,14 @@
                 pltpu.VMEM((occupied, width), jnp.float32),
             ],
         ),
-        out_shape=jax.ShapeDtypeStruct((VB, tasks, band, LANES), jnp.float32),
+        out_shape=jax.ShapeDtypeStruct((VB, tasks, band, LANES), jnp.bfloat16),
         compiler_params=pltpu.CompilerParams(dimension_semantics=("arbitrary",)),
         name="ladder",
     )(plan, factors, arrived, factors, arrived, amps, swap)
 
 
 def combine_kernel(plan, pieces, out):
-    total = jnp.sum(pieces[...], axis=0)
+    total = jnp.sum(pieces[...].astype(jnp.float32), axis=0)
     out[...] = jnp.zeros_like(out)
     for k in range(pieces.shape[1]):
         target = plan[k, 3]
@@ -211,12 +211,13 @@
         slots[g] = 0
 
     def clear(i, _):
-        uses[i] = 0
-        where_sent[i] = -1
-        pick[i] = 0
-        return 0
-
-    lax.fori_loop(0, groups * FPG, clear, 0)
+        for j in range(FPG):
+            uses[i * FPG + j] = 0
+            where_sent[i * FPG + j] = -1
+            pick[i * FPG + j] = 0
+        return 0
+
+    lax.fori_loop(0, groups, clear, 0)
     for i in range(send.shape[0]):
         send[i] = 0
     for k in range(plan.shape[0]):
@@ -231,7 +232,7 @@
             n1, n2 = uses[s1 * FPG + b1], uses[s2 * FPG + b2]
             at_first = 2 * load[s1] - jnp.where(n2 > 0, 0, FAST - sent[s2])
             at_second = 2 * load[s2] - jnp.where(n1 > 0, 0, FAST - sent[s1])
-            second = at_first > at_second
+            second = (at_first > at_second) & (s1 != s2)
             c, o = jnp.where(second, s2, s1), jnp.where(second, s1, s2)
             y, x = jnp.where(second, b2, b1), jnp.where(second, b1, b2)
             n = jnp.where(second, n1, n2)
@@ -297,24 +298,43 @@
         pick[jnp.where(remote, c * FPG + slot, groups * FPG)] = source * stride + at
         return jnp.where(remote, FPG + slot, block)
 
-    def deal(h, _):
+    def note(h, k, c, left, right):
+        o, s3 = table[h, RECORDS + 4 * k], table[h, RECORDS + 4 * k + 3]
+        t = load[c]
+        load[c] = t + 1
+        row = jnp.where(c == mine, t, FAST)
+        plan[row, 0] = left
+        plan[row, 1] = right
+        plan[row, 2] = s3 * (APG + 1) + table[s3, h]
+        plan[row, 3] = o * TPG + table[o, TARGET + h]
+
+    def deal_balanced(h, _):
         for k in range(TASKS):
-            o, s1, s2, s3 = [table[h, RECORDS + 4 * k + j] for j in range(4)]
-            c = jnp.where(good, compute[h * TASKS + k], h)
-            left = fetch(s1, table[s1, FACTOR_ROUTE + h], c)
-            right = fetch(s2, table[s2, FACTOR_ROUTE + h], c)
-            t = load[c]
-            load[c] = t + 1
-            row = jnp.where(c == mine, t, FAST)
-            plan[row, 0] = left
-            plan[row, 1] = right
-            plan[row, 2] = s3 * APG + table[s3, h]
-            plan[row, 3] = o * TPG + table[o, TARGET + h]
+            i = h * TASKS + k
+            c, y = compute[i], compute_block[i]
+            found = fetch(other[i], other_block[i], c)
+            first = c == table[h, RECORDS + 4 * k + 1]
+            note(h, k, c, jnp.where(first, y, found), jnp.where(first, found, y))
+        return 0
+
+    def deal_at_helper(h, _):
+        for k in range(TASKS):
+            s1, s2 = table[h, RECORDS + 4 * k + 1], table[h, RECORDS + 4 * k + 2]
+            left = fetch(s1, table[s1, FACTOR_ROUTE + h], h)
+            right = fetch(s2, table[s2, FACTOR_ROUTE + h], h)
+            note(h, k, h, left, right)
         return 0
 
     for g in range(groups):
         load[g] = 0
-    lax.fori_loop(0, groups, deal, 0)
+
+    @pl.when(good)
+    def _():
+        lax.fori_loop(0, groups, deal_balanced, 0)
+
+    @pl.when(jnp.logical_not(good))
+    def _():
+        lax.fori_loop(0, groups, deal_at_helper, 0)
 
 
 def assign(me, table):
@@ -337,79 +357,103 @@
     )(me, table)
 
 
-def cut_kernel(send, block, out):
+def cut_kernel(block, out):
     rows = out.shape[2]
     for piece in range(out.shape[0]):
         half, part = divmod(piece, block.shape[2] // LANES)
         out[piece, 0] = block[0, half * rows : (half + 1) * rows, part * LANES : (part + 1) * LANES]
 
 
-def cut_blocks(send, factors, count, pieces):
-    _, rows, width = factors.shape
+def cut_blocks(factors, pieces):
+    count, rows, width = factors.shape
     piece_rows = rows * width // LANES // pieces
+    size = factors.size * 2
     return pl.pallas_call(
         cut_kernel,
-        grid_spec=pltpu.PrefetchScalarGridSpec(
-            num_scalar_prefetch=1,
-            grid=(count,),
-            in_specs=[pl.BlockSpec((1, rows, width), lambda i, send: (send[i], 0, 0))],
-            out_specs=pl.BlockSpec((pieces, 1, piece_rows, LANES), lambda i, send: (0, i, 0, 0)),
-        ),
+        grid=(count,),
+        in_specs=[pl.BlockSpec((1, rows, width), lambda i: (i, 0, 0))],
+        out_specs=pl.BlockSpec((pieces, 1, piece_rows, LANES), lambda i: (0, i, 0, 0)),
         out_shape=jax.ShapeDtypeStruct((pieces, count, piece_rows, LANES), factors.dtype),
         compiler_params=pltpu.CompilerParams(dimension_semantics=("arbitrary",)),
+        cost_estimate=pl.CostEstimate(flops=0, bytes_accessed=2 * size, transcendentals=0),
         name="cut_blocks",
-    )(send, factors)
-
-
-def spread(block, axis):
+    )(factors)
+
+
+def spread(held, axis, bits):
     members = lax.axis_size(axis)
     me = lax.axis_index(axis)
-    held = block[None]
-    bit = 1
-    while bit < members:
+    for bit in bits:
         other = lax.ppermute(held, axis, [(i, i ^ bit) for i in range(members)])
         mine_first = (me & bit) == 0
         held = jnp.where(
             mine_first, jnp.concatenate([held, other]), jnp.concatenate([other, held])
         )
-        bit *= 2
     return held
 
 
-def group_blocks(amplitudes, factor_route, amp_route, task_list, target_tile):
+def facts_kernel(shard, amplitudes, amp_route, factor_route, target_tile, task_list, out):
+    tiles, occupied, width = amplitudes.shape
+    chosen = lax.broadcasted_iota(jnp.int32, (occupied, width), 0) == shard[0]
+    facts = [amp_route[...], factor_route[...], target_tile[...]]
+    facts += [task_list[0, k : k + 1, :] for k in range(TASKS)]
+    facts = jnp.concatenate(facts, axis=1).astype(jnp.float32)
+    facts = jnp.concatenate([facts, jnp.zeros((1, LANES - facts.shape[1]), jnp.float32)], axis=1)
+    parts = width // LANES
+    for i in range(tiles + 1):
+        if i < tiles:
+            row = jnp.sum(jnp.where(chosen, amplitudes[i].astype(jnp.float32), 0.0), axis=0, keepdims=True)
+            rows = [row[:, c * LANES : (c + 1) * LANES] for c in range(parts)]
+        else:
+            rows = [facts] + [jnp.zeros_like(facts)] * (parts - 1)
+        tile = jnp.concatenate(rows, axis=0).astype(out.dtype)
+        for g in range(out.shape[0]):
+            out[g, i] = tile
+
+
+def group_facts(amplitudes, factor_route, amp_route, task_list, target_tile):
     groups = lax.axis_size("group")
     tiles, _, width = amplitudes.shape
-    rows = lax.dynamic_index_in_dim(amplitudes, lax.axis_index("shard"), 1, keepdims=False)
-    facts = jnp.concatenate([amp_route[0], factor_route[0], target_tile[0], task_list[0].reshape(-1)])
-    facts = jnp.pad(facts, (0, width - facts.shape[0])).astype(rows.dtype)
-    block = jnp.concatenate([rows, facts[None], jnp.zeros((8 - tiles - 1, width), rows.dtype)])
-    held = lax.all_to_all(
-        jnp.broadcast_to(block[None], (groups, *block.shape)), "group", split_axis=0, concat_axis=0, tiled=True
-    )
-    return held[:, :tiles].reshape(groups * tiles, width), held[:, tiles, :LANES].astype(jnp.int32)
-
-
-def contributions(blocks_sent, slots, factors, amp_rows, send, pick, plan):
-    groups = lax.axis_size("group")
+    shard = lax.axis_index("shard").astype(jnp.int32).reshape(1)
+    vmem = pl.BlockSpec(memory_space=pltpu.VMEM)
+    facts = pl.pallas_call(
+        facts_kernel,
+        in_specs=[pl.BlockSpec(memory_space=pltpu.SMEM)] + [vmem] * 5,
+        out_specs=vmem,
+        out_shape=jax.ShapeDtypeStruct((groups, tiles + 1, width // LANES, LANES), amplitudes.dtype),
+        name="facts",
+    )(shard, amplitudes, amp_route, factor_route, target_tile, task_list)
+    held = lax.all_to_all(facts, "group", split_axis=0, concat_axis=0, tiled=True)
+    return held.reshape(groups * (tiles + 1), *held.shape[2:]), held[:, tiles, 0].astype(jnp.int32)
+
+
+def contributions(blocks_sent, slots, factors, cut, amp_rows, send, pick, plan):
+    groups, count = cut.shape[:2]
     width = factors.shape[2]
-    cut = cut_blocks(send, factors, blocks_sent, groups)
-    held = lax.all_to_all(cut, "group", split_axis=0, concat_axis=0, tiled=True)
+    piece = cut.shape[2:]
+    order = jnp.arange(groups, dtype=jnp.int32)[:, None] * count + send[None, :blocks_sent]
+    leaving = cut.reshape(groups * count, *piece).at[order.reshape(-1)].get(mode="promise_in_bounds")
+    leaving = leaving.reshape(groups, blocks_sent, *piece)
+    held = lax.all_to_all(leaving, "group", split_axis=0, concat_axis=0, tiled=True)
     chosen = amp_rows.at[plan[:FAST, 2]].get(mode="promise_in_bounds")
-    amps = spread(chosen.reshape(FAST, width // LANES, LANES), "shard")
+    amps = spread(chosen[None], "shard", (1, 2, 4))
+    held, amps = lax.optimization_barrier((held, amps))
+    wanted = pick[: groups * FPG].reshape(groups, FPG)[:, :slots].reshape(-1)
+    dealt = held.reshape(groups * blocks_sent, *piece).at[wanted].get(mode="promise_in_bounds")
+    dealt = dealt.reshape(groups, slots, *piece)
+    arrived = lax.all_to_all(dealt, "group", split_axis=0, concat_axis=0, tiled=True)
+    amps = spread(amps, "shard", (8, 16))
     amps = amps.reshape(-1, FAST, width).transpose(1, 0, 2)
-    wanted = pick[: groups * FPG].reshape(groups, FPG)[:, :slots].reshape(-1)
-    dealt = held.reshape(groups * blocks_sent, *held.shape[2:]).at[wanted].get(mode="promise_in_bounds")
-    dealt = dealt.reshape(groups, slots, *held.shape[2:])
-    arrived = lax.all_to_all(dealt, "group", split_axis=0, concat_axis=0, tiled=True)
     return ladder(plan, factors, arrived, amps)
 
 
 def body(factors, amplitudes, factor_route, amp_route, task_list, target_tile):
     groups = lax.axis_size("group")
-    amp_rows, table = group_blocks(amplitudes, factor_route, amp_route, task_list, target_tile)
+    amp_rows, table = group_facts(amplitudes, factor_route, amp_route, task_list, target_tile)
+    cut = cut_blocks(factors, groups)
     me = lax.axis_index("group").astype(jnp.int32).reshape(1)
     send, pick, plan, balanced = assign(me, table)
-    operands = (factors, amp_rows, send, pick, plan)
+    operands = (factors, cut, amp_rows, send, pick, plan)
     parts = lax.cond(
         balanced[0] == 1,
         functools.partial(contributions, FAST, FAST),

time: 200 us -> 192 us (0.960); the launches traced: 197 us -> 192 us
  Pallas kernels: 29.2 us -> 39.8 us
  blocking collectives: 48.9 us -> 39.6 us
  other arithmetic: 12.3 us -> 3.68 us
  starting transfers between devices: 43.6 us -> 46.9 us
    all_to_all x2, waiting for transfers between devices: 48.9 us -> 24 us  [the longest x1 20.5 us: contributions(): lax.all_to_all(leaving, 'group', split_axis=0, concat_axis=0, tiled=True)]
    all_to_all x1, waiting for transfers between devices: 0.01 us -> 11.9 us  [contributions(): lax.all_to_all(dealt, 'group', split_axis=0, concat_axis=0, tiled=True)]
    ppermute x5, waiting for transfers between devices: 4.32 us -> 15.8 us  [spread(): other = lax.ppermute(held, axis, [(i, i ^ bit) for i in range(members)])]
    all_to_all x1, blocking collectives: 22.2 us -> 15.8 us  [body(): lax.all_to_all(returns, 'group', split_axis=0, concat_axis=0, tiled=True)]
    select_n x7 -> x5, other arithmetic: 5.54 us -> 0.06 us  [spread(): jnp.where(mine_first, jnp.concatenate([held, other]), jnp.concatenate([ot...]
    gather x1 -> x2, local copies, waits for them, and re-layouts: 1.93 us -> 7.14 us  [the longest x1 3.83 us: contributions(): cut.reshape(groups * count, *piece).at[order.reshape(-1)]]
    concatenate x5 -> x2, local copies, waits for them, and re-layouts: 4.87 us -> 0.08 us  [spread(): jnp.concatenate([held, other])]
    pallas_call x1 -> x2, Pallas kernels: 4.27 us -> 8.25 us  [the longest x1 6.52 us: cut_blocks(): pl.pallas_call(cut_kernel, grid=(count,), in_specs=[pl.BlockSpec((1, rows...]
  transfers between devices with their start and end apart: 8 -> 8, of which waited for: 5 -> 8; matrix products, arithmetic and copies ran while one was open for 8% -> 2% of each run, Pallas kernels for 0% -> 3%
where the time goes in v5:
time: 192 us
  waiting for transfers between devices  51.8 us (27%)
  starting transfers between devices  46.9 us (24%)
  Pallas kernels  39.8 us (21%)
  blocking collectives  39.6 us (21%)
  local copies, waits for them, and re-layouts  9.37 us (5%)
  other arithmetic  3.68 us (2%)
    ppermute x5, starting transfers between devices, spread(): other = lax.ppermute(held, axis, [(i, i ^ bit) for i in range(members)])  25.7 us
    all_to_all x1, blocking collectives, body(): lax.all_to_all(parts, 'shard', split_axis=0, concat_axis=0, tiled=True)  23.8 us
    all_to_all x1, waiting for transfers between devices, contributions(): lax.all_to_all(leaving, 'group', split_axis=0, concat_axis=0, tiled=True)  20.5 us
    pallas_call x1, Pallas kernels, ladder(): pl.pallas_call(ladder_kernel, grid_spec=pltpu.PrefetchScalarGridSpec(num_...  20 us
    all_to_all x1, blocking collectives, body(): lax.all_to_all(returns, 'group', split_axis=0, concat_axis=0, tiled=True)  15.8 us
    ppermute x5, waiting for transfers between devices, spread(): other = lax.ppermute(held, axis, [(i, i ^ bit) for i in range(members)])  15.8 us
    all_to_all x1, waiting for transfers between devices, contributions(): lax.all_to_all(dealt, 'group', split_axis=0, concat_axis=0, tiled=True)  11.9 us
    all_to_all x1, starting transfers between devices, group_facts(): lax.all_to_all(facts, 'group', split_axis=0, concat_axis=0, tiled=True)  10 us
  transfers between devices with their start and end apart: 8, of which 8 were waited for; matrix products, arithmetic and copies ran while one was open for 2% of the time, Pallas kernels for 3%

profile of v5, /device:TPU:8, one launch (start us, length us, event | category | flops | bytes accessed | tf_op | source)
XLA Modules:
  0.0 192.0 jit_solution(4588727744256005522)
XLA Ops:
  0.0 1.3 copy.30.task_list
  1.3 1.7 facts.1
  3.0 10.0 %all-to-all-start.4 = ((bf16[16,5,8,128]{3,2,1,0:T(8,128)(2,1)}), bf16[16,5,8,128]{3,2,1,0:T(8,128)(2,1)S(1)}, u32[]{:S(2)}, u32[]{:S(2)}) async-start(bf16[16,5,8,128]{3,2,1,0:T(8,128)(2,1)} %facts.1), calls=%async_computation.4 | async-start | bytes 327680 | tf_op jit(solution)/shard_map/all_to_all | solution.py:426
  13.0 0.0 copy-start
  13.0 6.5 %cut_blocks.1 = bf16[16,8,96,128]{3,2,1,0:T(8,128)(2,1)} custom-call(bf16[8,192,1024]{2,1,0:T(8,128)(2,1)} %block.1), custom_call_target="tpu_custom_call" | custom-call | bytes 6291456 | tf_op jit(solution)/shard_map/cut_blocks/pallas_call | solution.py:371
  19.5 3.6 %all-to-all-done.4 = bf16[16,5,8,128]{3,2,1,0:T(8,128)(2,1)S(1)} async-done(((bf16[16,5,8,128]{3,2,1,0:T(8,128)(2,1)}), bf16[16,5,8,128]{3,2,1,0:T(8,128)(2,1)S(1)}, u32[]{:S(2)}, u32[]{:S(2)}) %all-to-all-start.4) | async-done | bytes 163872 | tf_op jit(solution)/shard_map/all_to_all | solution.py:426
  23.1 0.6 fusion.22.table
  23.7 8.2 %assign.1 = (s32[16]{0:T(128)S(1)}, s32[136]{0:T(256)S(1)}, s32[8,4]{1,0:T(8,128)S(1)}, s32[1]{0:T(128)}) custom-call(s32[1]{0:T(128)} %bitcast.20.me, s32[16,128]{1,0:T(8,128)} %fusion.22.table), custom_call_target="tpu_custom_call" | custom-call | tf_op jit(solution)/shard_map/assign/pallas_call | solution.py:345
  32.6 0.0 copy-done
  32.6 116.5 %conditional.1 = (bf16[32,4,8,128]{3,2,1,0:T(8,128)(2,1)S(1)}) conditional(s32[]{:T(128)} %bitcast.23, (bf16[16,8,96,128]{3,2,1,0:T(8,128)(2,1)}, s32[16]{0:T(128)S(1)}, s32[8,4]{1,0:T(8,128)S(1)}, bf16[80,8,128]{2,1,0:T(8,128)(2,1)S(1)}, s32[136]{0:T(256)S(1)}, /*index=5*/bf16[8,192,1024]{2,1,0:T(8,128)(2,1)S(1)}) %tuple.20, ...), branch_computations={%region_0.1_spmd, %region_1.2_spmd} | conditional | flops 6348616 | bytes 32756072 | solution.py:457
  32.6 0.1 broadcast_add_fusion.1
  32.7 0.1 add.151
  32.8 3.8 %gather_fusion.3 = bf16[64,96,128]{2,1,0:T(8,128)(2,1)} fusion(bf16[128,96,128]{2,1,0:T(8,128)(2,1)} %bitcast.53, s32[1024]{0:T(1024)S(1)} %pad_clamp_fusion.5), kind=kCustom, calls=%fused_computation.3 | custom fusion | bytes 3145984 | tf_op jit(solution)/shard_map/cond/branch_1_fun/gather | solution.py:435
  36.6 6.1 %all-to-all-start.2 = ((bf16[16,4,96,128]{3,2,1,0:T(8,128)(2,1)}), bf16[16,4,96,128]{3,2,1,0:T(8,128)(2,1)}, u32[]{:S(2)}, u32[]{:S(2)}) async-start(bf16[16,4,96,128]{3,2,1,0:T(8,128)(2,1)} %bitcast.56), calls=%async_computation.2 | async-start | bytes 3145728 | tf_op jit(solution)/shard_map/cond/branch_1_fun/all_to_all | solution.py:437
  42.7 0.2 fusion.19
  42.9 0.6 gather_fusion.4
  43.5 1.9 %collective-permute-start.5 = (bf16[1,4,8,128]{3,2,1,0:T(8,128)(2,1)S(1)}, bf16[1,4,8,128]{3,2,1,0:T(8,128)(2,1)S(1)}, u32[]{:S(2)}, u32[]{:S(2)}) collective-permute-start(bf16[1,4,8,128]{3,2,1,0:T(8,128)(2,1)S(1)} %bitcast.69), channel_id=1, source_target_pairs={{0,1},{1,0},{2,3},{3,2},{4,5},{5,4},{6,7},{7,6},{8,9},{9,8},{10,11... | collective-permute-start | bytes 24584 | tf_op jit(solution)/shard_map/cond/branch_1_fun/ppermute | solution.py:387
  45.4 0.1 reshape.417
  45.5 0.1 reshape.418
  45.6 0.9 collective-permute-done.5
  46.6 4.3 %collective-permute-start.6 = (bf16[2,4,8,128]{3,2,1,0:T(8,128)(2,1)S(1)}, bf16[2,4,8,128]{3,2,1,0:T(8,128)(2,1)S(1)}, u32[]{:S(2)}, u32[]{:S(2)}) collective-permute-start(bf16[2,4,8,128]{3,2,1,0:T(8,128)(2,1)S(1)} %maximum_select_fusion.11), channel_id=1, source_target_pairs={{0,2},{1,3},{2,0},{3,1},{4,6},{5,7},{6,4},{7,5},{8,10},{9,11},{10,... | collective-permute-start | bytes 49160 | tf_op jit(solution)/shard_map/cond/branch_1_fun/ppermute | solution.py:387
  50.9 1.7 collective-permute-done.6
  52.5 6.1 %collective-permute-start.7 = (bf16[4,4,8,128]{3,2,1,0:T(8,128)(2,1)S(1)}, bf16[4,4,8,128]{3,2,1,0:T(8,128)(2,1)S(1)}, u32[]{:S(2)}, u32[]{:S(2)}) collective-permute-start(bf16[4,4,8,128]{3,2,1,0:T(8,128)(2,1)S(1)} %maximum_select_fusion.10), channel_id=1, source_target_pairs={{0,4},{1,5},{2,6},{3,7},{4,0},{5,1},{6,2},{7,3},{8,12},{9,13},{10,... | collective-permute-start | bytes 98312 | tf_op jit(solution)/shard_map/cond/branch_1_fun/ppermute | solution.py:387
  58.7 2.2 %collective-permute-done.7 = bf16[4,4,8,128]{3,2,1,0:T(8,128)(2,1)S(1)} collective-permute-done((bf16[4,4,8,128]{3,2,1,0:T(8,128)(2,1)S(1)}, bf16[4,4,8,128]{3,2,1,0:T(8,128)(2,1)S(1)}, u32[]{:S(2)}, u32[]{:S(2)}) %collective-permute-start.7) | collective-permute-done | bytes 32800 | tf_op jit(solution)/shard_map/cond/branch_1_fun/ppermute | solution.py:387
  60.9 20.5 %all-to-all-done.2 = bf16[16,4,96,128]{3,2,1,0:T(8,128)(2,1)} async-done(((bf16[16,4,96,128]{3,2,1,0:T(8,128)(2,1)}), bf16[16,4,96,128]{3,2,1,0:T(8,128)(2,1)}, u32[]{:S(2)}, u32[]{:S(2)}) %all-to-all-start.2) | async-done | bytes 1572896 | tf_op jit(solution)/shard_map/cond/branch_1_fun/all_to_all | solution.py:437
  81.4 3.3 %gather_fusion.5 = bf16[64,96,128]{2,1,0:T(8,128)(2,1)} fusion(bf16[64,96,128]{2,1,0:T(8,128)(2,1)} %bitcast.14, s32[1024]{0:T(1024)S(1)} %pad_clamp_fusion.3), kind=kCustom, calls=%fused_computation.5 | custom fusion | bytes 3145984 | tf_op jit(solution)/shard_map/cond/branch_1_fun/gather | solution.py:442
  84.7 5.1 %all-to-all-start.3 = ((bf16[16,4,96,128]{3,2,1,0:T(8,128)(2,1)}), bf16[16,4,96,128]{3,2,1,0:T(8,128)(2,1)}, u32[]{:S(2)}, u32[]{:S(2)}) async-start(bf16[16,4,96,128]{3,2,1,0:T(8,128)(2,1)} %bitcast.57), calls=%async_computation.3 | async-start | bytes 3145728 | tf_op jit(solution)/shard_map/cond/branch_1_fun/all_to_all | solution.py:444
  89.8 10.9 %collective-permute-start.8 = (bf16[8,4,8,128]{3,2,1,0:T(8,128)(2,1)S(1)}, bf16[8,4,8,128]{3,2,1,0:T(8,128)(2,1)S(1)}, u32[]{:S(2)}, u32[]{:S(2)}) collective-permute-start(bf16[8,4,8,128]{3,2,1,0:T(8,128)(2,1)S(1)} %maximum_select_fusion.9), channel_id=1, source_target_pairs={{0,8},{1,9},{2,10},{3,11},{4,12},{5,13},{6,14},{7,15},{8,0},{9,1},... | collective-permute-start | bytes 196616 | tf_op jit(solution)/shard_map/cond/branch_1_fun/ppermute | solution.py:387
  100.7 2.6 %collective-permute-done.8 = bf16[8,4,8,128]{3,2,1,0:T(8,128)(2,1)S(1)} collective-permute-done((bf16[8,4,8,128]{3,2,1,0:T(8,128)(2,1)S(1)}, bf16[8,4,8,128]{3,2,1,0:T(8,128)(2,1)S(1)}, u32[]{:S(2)}, u32[]{:S(2)}) %collective-permute-start.8) | collective-permute-done | bytes 65568 | tf_op jit(solution)/shard_map/cond/branch_1_fun/ppermute | solution.py:387
  103.3 2.5 %collective-permute-start.9 = (bf16[16,4,8,128]{3,2,1,0:T(8,128)(2,1)S(1)}, bf16[16,4,8,128]{3,2,1,0:T(8,128)(2,1)S(1)}, u32[]{:S(2)}, u32[]{:S(2)}) collective-permute-start(bf16[16,4,8,128]{3,2,1,0:T(8,128)(2,1)S(1)} %maximum_select_fusion.8), channel_id=1, source_target_pairs={{0,16},{1,17},{2,18},{3,19},{4,20},{5,21},{6,22},{7,23},{8,24},{9,... | collective-permute-start | bytes 393224 | tf_op jit(solution)/shard_map/cond/branch_1_fun/ppermute | solution.py:387
  105.8 2.0 %and_convert_fusion.1.swap = bf16[1024,1024]{1,0:T(8,128)(2,1)} fusion(s32[1024]{0:T(1024)S(1)} %get-tuple-element.59, s32[1024]{0:T(1024)S(1)} %get-tuple-element.58), kind=kLoop, calls=%fused_computation.38 | loop fusion | flops 4194304 | bytes 2105344 | tf_op jit(solution)/shard_map/cond/branch_1_fun/convert_element_type | solution.py:115
  107.9 8.4 %collective-permute-done.9 = bf16[16,4,8,128]{3,2,1,0:T(8,128)(2,1)S(1)} collective-permute-done((bf16[16,4,8,128]{3,2,1,0:T(8,128)(2,1)S(1)}, bf16[16,4,8,128]{3,2,1,0:T(8,128)(2,1)S(1)}, u32[]{:S(2)}, u32[]{:S(2)}) %collective-permute-start.9) | collective-permute-done | bytes 131104 | tf_op jit(solution)/shard_map/cond/branch_1_fun/ppermute | solution.py:387
  116.4 0.8 fusion.11.amp
  117.1 11.9 %all-to-all-done.3.left_cut.right_cut = bf16[16,4,96,128]{3,2,1,0:T(8,128)(2,1)} async-done(((bf16[16,4,96,128]{3,2,1,0:T(8,128)(2,1)}), bf16[16,4,96,128]{3,2,1,0:T(8,128)(2,1)}, u32[]{:S(2)}, u32[]{:S(2)}) %all-to-all-start.3) | async-done | bytes 1572896 | tf_op jit(solution)/shard_map/cond/branch_1_fun/all_to_all | solution.py:444
  129.1 20.0 %ladder.3 = bf16[32,4,8,128]{3,2,1,0:T(8,128)(2,1)S(1)} custom-call(s32[8,4]{1,0:T(8,128)S(1)} %get-tuple-element.40.plan, bf16[8,192,1024]{2,1,0:T(8,128)(2,1)S(1)} %get-tuple-element.41.left_whole.right_whole, bf16[16,4,96,128]{3,2,1,0:T(8,128)(2,1)} %all-to-all-done.3.left_cut.right_cut, ...), custom_call_target="tpu_custom_call" | custom-call | tf_op jit(solution)/shard_map/cond/branch_1_fun/ladder/pallas_call | solution.py:131
  149.1 23.8 %all_to_all.31.pieces = bf16[32,4,8,128]{3,2,1,0:T(8,128)(2,1)} all-to-all(bf16[32,4,8,128]{3,2,1,0:T(8,128)(2,1)S(1)} %get-tuple-element.60), channel_id=1, replica_groups=mesh['group'=16,'shard'=32] {'shard'}, dimensions={0} | all-to-all | bytes 524288 | tf_op jit(solution)/shard_map/all_to_all | solution.py:463
  172.9 1.7 combine.1
  174.6 15.8 %all_to_all.32 = f32[32,8,128]{2,1,0:T(8,128)} all-to-all(f32[32,8,128]{2,1,0:T(8,128)} %combine.1), channel_id=1, replica_groups=mesh['group'=16,'shard'=32] {'group'}, dimensions={0} | all-to-all | bytes 262144 | tf_op jit(solution)/shard_map/all_to_all | solution.py:465
  190.4 1.6 owned.1
  (18 shorter events, 0.2 us)
Async XLA Ops:
  3.0 20.1 %all-to-all-start.4 = ((bf16[16,5,8,128]{3,2,1,0:T(8,128)(2,1)}), bf16[16,5,8,128]{3,2,1,0:T(8,128)(2,1)S(1)}, u32[]{:S(2)}, u32[]{:S(2)}) async-start(bf16[16,5,8,128]{3,2,1,0:T(8,128)(2,1)} %facts.1), calls=%async_computation.4 | async-start | bytes 327680 | tf_op jit(solution)/shard_map/all_to_all | solution.py:426
  13.0 19.6 %copy-start = (bf16[8,192,1024]{2,1,0:T(8,128)(2,1)S(1)}, bf16[8,192,1024]{2,1,0:T(8,128)(2,1)}, u32[]{:S(2)}) copy-start(bf16[8,192,1024]{2,1,0:T(8,128)(2,1)} %block.1) | copy-start | bytes 9437188
  36.6 44.7 %all-to-all-start.2 = ((bf16[16,4,96,128]{3,2,1,0:T(8,128)(2,1)}), bf16[16,4,96,128]{3,2,1,0:T(8,128)(2,1)}, u32[]{:S(2)}, u32[]{:S(2)}) async-start(bf16[16,4,96,128]{3,2,1,0:T(8,128)(2,1)} %bitcast.56), calls=%async_computation.2 | async-start | bytes 3145728 | tf_op jit(solution)/shard_map/cond/branch_1_fun/all_to_all | solution.py:437
  43.5 3.1 %collective-permute-start.5 = (bf16[1,4,8,128]{3,2,1,0:T(8,128)(2,1)S(1)}, bf16[1,4,8,128]{3,2,1,0:T(8,128)(2,1)S(1)}, u32[]{:S(2)}, u32[]{:S(2)}) collective-permute-start(bf16[1,4,8,128]{3,2,1,0:T(8,128)(2,1)S(1)} %bitcast.69), channel_id=1, source_target_pairs={{0,1},{1,0},{2,3},{3,2},{4,5},{5,4},{6,7},{7,6},{8,9},{9,8},{10,11... | collective-permute-start | bytes 24584 | tf_op jit(solution)/shard_map/cond/branch_1_fun/ppermute | solution.py:387
  46.6 6.0 %collective-permute-start.6 = (bf16[2,4,8,128]{3,2,1,0:T(8,128)(2,1)S(1)}, bf16[2,4,8,128]{3,2,1,0:T(8,128)(2,1)S(1)}, u32[]{:S(2)}, u32[]{:S(2)}) collective-permute-start(bf16[2,4,8,128]{3,2,1,0:T(8,128)(2,1)S(1)} %maximum_select_fusion.11), channel_id=1, source_target_pairs={{0,2},{1,3},{2,0},{3,1},{4,6},{5,7},{6,4},{7,5},{8,10},{9,11},{10,... | collective-permute-start | bytes 49160 | tf_op jit(solution)/shard_map/cond/branch_1_fun/ppermute | solution.py:387
  52.5 8.3 %collective-permute-start.7 = (bf16[4,4,8,128]{3,2,1,0:T(8,128)(2,1)S(1)}, bf16[4,4,8,128]{3,2,1,0:T(8,128)(2,1)S(1)}, u32[]{:S(2)}, u32[]{:S(2)}) collective-permute-start(bf16[4,4,8,128]{3,2,1,0:T(8,128)(2,1)S(1)} %maximum_select_fusion.10), channel_id=1, source_target_pairs={{0,4},{1,5},{2,6},{3,7},{4,0},{5,1},{6,2},{7,3},{8,12},{9,13},{10,... | collective-permute-start | bytes 98312 | tf_op jit(solution)/shard_map/cond/branch_1_fun/ppermute | solution.py:387
  84.7 44.4 %all-to-all-start.3 = ((bf16[16,4,96,128]{3,2,1,0:T(8,128)(2,1)}), bf16[16,4,96,128]{3,2,1,0:T(8,128)(2,1)}, u32[]{:S(2)}, u32[]{:S(2)}) async-start(bf16[16,4,96,128]{3,2,1,0:T(8,128)(2,1)} %bitcast.57), calls=%async_computation.3 | async-start | bytes 3145728 | tf_op jit(solution)/shard_map/cond/branch_1_fun/all_to_all | solution.py:444
  89.8 13.5 %collective-permute-start.8 = (bf16[8,4,8,128]{3,2,1,0:T(8,128)(2,1)S(1)}, bf16[8,4,8,128]{3,2,1,0:T(8,128)(2,1)S(1)}, u32[]{:S(2)}, u32[]{:S(2)}) collective-permute-start(bf16[8,4,8,128]{3,2,1,0:T(8,128)(2,1)S(1)} %maximum_select_fusion.9), channel_id=1, source_target_pairs={{0,8},{1,9},{2,10},{3,11},{4,12},{5,13},{6,14},{7,15},{8,0},{9,1},... | collective-permute-start | bytes 196616 | tf_op jit(solution)/shard_map/cond/branch_1_fun/ppermute | solution.py:387
  103.3 13.0 %collective-permute-start.9 = (bf16[16,4,8,128]{3,2,1,0:T(8,128)(2,1)S(1)}, bf16[16,4,8,128]{3,2,1,0:T(8,128)(2,1)S(1)}, u32[]{:S(2)}, u32[]{:S(2)}) collective-permute-start(bf16[16,4,8,128]{3,2,1,0:T(8,128)(2,1)S(1)} %maximum_select_fusion.8), channel_id=1, source_target_pairs={{0,16},{1,17},{2,18},{3,19},{4,20},{5,21},{6,22},{7,23},{8,24},{9,... | collective-permute-start | bytes 393224 | tf_op jit(solution)/shard_map/cond/branch_1_fun/ppermute | solution.py:387

commit v6 on v5

--- a/solution.py
+++ b/solution.py
@@ -357,27 +357,70 @@
     )(me, table)
 
 
-def cut_kernel(block, out):
-    rows = out.shape[2]
-    for piece in range(out.shape[0]):
-        half, part = divmod(piece, block.shape[2] // LANES)
-        out[piece, 0] = block[0, half * rows : (half + 1) * rows, part * LANES : (part + 1) * LANES]
-
-
-def cut_blocks(factors, pieces):
-    count, rows, width = factors.shape
+def leave_kernel(send, factors, out, held, arrive, leave):
+    pieces, count, rows, _ = out.shape
+    width = factors.shape[2]
+    blocks = [pltpu.make_async_copy(factors.at[send[i]], held.at[i], arrive.at[i]) for i in range(count)]
+    parts = []
+    for block in blocks:
+        block.start()
+    for i, block in enumerate(blocks):
+        block.wait()
+        for piece in range(pieces):
+            half, part = divmod(piece, width // LANES)
+            piece_of = held.at[i, half * rows : (half + 1) * rows, part * LANES : (part + 1) * LANES]
+            parts.append(pltpu.make_async_copy(piece_of, out.at[piece, i], leave.at[i * pieces + piece]))
+            parts[-1].start()
+    for part in parts:
+        part.wait()
+
+
+def leaving_pieces(send, factors, count, pieces):
+    _, rows, width = factors.shape
     piece_rows = rows * width // LANES // pieces
-    size = factors.size * 2
     return pl.pallas_call(
-        cut_kernel,
-        grid=(count,),
-        in_specs=[pl.BlockSpec((1, rows, width), lambda i: (i, 0, 0))],
-        out_specs=pl.BlockSpec((pieces, 1, piece_rows, LANES), lambda i: (0, i, 0, 0)),
+        leave_kernel,
+        in_specs=[pl.BlockSpec(memory_space=pltpu.SMEM), pl.BlockSpec(memory_space=pl.ANY)],
+        out_specs=pl.BlockSpec(memory_space=pl.ANY),
         out_shape=jax.ShapeDtypeStruct((pieces, count, piece_rows, LANES), factors.dtype),
-        compiler_params=pltpu.CompilerParams(dimension_semantics=("arbitrary",)),
-        cost_estimate=pl.CostEstimate(flops=0, bytes_accessed=2 * size, transcendentals=0),
-        name="cut_blocks",
-    )(factors)
+        scratch_shapes=[
+            pltpu.VMEM((count, rows, width), factors.dtype),
+            pltpu.SemaphoreType.DMA((count,)),
+            pltpu.SemaphoreType.DMA((count * pieces,)),
+        ],
+        name="leaving_pieces",
+    )(send, factors)
+
+
+def deal_kernel(pick, pieces, out, held, arrive, leave):
+    groups, slots = out.shape[:2]
+    whole = pltpu.make_async_copy(pieces, held, arrive)
+    whole.start()
+    whole.wait()
+    parts = []
+    for g in range(groups):
+        for j in range(slots):
+            source = held.at[pick[g * FPG + j]]
+            parts.append(pltpu.make_async_copy(source, out.at[g, j], leave.at[g * slots + j]))
+            parts[-1].start()
+    for part in parts:
+        part.wait()
+
+
+def dealt_pieces(pick, pieces, groups, slots):
+    count, rows, lanes = pieces.shape
+    return pl.pallas_call(
+        deal_kernel,
+        in_specs=[pl.BlockSpec(memory_space=pltpu.SMEM), pl.BlockSpec(memory_space=pl.ANY)],
+        out_specs=pl.BlockSpec(memory_space=pl.ANY),
+        out_shape=jax.ShapeDtypeStruct((groups, slots, rows, lanes), pieces.dtype),
+        scratch_shapes=[
+            pltpu.VMEM(pieces.shape, pieces.dtype),
+            pltpu.SemaphoreType.DMA,
+            pltpu.SemaphoreType.DMA((groups * slots,)),
+        ],
+        name="dealt_pieces",
+    )(pick, pieces)
 
 
 def spread(held, axis, bits):
@@ -396,7 +439,7 @@
     tiles, occupied, width = amplitudes.shape
     chosen = lax.broadcasted_iota(jnp.int32, (occupied, width), 0) == shard[0]
     facts = [amp_route[...], factor_route[...], target_tile[...]]
-    facts += [task_list[0, k : k + 1, :] for k in range(TASKS)]
+    facts += [task_list[k] for k in range(TASKS)]
     facts = jnp.concatenate(facts, axis=1).astype(jnp.float32)
     facts = jnp.concatenate([facts, jnp.zeros((1, LANES - facts.shape[1]), jnp.float32)], axis=1)
     parts = width // LANES
@@ -422,25 +465,20 @@
         out_specs=vmem,
         out_shape=jax.ShapeDtypeStruct((groups, tiles + 1, width // LANES, LANES), amplitudes.dtype),
         name="facts",
-    )(shard, amplitudes, amp_route, factor_route, target_tile, task_list)
+    )(shard, amplitudes, amp_route, factor_route, target_tile, task_list.transpose(1, 0, 2))
     held = lax.all_to_all(facts, "group", split_axis=0, concat_axis=0, tiled=True)
     return held.reshape(groups * (tiles + 1), *held.shape[2:]), held[:, tiles, 0].astype(jnp.int32)
 
 
-def contributions(blocks_sent, slots, factors, cut, amp_rows, send, pick, plan):
-    groups, count = cut.shape[:2]
+def contributions(blocks_sent, slots, factors, amp_rows, send, pick, plan):
+    groups = lax.axis_size("group")
     width = factors.shape[2]
-    piece = cut.shape[2:]
-    order = jnp.arange(groups, dtype=jnp.int32)[:, None] * count + send[None, :blocks_sent]
-    leaving = cut.reshape(groups * count, *piece).at[order.reshape(-1)].get(mode="promise_in_bounds")
-    leaving = leaving.reshape(groups, blocks_sent, *piece)
+    leaving = leaving_pieces(send, factors, blocks_sent, groups)
     held = lax.all_to_all(leaving, "group", split_axis=0, concat_axis=0, tiled=True)
     chosen = amp_rows.at[plan[:FAST, 2]].get(mode="promise_in_bounds")
     amps = spread(chosen[None], "shard", (1, 2, 4))
     held, amps = lax.optimization_barrier((held, amps))
-    wanted = pick[: groups * FPG].reshape(groups, FPG)[:, :slots].reshape(-1)
-    dealt = held.reshape(groups * blocks_sent, *piece).at[wanted].get(mode="promise_in_bounds")
-    dealt = dealt.reshape(groups, slots, *piece)
+    dealt = dealt_pieces(pick, held.reshape(groups * blocks_sent, *held.shape[2:]), groups, slots)
     arrived = lax.all_to_all(dealt, "group", split_axis=0, concat_axis=0, tiled=True)
     amps = spread(amps, "shard", (8, 16))
     amps = amps.reshape(-1, FAST, width).transpose(1, 0, 2)
@@ -450,10 +488,9 @@
 def body(factors, amplitudes, factor_route, amp_route, task_list, target_tile):
     groups = lax.axis_size("group")
     amp_rows, table = group_facts(amplitudes, factor_route, amp_route, task_list, target_tile)
-    cut = cut_blocks(factors, groups)
     me = lax.axis_index("group").astype(jnp.int32).reshape(1)
     send, pick, plan, balanced = assign(me, table)
-    operands = (factors, cut, amp_rows, send, pick, plan)
+    operands = (factors, amp_rows, send, pick, plan)
     parts = lax.cond(
         balanced[0] == 1,
         functools.partial(contributions, FAST, FAST),

time: 192 us -> 187 us (0.974)
  Pallas kernels: 39.8 us -> 30.6 us
  blocking collectives: 39.6 us -> 47.3 us
  local copies, waits for them, and re-layouts: 9.37 us -> 1.86 us
  waiting for transfers between devices: 51.8 us -> 58 us
    pallas_call x1, Pallas kernels: 20 us -> 12.2 us  [ladder(): pl.pallas_call(ladder_kernel, grid_spec=pltpu.PrefetchScalarGridSpec(num_...]
    all_to_all x1, blocking collectives: 15.8 us -> 23.3 us  [body(): lax.all_to_all(returns, 'group', split_axis=0, concat_axis=0, tiled=True)]
    gather x2 -> x0, local copies, waits for them, and re-layouts: 7.14 us -> none  [the longest x1 3.83 us: contributions(): cut.reshape(groups * count, *piece).at[order.reshape(-1)]]
    all_to_all x1, waiting for transfers between devices: 3.55 us -> 10.1 us  [group_facts(): lax.all_to_all(facts, 'group', split_axis=0, concat_axis=0, tiled=True)]
    all_to_all x1, starting transfers between devices: 6.08 us -> 3.89 us  [contributions(): lax.all_to_all(leaving, 'group', split_axis=0, concat_axis=0, tiled=True)]
    pallas_call x1, Pallas kernels: 8.23 us -> 6.16 us  [assign(): pl.pallas_call(assign_kernel, in_specs=[smem, smem], out_specs=[smem] * 4...]
    pallas_call x1 -> x2, Pallas kernels: 6.52 us -> 7.33 us  [the longest x1 3.69 us: dealt_pieces(): pl.pallas_call(deal_kernel, in_specs=[pl.BlockSpec(memory_space=pltpu.SME...]
  transfers between devices with their start and end apart: 8 -> 8, of which waited for: 8 -> 8; matrix products, arithmetic and copies ran while one was open for 2% -> 2% of each run, Pallas kernels for 3% -> 0%
where the time goes in v6:
time: 187 us; the launch traced here: 188 us
  waiting for transfers between devices  58 us (31%)
  blocking collectives  47.3 us (25%)
  starting transfers between devices  45.2 us (24%)
  Pallas kernels  30.6 us (16%)
  other arithmetic  3.6 us (2%)
    ppermute x5, starting transfers between devices, spread(): other = lax.ppermute(held, axis, [(i, i ^ bit) for i in range(members)])  25.9 us
    all_to_all x1, blocking collectives, body(): lax.all_to_all(parts, 'shard', split_axis=0, concat_axis=0, tiled=True)  24 us
    all_to_all x1, blocking collectives, body(): lax.all_to_all(returns, 'group', split_axis=0, concat_axis=0, tiled=True)  23.3 us
    all_to_all x1, waiting for transfers between devices, contributions(): lax.all_to_all(leaving, 'group', split_axis=0, concat_axis=0, tiled=True)  20.2 us
    ppermute x5, waiting for transfers between devices, spread(): other = lax.ppermute(held, axis, [(i, i ^ bit) for i in range(members)])  15.5 us
    all_to_all x1, waiting for transfers between devices, contributions(): lax.all_to_all(dealt, 'group', split_axis=0, concat_axis=0, tiled=True)  12.2 us
    pallas_call x1, Pallas kernels, ladder(): pl.pallas_call(ladder_kernel, grid_spec=pltpu.PrefetchScalarGridSpec(num_...  12.2 us
    all_to_all x1, waiting for transfers between devices, group_facts(): lax.all_to_all(facts, 'group', split_axis=0, concat_axis=0, tiled=True)  10.1 us
  transfers between devices with their start and end apart: 8, of which 8 were waited for; matrix products, arithmetic and copies ran while one was open for 2% of the time, Pallas kernels for 0%

profile of v6, /device:TPU:8, one launch (start us, length us, event | category | flops | bytes accessed | tf_op | source)
XLA Modules:
  0.0 187.5 jit_solution(10227096324965484421)
XLA Ops:
  0.0 1.7 facts.1
  1.7 10.0 %all-to-all-start.4 = ((bf16[16,5,8,128]{3,2,1,0:T(8,128)(2,1)}), bf16[16,5,8,128]{3,2,1,0:T(8,128)(2,1)S(1)}, u32[]{:S(2)}, u32[]{:S(2)}) async-start(bf16[16,5,8,128]{3,2,1,0:T(8,128)(2,1)} %facts.1), calls=%async_computation.4 | async-start | bytes 327680 | tf_op jit(solution)/shard_map/all_to_all | solution.py:469
  11.8 10.1 %all-to-all-done.4 = bf16[16,5,8,128]{3,2,1,0:T(8,128)(2,1)S(1)} async-done(((bf16[16,5,8,128]{3,2,1,0:T(8,128)(2,1)}), bf16[16,5,8,128]{3,2,1,0:T(8,128)(2,1)S(1)}, u32[]{:S(2)}, u32[]{:S(2)}) %all-to-all-start.4) | async-done | bytes 163872 | tf_op jit(solution)/shard_map/all_to_all | solution.py:469
  21.8 0.6 fusion.18.table
  22.5 6.2 %assign.1 = (s32[16]{0:T(128)S(1)}, s32[136]{0:T(256)S(1)}, s32[8,4]{1,0:T(8,128)S(1)}, s32[1]{0:T(128)}) custom-call(s32[1]{0:T(128)} %bitcast.10.me, s32[16,128]{1,0:T(8,128)} %fusion.18.table), custom_call_target="tpu_custom_call" | custom-call | tf_op jit(solution)/shard_map/assign/pallas_call | solution.py:345
  29.3 107.6 %conditional.1 = (bf16[32,4,8,128]{3,2,1,0:T(8,128)(2,1)S(1)}) conditional(s32[]{:T(128)} %bitcast.14, (s32[16]{0:T(128)S(1)}, bf16[8,192,1024]{2,1,0:T(8,128)(2,1)}, s32[8,4]{1,0:T(8,128)S(1)}, bf16[80,8,128]{2,1,0:T(8,128)(2,1)S(1)}, s32[136]{0:T(256)S(1)}) %tuple.18, (s32[16]{0:T(128)S(1)}, bf16[8,192,1024]{2,1,0:T(8,128)(2,1)}, ...), branch_computations={%region_0.1_spmd, %region_1.2_spmd} | conditional | flops 6345752 | bytes 46895616 | solution.py:494
  29.3 3.6 %leaving_pieces.3 = bf16[16,4,96,128]{3,2,1,0:T(8,128)(2,1)} custom-call(s32[16]{0:T(128)S(1)} %get-tuple-element.38.send, bf16[8,192,1024]{2,1,0:T(8,128)(2,1)} %get-tuple-element.36.factors.left_whole.right_whole), custom_call_target="tpu_custom_call" | custom-call | tf_op jit(solution)/shard_map/cond/branch_1_fun/leaving_pieces/pallas_call | solution.py:381
  33.0 3.9 %all-to-all-start.2 = ((bf16[16,4,96,128]{3,2,1,0:T(8,128)(2,1)}), bf16[16,4,96,128]{3,2,1,0:T(8,128)(2,1)S(1)}, u32[]{:S(2)}, u32[]{:S(2)}) async-start(bf16[16,4,96,128]{3,2,1,0:T(8,128)(2,1)} %leaving_pieces.3), calls=%async_computation.2 | async-start | bytes 3145728 | tf_op jit(solution)/shard_map/cond/branch_1_fun/all_to_all | solution.py:477
  36.9 0.2 fusion.17
  37.1 0.6 gather_fusion.1
  37.6 1.9 %collective-permute-start.5 = (bf16[1,4,8,128]{3,2,1,0:T(8,128)(2,1)S(1)}, bf16[1,4,8,128]{3,2,1,0:T(8,128)(2,1)S(1)}, u32[]{:S(2)}, u32[]{:S(2)}) collective-permute-start(bf16[1,4,8,128]{3,2,1,0:T(8,128)(2,1)S(1)} %bitcast.46), channel_id=1, source_target_pairs={{0,1},{1,0},{2,3},{3,2},{4,5},{5,4},{6,7},{7,6},{8,9},{9,8},{10,11... | collective-permute-start | bytes 24584 | tf_op jit(solution)/shard_map/cond/branch_1_fun/ppermute | solution.py:430
  39.6 1.1 collective-permute-done.5
  40.7 4.3 %collective-permute-start.6 = (bf16[2,4,8,128]{3,2,1,0:T(8,128)(2,1)S(1)}, bf16[2,4,8,128]{3,2,1,0:T(8,128)(2,1)S(1)}, u32[]{:S(2)}, u32[]{:S(2)}) collective-permute-start(bf16[2,4,8,128]{3,2,1,0:T(8,128)(2,1)S(1)} %maximum_select_fusion.11), channel_id=1, source_target_pairs={{0,2},{1,3},{2,0},{3,1},{4,6},{5,7},{6,4},{7,5},{8,10},{9,11},{10,... | collective-permute-start | bytes 49160 | tf_op jit(solution)/shard_map/cond/branch_1_fun/ppermute | solution.py:430
  45.0 1.7 collective-permute-done.6
  46.7 6.1 %collective-permute-start.7 = (bf16[4,4,8,128]{3,2,1,0:T(8,128)(2,1)S(1)}, bf16[4,4,8,128]{3,2,1,0:T(8,128)(2,1)S(1)}, u32[]{:S(2)}, u32[]{:S(2)}) collective-permute-start(bf16[4,4,8,128]{3,2,1,0:T(8,128)(2,1)S(1)} %maximum_select_fusion.10), channel_id=1, source_target_pairs={{0,4},{1,5},{2,6},{3,7},{4,0},{5,1},{6,2},{7,3},{8,12},{9,13},{10,... | collective-permute-start | bytes 98312 | tf_op jit(solution)/shard_map/cond/branch_1_fun/ppermute | solution.py:430
  52.8 2.2 %collective-permute-done.7 = bf16[4,4,8,128]{3,2,1,0:T(8,128)(2,1)S(1)} collective-permute-done((bf16[4,4,8,128]{3,2,1,0:T(8,128)(2,1)S(1)}, bf16[4,4,8,128]{3,2,1,0:T(8,128)(2,1)S(1)}, u32[]{:S(2)}, u32[]{:S(2)}) %collective-permute-start.7) | collective-permute-done | bytes 32800 | tf_op jit(solution)/shard_map/cond/branch_1_fun/ppermute | solution.py:430
  55.0 20.2 %all-to-all-done.2 = bf16[16,4,96,128]{3,2,1,0:T(8,128)(2,1)S(1)} async-done(((bf16[16,4,96,128]{3,2,1,0:T(8,128)(2,1)}), bf16[16,4,96,128]{3,2,1,0:T(8,128)(2,1)S(1)}, u32[]{:S(2)}, u32[]{:S(2)}) %all-to-all-start.2) | async-done | bytes 1572896 | tf_op jit(solution)/shard_map/cond/branch_1_fun/all_to_all | solution.py:477
  75.2 0.0 copy-start.3
  75.2 1.1 copy-done.3
  76.4 3.7 %dealt_pieces.3 = bf16[16,4,96,128]{3,2,1,0:T(8,128)(2,1)} custom-call(s32[136]{0:T(256)S(1)} %get-tuple-element.37.pick, bf16[64,96,128]{2,1,0:T(8,128)(2,1)} %bitcast.36), custom_call_target="tpu_custom_call" | custom-call | tf_op jit(solution)/shard_map/cond/branch_1_fun/dealt_pieces/pallas_call | solution.py:412
  80.1 0.0 copy-start.1
  80.1 5.4 %all-to-all-start.3 = ((bf16[16,4,96,128]{3,2,1,0:T(8,128)(2,1)}), bf16[16,4,96,128]{3,2,1,0:T(8,128)(2,1)}, u32[]{:S(2)}, u32[]{:S(2)}) async-start(bf16[16,4,96,128]{3,2,1,0:T(8,128)(2,1)} %dealt_pieces.3), calls=%async_computation.3 | async-start | bytes 3145728 | tf_op jit(solution)/shard_map/cond/branch_1_fun/all_to_all | solution.py:482
  85.5 10.9 %collective-permute-start.8 = (bf16[8,4,8,128]{3,2,1,0:T(8,128)(2,1)S(1)}, bf16[8,4,8,128]{3,2,1,0:T(8,128)(2,1)S(1)}, u32[]{:S(2)}, u32[]{:S(2)}) collective-permute-start(bf16[8,4,8,128]{3,2,1,0:T(8,128)(2,1)S(1)} %maximum_select_fusion.9), channel_id=1, source_target_pairs={{0,8},{1,9},{2,10},{3,11},{4,12},{5,13},{6,14},{7,15},{8,0},{9,1},... | collective-permute-start | bytes 196616 | tf_op jit(solution)/shard_map/cond/branch_1_fun/ppermute | solution.py:430
  96.4 2.6 %collective-permute-done.8 = bf16[8,4,8,128]{3,2,1,0:T(8,128)(2,1)S(1)} collective-permute-done((bf16[8,4,8,128]{3,2,1,0:T(8,128)(2,1)S(1)}, bf16[8,4,8,128]{3,2,1,0:T(8,128)(2,1)S(1)}, u32[]{:S(2)}, u32[]{:S(2)}) %collective-permute-start.8) | collective-permute-done | bytes 65568 | tf_op jit(solution)/shard_map/cond/branch_1_fun/ppermute | solution.py:430
  99.0 2.7 %collective-permute-start.9 = (bf16[16,4,8,128]{3,2,1,0:T(8,128)(2,1)S(1)}, bf16[16,4,8,128]{3,2,1,0:T(8,128)(2,1)S(1)}, u32[]{:S(2)}, u32[]{:S(2)}) collective-permute-start(bf16[16,4,8,128]{3,2,1,0:T(8,128)(2,1)S(1)} %maximum_select_fusion.8), channel_id=1, source_target_pairs={{0,16},{1,17},{2,18},{3,19},{4,20},{5,21},{6,22},{7,23},{8,24},{9,... | collective-permute-start | bytes 393224 | tf_op jit(solution)/shard_map/cond/branch_1_fun/ppermute | solution.py:430
  101.7 2.0 %and_convert_fusion.1.swap = bf16[1024,1024]{1,0:T(8,128)(2,1)} fusion(s32[1024]{0:T(1024)S(1)} %get-tuple-element.53, s32[1024]{0:T(1024)S(1)} %get-tuple-element.52), kind=kLoop, calls=%fused_computation.26 | loop fusion | flops 4194304 | bytes 2105344 | tf_op jit(solution)/shard_map/cond/branch_1_fun/convert_element_type | solution.py:115
  103.8 7.9 %collective-permute-done.9 = bf16[16,4,8,128]{3,2,1,0:T(8,128)(2,1)S(1)} collective-permute-done((bf16[16,4,8,128]{3,2,1,0:T(8,128)(2,1)S(1)}, bf16[16,4,8,128]{3,2,1,0:T(8,128)(2,1)S(1)}, u32[]{:S(2)}, u32[]{:S(2)}) %collective-permute-start.9) | collective-permute-done | bytes 131104 | tf_op jit(solution)/shard_map/cond/branch_1_fun/ppermute | solution.py:430
  111.8 0.8 fusion.9.amp
  112.6 12.2 %all-to-all-done.3.left_cut.right_cut = bf16[16,4,96,128]{3,2,1,0:T(8,128)(2,1)} async-done(((bf16[16,4,96,128]{3,2,1,0:T(8,128)(2,1)}), bf16[16,4,96,128]{3,2,1,0:T(8,128)(2,1)}, u32[]{:S(2)}, u32[]{:S(2)}) %all-to-all-start.3) | async-done | bytes 1572896 | tf_op jit(solution)/shard_map/cond/branch_1_fun/all_to_all | solution.py:482
  124.8 0.0 copy-done.1
  124.8 12.2 %ladder.3 = bf16[32,4,8,128]{3,2,1,0:T(8,128)(2,1)S(1)} custom-call(s32[8,4]{1,0:T(8,128)S(1)} %get-tuple-element.35.plan, bf16[8,192,1024]{2,1,0:T(8,128)(2,1)S(1)} %copy-done.1, bf16[16,4,96,128]{3,2,1,0:T(8,128)(2,1)} %all-to-all-done.3.left_cut.right_cut, bf16[8,192,1024]{2,1,0:T(8,128)(2,1)S(1)} %copy-done.1, ...), custom_call_target="tpu_custom_call" | custom-call | tf_op jit(solution)/shard_map/cond/branch_1_fun/ladder/pallas_call | solution.py:131
  136.9 24.0 %all_to_all.31.pieces = bf16[32,4,8,128]{3,2,1,0:T(8,128)(2,1)} all-to-all(bf16[32,4,8,128]{3,2,1,0:T(8,128)(2,1)S(1)} %get-tuple-element.54), channel_id=1, replica_groups=mesh['group'=16,'shard'=32] {'shard'}, dimensions={0} | all-to-all | bytes 524288 | tf_op jit(solution)/shard_map/all_to_all | solution.py:500
  160.9 1.7 combine.1
  162.6 23.3 %all_to_all.32 = f32[32,8,128]{2,1,0:T(8,128)} all-to-all(f32[32,8,128]{2,1,0:T(8,128)} %combine.1), channel_id=1, replica_groups=mesh['group'=16,'shard'=32] {'group'}, dimensions={0} | all-to-all | bytes 262144 | tf_op jit(solution)/shard_map/all_to_all | solution.py:502
  185.9 1.6 owned.1
  (12 shorter events, 0.2 us)
Async XLA Ops:
  1.7 20.1 %all-to-all-start.4 = ((bf16[16,5,8,128]{3,2,1,0:T(8,128)(2,1)}), bf16[16,5,8,128]{3,2,1,0:T(8,128)(2,1)S(1)}, u32[]{:S(2)}, u32[]{:S(2)}) async-start(bf16[16,5,8,128]{3,2,1,0:T(8,128)(2,1)} %facts.1), calls=%async_computation.4 | async-start | bytes 327680 | tf_op jit(solution)/shard_map/all_to_all | solution.py:469
  33.0 42.2 %all-to-all-start.2 = ((bf16[16,4,96,128]{3,2,1,0:T(8,128)(2,1)}), bf16[16,4,96,128]{3,2,1,0:T(8,128)(2,1)S(1)}, u32[]{:S(2)}, u32[]{:S(2)}) async-start(bf16[16,4,96,128]{3,2,1,0:T(8,128)(2,1)} %leaving_pieces.3), calls=%async_computation.2 | async-start | bytes 3145728 | tf_op jit(solution)/shard_map/cond/branch_1_fun/all_to_all | solution.py:477
  37.6 3.1 %collective-permute-start.5 = (bf16[1,4,8,128]{3,2,1,0:T(8,128)(2,1)S(1)}, bf16[1,4,8,128]{3,2,1,0:T(8,128)(2,1)S(1)}, u32[]{:S(2)}, u32[]{:S(2)}) collective-permute-start(bf16[1,4,8,128]{3,2,1,0:T(8,128)(2,1)S(1)} %bitcast.46), channel_id=1, source_target_pairs={{0,1},{1,0},{2,3},{3,2},{4,5},{5,4},{6,7},{7,6},{8,9},{9,8},{10,11... | collective-permute-start | bytes 24584 | tf_op jit(solution)/shard_map/cond/branch_1_fun/ppermute | solution.py:430
  40.7 6.0 %collective-permute-start.6 = (bf16[2,4,8,128]{3,2,1,0:T(8,128)(2,1)S(1)}, bf16[2,4,8,128]{3,2,1,0:T(8,128)(2,1)S(1)}, u32[]{:S(2)}, u32[]{:S(2)}) collective-permute-start(bf16[2,4,8,128]{3,2,1,0:T(8,128)(2,1)S(1)} %maximum_select_fusion.11), channel_id=1, source_target_pairs={{0,2},{1,3},{2,0},{3,1},{4,6},{5,7},{6,4},{7,5},{8,10},{9,11},{10,... | collective-permute-start | bytes 49160 | tf_op jit(solution)/shard_map/cond/branch_1_fun/ppermute | solution.py:430
  46.7 8.3 %collective-permute-start.7 = (bf16[4,4,8,128]{3,2,1,0:T(8,128)(2,1)S(1)}, bf16[4,4,8,128]{3,2,1,0:T(8,128)(2,1)S(1)}, u32[]{:S(2)}, u32[]{:S(2)}) collective-permute-start(bf16[4,4,8,128]{3,2,1,0:T(8,128)(2,1)S(1)} %maximum_select_fusion.10), channel_id=1, source_target_pairs={{0,4},{1,5},{2,6},{3,7},{4,0},{5,1},{6,2},{7,3},{8,12},{9,13},{10,... | collective-permute-start | bytes 98312 | tf_op jit(solution)/shard_map/cond/branch_1_fun/ppermute | solution.py:430
  75.2 1.1 copy-start.3
  80.1 44.7 %copy-start.1 = (bf16[8,192,1024]{2,1,0:T(8,128)(2,1)S(1)}, bf16[8,192,1024]{2,1,0:T(8,128)(2,1)}, u32[]{:S(2)}) copy-start(bf16[8,192,1024]{2,1,0:T(8,128)(2,1)} %get-tuple-element.36.factors.left_whole.right_whole) | copy-start | bytes 9437188 | tf_op jit(solution)/shard_map/cond
  80.1 44.7 %all-to-all-start.3 = ((bf16[16,4,96,128]{3,2,1,0:T(8,128)(2,1)}), bf16[16,4,96,128]{3,2,1,0:T(8,128)(2,1)}, u32[]{:S(2)}, u32[]{:S(2)}) async-start(bf16[16,4,96,128]{3,2,1,0:T(8,128)(2,1)} %dealt_pieces.3), calls=%async_computation.3 | async-start | bytes 3145728 | tf_op jit(solution)/shard_map/cond/branch_1_fun/all_to_all | solution.py:482
  85.5 13.5 %collective-permute-start.8 = (bf16[8,4,8,128]{3,2,1,0:T(8,128)(2,1)S(1)}, bf16[8,4,8,128]{3,2,1,0:T(8,128)(2,1)S(1)}, u32[]{:S(2)}, u32[]{:S(2)}) collective-permute-start(bf16[8,4,8,128]{3,2,1,0:T(8,128)(2,1)S(1)} %maximum_select_fusion.9), channel_id=1, source_target_pairs={{0,8},{1,9},{2,10},{3,11},{4,12},{5,13},{6,14},{7,15},{8,0},{9,1},... | collective-permute-start | bytes 196616 | tf_op jit(solution)/shard_map/cond/branch_1_fun/ppermute | solution.py:430
  99.0 12.7 %collective-permute-start.9 = (bf16[16,4,8,128]{3,2,1,0:T(8,128)(2,1)S(1)}, bf16[16,4,8,128]{3,2,1,0:T(8,128)(2,1)S(1)}, u32[]{:S(2)}, u32[]{:S(2)}) collective-permute-start(bf16[16,4,8,128]{3,2,1,0:T(8,128)(2,1)S(1)} %maximum_select_fusion.8), channel_id=1, source_target_pairs={{0,16},{1,17},{2,18},{3,19},{4,20},{5,21},{6,22},{7,23},{8,24},{9,... | collective-permute-start | bytes 393224 | tf_op jit(solution)/shard_map/cond/branch_1_fun/ppermute | solution.py:430

commit v7 on v6

--- a/solution.py
+++ b/solution.py
@@ -19,20 +19,35 @@
 FOLD = LANES // VB
 
 
-def swap_lane_blocks(tiles):
+def swap_lane_blocks(tiles, unit):
     lane = lax.broadcasted_iota(jnp.int32, tiles[0].shape, 1)
-    low = lane.astype(tiles[0].dtype) < 2 * VB
-    even = (lane % (2 * VB)).astype(tiles[0].dtype) < VB
+    low = (lane % (4 * unit)).astype(tiles[0].dtype) < 2 * unit
+    even = (lane % (2 * unit)).astype(tiles[0].dtype) < unit
     x0, x1, x2, x3 = tiles
-    y0 = jnp.where(low, x0, pltpu.roll(x2, 2 * VB, 1))
-    y2 = jnp.where(low, pltpu.roll(x0, 2 * VB, 1), x2)
-    y1 = jnp.where(low, x1, pltpu.roll(x3, 2 * VB, 1))
-    y3 = jnp.where(low, pltpu.roll(x1, 2 * VB, 1), x3)
-    z0 = jnp.where(even, y0, pltpu.roll(y1, VB, 1))
-    z1 = jnp.where(even, pltpu.roll(y0, LANES - VB, 1), y1)
-    z2 = jnp.where(even, y2, pltpu.roll(y3, VB, 1))
-    z3 = jnp.where(even, pltpu.roll(y2, LANES - VB, 1), y3)
+    y0 = jnp.where(low, x0, pltpu.roll(x2, 2 * unit, 1))
+    y2 = jnp.where(low, pltpu.roll(x0, LANES - 2 * unit, 1), x2)
+    y1 = jnp.where(low, x1, pltpu.roll(x3, 2 * unit, 1))
+    y3 = jnp.where(low, pltpu.roll(x1, LANES - 2 * unit, 1), x3)
+    z0 = jnp.where(even, y0, pltpu.roll(y1, unit, 1))
+    z1 = jnp.where(even, pltpu.roll(y0, LANES - unit, 1), y1)
+    z2 = jnp.where(even, y2, pltpu.roll(y3, unit, 1))
+    z3 = jnp.where(even, pltpu.roll(y2, LANES - unit, 1), y3)
     return z0, z1, z2, z3
+
+
+def swap_pairs(source, swap, out):
+    count, width = source.shape
+    span = swap.shape[0]
+    for group in range(width // span):
+        columns = slice(group * span, (group + 1) * span)
+        out[:, columns] = jnp.dot(source[:, columns], swap[...], preferred_element_type=jnp.float32).astype(out.dtype)
+    for chunk in range(count // VB):
+        rows = slice(chunk * VB, (chunk + 1) * VB)
+        for odd in range(2):
+            lanes = [slice((2 * i + odd) * LANES, (2 * i + odd + 1) * LANES) for i in range(FOLD)]
+            tiles = swap_lane_blocks([out[rows, at] for at in lanes], VB // FOLD)
+            for at, tile in zip(lanes, tiles):
+                out[rows, at] = tile
 
 
 def assemble(select, whole, cut, out):
@@ -70,8 +85,8 @@
     occupied = amp.shape[1]
     per_pass = 2 * FOLD
     span = per_pass * VB
-    right_t[...] = jnp.dot(right[...], swap[...], preferred_element_type=jnp.float32).astype(jnp.bfloat16)
-    amp_t[...] = jnp.dot(amp[0], swap[...], preferred_element_type=jnp.float32).astype(jnp.bfloat16)
+    swap_pairs(right, swap, right_t)
+    swap_pairs(amp.at[0], swap, amp_t)
 
     def products(step, _):
         columns = pl.ds(pl.multiple_of(step * 2 * span, 2 * span), 2 * span)
@@ -91,7 +106,7 @@
                 tiles = [
                     integral[pl.ds(pl.multiple_of(step * span + rows + a * VB, VB), VB), lanes] for a in range(FOLD)
                 ]
-                for d, tile in enumerate(swap_lane_blocks(tiles)):
+                for d, tile in enumerate(swap_lane_blocks(tiles, VB)):
                     base = (part * FOLD + d) * VB
                     folded[base : base + VB, half * LANES : (half + 1) * LANES] = tile
         result[:, columns] = jnp.dot(amp_t[...], folded[...], preferred_element_type=jnp.float32)
@@ -102,17 +117,17 @@
     for group in range(width // LANES):
         lanes = slice(group * LANES, (group + 1) * LANES)
         tiles = [result[i * band : (i + 1) * band, lanes] for i in range(FOLD)]
-        for a, tile in enumerate(swap_lane_blocks(tiles)):
+        for a, tile in enumerate(swap_lane_blocks(tiles, VB)):
             out[group * FOLD + a, 0] = tile.astype(out.dtype)
 
 
 def ladder(plan, factors, arrived, amps):
     rows, width = factors.shape[1:]
     tasks, occupied = amps.shape[:2]
-    index = jnp.arange(width, dtype=jnp.int32)
-    swap = (
-        (index[:, None] // VB == index[None, :] % VB) & (index[:, None] % VB == index[None, :] // VB)
-    ).astype(jnp.bfloat16)
+    span = 2 * LANES
+    index = jnp.arange(span, dtype=jnp.int32)
+    p, q = index // VB, index % VB
+    swap = ((q % 8 * VB + q // 8 * 8 + p)[:, None] == index[None, :]).astype(jnp.bfloat16)
     band = occupied // FOLD
     pieces, _, piece_rows, _ = arrived.shape
 
@@ -139,7 +154,7 @@
                 whole(1),
                 cut(1),
                 pl.BlockSpec((1, occupied, width), lambda k, plan: (k, 0, 0)),
-                pl.BlockSpec((width, width), lambda k, plan: (0, 0)),
+                pl.BlockSpec((span, span), lambda k, plan: (0, 0)),
             ],
             out_specs=pl.BlockSpec((VB, 1, band, LANES), lambda k, plan: (0, k, 0, 0)),
             scratch_shapes=[
@@ -357,22 +372,17 @@
     )(me, table)
 
 
-def leave_kernel(send, factors, out, held, arrive, leave):
+def leave_kernel(send, factors, out, held, arrive):
     pieces, count, rows, _ = out.shape
     width = factors.shape[2]
     blocks = [pltpu.make_async_copy(factors.at[send[i]], held.at[i], arrive.at[i]) for i in range(count)]
-    parts = []
     for block in blocks:
         block.start()
     for i, block in enumerate(blocks):
         block.wait()
         for piece in range(pieces):
             half, part = divmod(piece, width // LANES)
-            piece_of = held.at[i, half * rows : (half + 1) * rows, part * LANES : (part + 1) * LANES]
-            parts.append(pltpu.make_async_copy(piece_of, out.at[piece, i], leave.at[i * pieces + piece]))
-            parts[-1].start()
-    for part in parts:
-        part.wait()
+            out[piece, i] = held[i, half * rows : (half + 1) * rows, part * LANES : (part + 1) * LANES]
 
 
 def leaving_pieces(send, factors, count, pieces):
@@ -381,44 +391,31 @@
     return pl.pallas_call(
         leave_kernel,
         in_specs=[pl.BlockSpec(memory_space=pltpu.SMEM), pl.BlockSpec(memory_space=pl.ANY)],
-        out_specs=pl.BlockSpec(memory_space=pl.ANY),
+        out_specs=pl.BlockSpec(memory_space=pltpu.VMEM),
         out_shape=jax.ShapeDtypeStruct((pieces, count, piece_rows, LANES), factors.dtype),
         scratch_shapes=[
             pltpu.VMEM((count, rows, width), factors.dtype),
             pltpu.SemaphoreType.DMA((count,)),
-            pltpu.SemaphoreType.DMA((count * pieces,)),
         ],
+        compiler_params=pltpu.CompilerParams(vmem_limit_bytes=16 << 20),
         name="leaving_pieces",
     )(send, factors)
 
 
-def deal_kernel(pick, pieces, out, held, arrive, leave):
-    groups, slots = out.shape[:2]
-    whole = pltpu.make_async_copy(pieces, held, arrive)
-    whole.start()
-    whole.wait()
-    parts = []
-    for g in range(groups):
-        for j in range(slots):
-            source = held.at[pick[g * FPG + j]]
-            parts.append(pltpu.make_async_copy(source, out.at[g, j], leave.at[g * slots + j]))
-            parts[-1].start()
-    for part in parts:
-        part.wait()
+def deal_kernel(pick, pieces, out):
+    for g in range(out.shape[0]):
+        for j in range(out.shape[1]):
+            out[g, j] = pieces[pick[g * FPG + j]]
 
 
 def dealt_pieces(pick, pieces, groups, slots):
     count, rows, lanes = pieces.shape
     return pl.pallas_call(
         deal_kernel,
-        in_specs=[pl.BlockSpec(memory_space=pltpu.SMEM), pl.BlockSpec(memory_space=pl.ANY)],
-        out_specs=pl.BlockSpec(memory_space=pl.ANY),
+        in_specs=[pl.BlockSpec(memory_space=pltpu.SMEM), pl.BlockSpec(memory_space=pltpu.VMEM)],
+        out_specs=pl.BlockSpec(memory_space=pltpu.VMEM),
         out_shape=jax.ShapeDtypeStruct((groups, slots, rows, lanes), pieces.dtype),
-        scratch_shapes=[
-            pltpu.VMEM(pieces.shape, pieces.dtype),
-            pltpu.SemaphoreType.DMA,
-            pltpu.SemaphoreType.DMA((groups * slots,)),
-        ],
+        compiler_params=pltpu.CompilerParams(vmem_limit_bytes=12 << 20),
         name="dealt_pieces",
     )(pick, pieces)
 

time: 187 us -> 185 us (0.989)
    all_to_all x1, waiting for transfers between devices: 12.2 us -> 9.68 us  [contributions(): lax.all_to_all(dealt, 'group', split_axis=0, concat_axis=0, tiled=True)]
    ppermute x5, waiting for transfers between devices: 15.5 us -> 17.7 us  [spread(): other = lax.ppermute(held, axis, [(i, i ^ bit) for i in range(members)])]
    pallas_call x1, Pallas kernels: 6.16 us -> 8.23 us  [assign(): pl.pallas_call(assign_kernel, in_specs=[smem, smem], out_specs=[smem] * 4...]
    pallas_call x1, Pallas kernels: 3.69 us -> 1.79 us  [dealt_pieces(): pl.pallas_call(deal_kernel, in_specs=[pl.BlockSpec(memory_space=pltpu.SME...]
where the time goes in v7:
time: 185 us
  waiting for transfers between devices  57.7 us (31%)
  blocking collectives  47 us (25%)
  starting transfers between devices  45.4 us (25%)
  Pallas kernels  29 us (16%)
  other arithmetic  3.02 us (2%)
    ppermute x5, starting transfers between devices, spread(): other = lax.ppermute(held, axis, [(i, i ^ bit) for i in range(members)])  25.9 us
    all_to_all x1, blocking collectives, body(): lax.all_to_all(parts, 'shard', split_axis=0, concat_axis=0, tiled=True)  24.1 us
    all_to_all x1, blocking collectives, body(): lax.all_to_all(returns, 'group', split_axis=0, concat_axis=0, tiled=True)  22.9 us
    all_to_all x1, waiting for transfers between devices, contributions(): lax.all_to_all(leaving, 'group', split_axis=0, concat_axis=0, tiled=True)  20.3 us
    ppermute x5, waiting for transfers between devices, spread(): other = lax.ppermute(held, axis, [(i, i ^ bit) for i in range(members)])  17.7 us
    pallas_call x1, Pallas kernels, ladder(): pl.pallas_call(ladder_kernel, grid_spec=pltpu.PrefetchScalarGridSpec(num_...  10.8 us
    all_to_all x1, waiting for transfers between devices, group_facts(): lax.all_to_all(facts, 'group', split_axis=0, concat_axis=0, tiled=True)  10.1 us
    all_to_all x1, starting transfers between devices, group_facts(): lax.all_to_all(facts, 'group', split_axis=0, concat_axis=0, tiled=True)  10 us
  transfers between devices with their start and end apart: 8, of which 8 were waited for; matrix products, arithmetic and copies ran while one was open for 2% of the time, Pallas kernels for 0%

profile of v7, /device:TPU:8, one launch (start us, length us, event | category | flops | bytes accessed | tf_op | source)
XLA Modules:
  0.0 184.5 jit_solution(17757446757041583542)
XLA Ops:
  0.0 1.7 facts.1
  1.7 10.0 %all-to-all-start.4 = ((bf16[16,5,8,128]{3,2,1,0:T(8,128)(2,1)}), bf16[16,5,8,128]{3,2,1,0:T(8,128)(2,1)S(1)}, u32[]{:S(2)}, u32[]{:S(2)}) async-start(bf16[16,5,8,128]{3,2,1,0:T(8,128)(2,1)} %facts.1), calls=%async_computation.4 | async-start | bytes 327680 | tf_op jit(solution)/shard_map/all_to_all | solution.py:466
  11.8 10.1 %all-to-all-done.4 = bf16[16,5,8,128]{3,2,1,0:T(8,128)(2,1)S(1)} async-done(((bf16[16,5,8,128]{3,2,1,0:T(8,128)(2,1)}), bf16[16,5,8,128]{3,2,1,0:T(8,128)(2,1)S(1)}, u32[]{:S(2)}, u32[]{:S(2)}) %all-to-all-start.4) | async-done | bytes 163872 | tf_op jit(solution)/shard_map/all_to_all | solution.py:466
  21.9 0.6 fusion.16.table
  22.5 8.2 %assign.1 = (s32[16]{0:T(128)S(1)}, s32[136]{0:T(256)S(1)}, s32[8,4]{1,0:T(8,128)S(1)}, s32[1]{0:T(128)}) custom-call(s32[1]{0:T(128)} %bitcast.10.me, s32[16,128]{1,0:T(8,128)} %fusion.16.table), custom_call_target="tpu_custom_call" | custom-call | tf_op jit(solution)/shard_map/assign/pallas_call | solution.py:360
  31.3 103.0 %conditional.1 = (bf16[32,4,8,128]{3,2,1,0:T(8,128)(2,1)S(1)}) conditional(s32[]{:T(128)} %bitcast.14, (s32[16]{0:T(128)S(1)}, bf16[8,192,1024]{2,1,0:T(8,128)(2,1)}, s32[8,4]{1,0:T(8,128)S(1)}, bf16[80,8,128]{2,1,0:T(8,128)(2,1)S(1)}, s32[136]{0:T(256)S(1)}) %tuple.16, (s32[16]{0:T(128)S(1)}, bf16[8,192,1024]{2,1,0:T(8,128)(2,1)}, ...), branch_computations={%region_0.1_spmd, %region_1.2_spmd} | conditional | flops 2279192 | bytes 54352412 | solution.py:491
  31.3 3.2 %leaving_pieces.3 = bf16[16,4,96,128]{3,2,1,0:T(8,128)(2,1)} custom-call(s32[16]{0:T(128)S(1)} %get-tuple-element.38.send, bf16[8,192,1024]{2,1,0:T(8,128)(2,1)} %get-tuple-element.36.factors.left_whole.right_whole), custom_call_target="tpu_custom_call" | custom-call | tf_op jit(solution)/shard_map/cond/branch_1_fun/leaving_pieces/pallas_call | solution.py:391
  34.5 4.1 %all-to-all-start.2 = ((bf16[16,4,96,128]{3,2,1,0:T(8,128)(2,1)}), bf16[16,4,96,128]{3,2,1,0:T(8,128)(2,1)S(1)}, u32[]{:S(2)}, u32[]{:S(2)}) async-start(bf16[16,4,96,128]{3,2,1,0:T(8,128)(2,1)} %leaving_pieces.3), calls=%async_computation.2 | async-start | bytes 3145728 | tf_op jit(solution)/shard_map/cond/branch_1_fun/all_to_all | solution.py:474
  38.6 0.2 fusion.10
  38.8 0.6 gather_fusion.1
  39.3 1.9 %collective-permute-start.5 = (bf16[1,4,8,128]{3,2,1,0:T(8,128)(2,1)S(1)}, bf16[1,4,8,128]{3,2,1,0:T(8,128)(2,1)S(1)}, u32[]{:S(2)}, u32[]{:S(2)}) collective-permute-start(bf16[1,4,8,128]{3,2,1,0:T(8,128)(2,1)S(1)} %bitcast.46), channel_id=1, source_target_pairs={{0,1},{1,0},{2,3},{3,2},{4,5},{5,4},{6,7},{7,6},{8,9},{9,8},{10,11... | collective-permute-start | bytes 24584 | tf_op jit(solution)/shard_map/cond/branch_1_fun/ppermute | solution.py:427
  41.3 1.1 collective-permute-done.5
  42.4 4.3 %collective-permute-start.6 = (bf16[2,4,8,128]{3,2,1,0:T(8,128)(2,1)S(1)}, bf16[2,4,8,128]{3,2,1,0:T(8,128)(2,1)S(1)}, u32[]{:S(2)}, u32[]{:S(2)}) collective-permute-start(bf16[2,4,8,128]{3,2,1,0:T(8,128)(2,1)S(1)} %maximum_select_fusion.11), channel_id=1, source_target_pairs={{0,2},{1,3},{2,0},{3,1},{4,6},{5,7},{6,4},{7,5},{8,10},{9,11},{10,... | collective-permute-start | bytes 49160 | tf_op jit(solution)/shard_map/cond/branch_1_fun/ppermute | solution.py:427
  46.7 1.7 collective-permute-done.6
  48.4 6.1 %collective-permute-start.7 = (bf16[4,4,8,128]{3,2,1,0:T(8,128)(2,1)S(1)}, bf16[4,4,8,128]{3,2,1,0:T(8,128)(2,1)S(1)}, u32[]{:S(2)}, u32[]{:S(2)}) collective-permute-start(bf16[4,4,8,128]{3,2,1,0:T(8,128)(2,1)S(1)} %maximum_select_fusion.10), channel_id=1, source_target_pairs={{0,4},{1,5},{2,6},{3,7},{4,0},{5,1},{6,2},{7,3},{8,12},{9,13},{10,... | collective-permute-start | bytes 98312 | tf_op jit(solution)/shard_map/cond/branch_1_fun/ppermute | solution.py:427
  54.5 2.2 %collective-permute-done.7 = bf16[4,4,8,128]{3,2,1,0:T(8,128)(2,1)S(1)} collective-permute-done((bf16[4,4,8,128]{3,2,1,0:T(8,128)(2,1)S(1)}, bf16[4,4,8,128]{3,2,1,0:T(8,128)(2,1)S(1)}, u32[]{:S(2)}, u32[]{:S(2)}) %collective-permute-start.7) | collective-permute-done | bytes 32800 | tf_op jit(solution)/shard_map/cond/branch_1_fun/ppermute | solution.py:427
  56.7 20.3 %all-to-all-done.2 = bf16[16,4,96,128]{3,2,1,0:T(8,128)(2,1)S(1)} async-done(((bf16[16,4,96,128]{3,2,1,0:T(8,128)(2,1)}), bf16[16,4,96,128]{3,2,1,0:T(8,128)(2,1)S(1)}, u32[]{:S(2)}, u32[]{:S(2)}) %all-to-all-start.2) | async-done | bytes 1572896 | tf_op jit(solution)/shard_map/cond/branch_1_fun/all_to_all | solution.py:474
  77.0 1.8 dealt_pieces.3
  78.8 0.0 copy-start.3
  78.8 5.4 %all-to-all-start.3 = ((bf16[16,4,96,128]{3,2,1,0:T(8,128)(2,1)}), bf16[16,4,96,128]{3,2,1,0:T(8,128)(2,1)}, u32[]{:S(2)}, u32[]{:S(2)}) async-start(bf16[16,4,96,128]{3,2,1,0:T(8,128)(2,1)} %dealt_pieces.3), calls=%async_computation.3 | async-start | bytes 3145728 | tf_op jit(solution)/shard_map/cond/branch_1_fun/all_to_all | solution.py:479
  84.2 10.9 %collective-permute-start.8 = (bf16[8,4,8,128]{3,2,1,0:T(8,128)(2,1)S(1)}, bf16[8,4,8,128]{3,2,1,0:T(8,128)(2,1)S(1)}, u32[]{:S(2)}, u32[]{:S(2)}) collective-permute-start(bf16[8,4,8,128]{3,2,1,0:T(8,128)(2,1)S(1)} %maximum_select_fusion.9), channel_id=1, source_target_pairs={{0,8},{1,9},{2,10},{3,11},{4,12},{5,13},{6,14},{7,15},{8,0},{9,1},... | collective-permute-start | bytes 196616 | tf_op jit(solution)/shard_map/cond/branch_1_fun/ppermute | solution.py:427
  95.2 2.5 %collective-permute-done.8 = bf16[8,4,8,128]{3,2,1,0:T(8,128)(2,1)S(1)} collective-permute-done((bf16[8,4,8,128]{3,2,1,0:T(8,128)(2,1)S(1)}, bf16[8,4,8,128]{3,2,1,0:T(8,128)(2,1)S(1)}, u32[]{:S(2)}, u32[]{:S(2)}) %collective-permute-start.8) | collective-permute-done | bytes 65568 | tf_op jit(solution)/shard_map/cond/branch_1_fun/ppermute | solution.py:427
  97.7 0.7 maximum_select_fusion.8
  98.4 2.8 %collective-permute-start.9 = (bf16[16,4,8,128]{3,2,1,0:T(8,128)(2,1)}, bf16[16,4,8,128]{3,2,1,0:T(8,128)(2,1)}, u32[]{:S(2)}, u32[]{:S(2)}) collective-permute-start(bf16[16,4,8,128]{3,2,1,0:T(8,128)(2,1)} %maximum_select_fusion.8), channel_id=1, source_target_pairs={{0,16},{1,17},{2,18},{3,19},{4,20},{5,21},{6,22},{7,23},{8,24},{9,... | collective-permute-start | bytes 393224 | tf_op jit(solution)/shard_map/cond/branch_1_fun/ppermute | solution.py:427
  101.1 0.8 fusion.9.swap
  102.0 10.1 %collective-permute-done.9 = bf16[16,4,8,128]{3,2,1,0:T(8,128)(2,1)} collective-permute-done((bf16[16,4,8,128]{3,2,1,0:T(8,128)(2,1)}, bf16[16,4,8,128]{3,2,1,0:T(8,128)(2,1)}, u32[]{:S(2)}, u32[]{:S(2)}) %collective-permute-start.9) | collective-permute-done | bytes 131104 | tf_op jit(solution)/shard_map/cond/branch_1_fun/ppermute | solution.py:427
  112.1 0.9 reshape.165
  113.1 0.8 fusion.8.amp
  113.8 9.7 %all-to-all-done.3.left_cut.right_cut = bf16[16,4,96,128]{3,2,1,0:T(8,128)(2,1)} async-done(((bf16[16,4,96,128]{3,2,1,0:T(8,128)(2,1)}), bf16[16,4,96,128]{3,2,1,0:T(8,128)(2,1)}, u32[]{:S(2)}, u32[]{:S(2)}) %all-to-all-start.3) | async-done | bytes 1572896 | tf_op jit(solution)/shard_map/cond/branch_1_fun/all_to_all | solution.py:479
  123.5 0.0 copy-done.3
  123.5 10.8 %ladder.3 = bf16[32,4,8,128]{3,2,1,0:T(8,128)(2,1)S(1)} custom-call(s32[8,4]{1,0:T(8,128)S(1)} %get-tuple-element.35.plan, bf16[8,192,1024]{2,1,0:T(8,128)(2,1)S(1)} %copy-done.3, bf16[16,4,96,128]{3,2,1,0:T(8,128)(2,1)} %all-to-all-done.3.left_cut.right_cut, bf16[8,192,1024]{2,1,0:T(8,128)(2,1)S(1)} %copy-done.3, ...), custom_call_target="tpu_custom_call" | custom-call | tf_op jit(solution)/shard_map/cond/branch_1_fun/ladder/pallas_call | solution.py:146
  134.3 24.1 %all_to_all.31.pieces = bf16[32,4,8,128]{3,2,1,0:T(8,128)(2,1)} all-to-all(bf16[32,4,8,128]{3,2,1,0:T(8,128)(2,1)S(1)} %get-tuple-element.50), channel_id=1, replica_groups=mesh['group'=16,'shard'=32] {'shard'}, dimensions={0} | all-to-all | bytes 524288 | tf_op jit(solution)/shard_map/all_to_all | solution.py:497
  158.4 1.7 combine.1
  160.0 22.9 %all_to_all.32 = f32[32,8,128]{2,1,0:T(8,128)} all-to-all(f32[32,8,128]{2,1,0:T(8,128)} %combine.1), channel_id=1, replica_groups=mesh['group'=16,'shard'=32] {'group'}, dimensions={0} | all-to-all | bytes 262144 | tf_op jit(solution)/shard_map/all_to_all | solution.py:499
  182.9 1.6 owned.1
  (10 shorter events, 0.2 us)
Async XLA Ops:
  1.7 20.1 %all-to-all-start.4 = ((bf16[16,5,8,128]{3,2,1,0:T(8,128)(2,1)}), bf16[16,5,8,128]{3,2,1,0:T(8,128)(2,1)S(1)}, u32[]{:S(2)}, u32[]{:S(2)}) async-start(bf16[16,5,8,128]{3,2,1,0:T(8,128)(2,1)} %facts.1), calls=%async_computation.4 | async-start | bytes 327680 | tf_op jit(solution)/shard_map/all_to_all | solution.py:466
  34.5 42.5 %all-to-all-start.2 = ((bf16[16,4,96,128]{3,2,1,0:T(8,128)(2,1)}), bf16[16,4,96,128]{3,2,1,0:T(8,128)(2,1)S(1)}, u32[]{:S(2)}, u32[]{:S(2)}) async-start(bf16[16,4,96,128]{3,2,1,0:T(8,128)(2,1)} %leaving_pieces.3), calls=%async_computation.2 | async-start | bytes 3145728 | tf_op jit(solution)/shard_map/cond/branch_1_fun/all_to_all | solution.py:474
  39.3 3.1 %collective-permute-start.5 = (bf16[1,4,8,128]{3,2,1,0:T(8,128)(2,1)S(1)}, bf16[1,4,8,128]{3,2,1,0:T(8,128)(2,1)S(1)}, u32[]{:S(2)}, u32[]{:S(2)}) collective-permute-start(bf16[1,4,8,128]{3,2,1,0:T(8,128)(2,1)S(1)} %bitcast.46), channel_id=1, source_target_pairs={{0,1},{1,0},{2,3},{3,2},{4,5},{5,4},{6,7},{7,6},{8,9},{9,8},{10,11... | collective-permute-start | bytes 24584 | tf_op jit(solution)/shard_map/cond/branch_1_fun/ppermute | solution.py:427
  42.4 6.0 %collective-permute-start.6 = (bf16[2,4,8,128]{3,2,1,0:T(8,128)(2,1)S(1)}, bf16[2,4,8,128]{3,2,1,0:T(8,128)(2,1)S(1)}, u32[]{:S(2)}, u32[]{:S(2)}) collective-permute-start(bf16[2,4,8,128]{3,2,1,0:T(8,128)(2,1)S(1)} %maximum_select_fusion.11), channel_id=1, source_target_pairs={{0,2},{1,3},{2,0},{3,1},{4,6},{5,7},{6,4},{7,5},{8,10},{9,11},{10,... | collective-permute-start | bytes 49160 | tf_op jit(solution)/shard_map/cond/branch_1_fun/ppermute | solution.py:427
  48.4 8.3 %collective-permute-start.7 = (bf16[4,4,8,128]{3,2,1,0:T(8,128)(2,1)S(1)}, bf16[4,4,8,128]{3,2,1,0:T(8,128)(2,1)S(1)}, u32[]{:S(2)}, u32[]{:S(2)}) collective-permute-start(bf16[4,4,8,128]{3,2,1,0:T(8,128)(2,1)S(1)} %maximum_select_fusion.10), channel_id=1, source_target_pairs={{0,4},{1,5},{2,6},{3,7},{4,0},{5,1},{6,2},{7,3},{8,12},{9,13},{10,... | collective-permute-start | bytes 98312 | tf_op jit(solution)/shard_map/cond/branch_1_fun/ppermute | solution.py:427
  78.8 44.7 %copy-start.3 = (bf16[8,192,1024]{2,1,0:T(8,128)(2,1)S(1)}, bf16[8,192,1024]{2,1,0:T(8,128)(2,1)}, u32[]{:S(2)}) copy-start(bf16[8,192,1024]{2,1,0:T(8,128)(2,1)} %get-tuple-element.36.factors.left_whole.right_whole) | copy-start | bytes 9437188 | tf_op jit(solution)/shard_map/cond
  78.8 44.7 %all-to-all-start.3 = ((bf16[16,4,96,128]{3,2,1,0:T(8,128)(2,1)}), bf16[16,4,96,128]{3,2,1,0:T(8,128)(2,1)}, u32[]{:S(2)}, u32[]{:S(2)}) async-start(bf16[16,4,96,128]{3,2,1,0:T(8,128)(2,1)} %dealt_pieces.3), calls=%async_computation.3 | async-start | bytes 3145728 | tf_op jit(solution)/shard_map/cond/branch_1_fun/all_to_all | solution.py:479
  84.2 13.5 %collective-permute-start.8 = (bf16[8,4,8,128]{3,2,1,0:T(8,128)(2,1)S(1)}, bf16[8,4,8,128]{3,2,1,0:T(8,128)(2,1)S(1)}, u32[]{:S(2)}, u32[]{:S(2)}) collective-permute-start(bf16[8,4,8,128]{3,2,1,0:T(8,128)(2,1)S(1)} %maximum_select_fusion.9), channel_id=1, source_target_pairs={{0,8},{1,9},{2,10},{3,11},{4,12},{5,13},{6,14},{7,15},{8,0},{9,1},... | collective-permute-start | bytes 196616 | tf_op jit(solution)/shard_map/cond/branch_1_fun/ppermute | solution.py:427
  98.4 13.7 %collective-permute-start.9 = (bf16[16,4,8,128]{3,2,1,0:T(8,128)(2,1)}, bf16[16,4,8,128]{3,2,1,0:T(8,128)(2,1)}, u32[]{:S(2)}, u32[]{:S(2)}) collective-permute-start(bf16[16,4,8,128]{3,2,1,0:T(8,128)(2,1)} %maximum_select_fusion.8), channel_id=1, source_target_pairs={{0,16},{1,17},{2,18},{3,19},{4,20},{5,21},{6,22},{7,23},{8,24},{9,... | collective-permute-start | bytes 393224 | tf_op jit(solution)/shard_map/cond/branch_1_fun/ppermute | solution.py:427

commit v8 on v7

--- a/solution.py
+++ b/solution.py
@@ -214,7 +214,7 @@
 
 
 def assign_kernel(
-    me, table, send, pick, plan, balanced,
+    me, table, factors, send, pick, plan, balanced, ready,
     compute, other, compute_block, other_block, load, sent, uses, filled, slots, where_sent,
 ):
     groups = table.shape[0]
@@ -351,25 +351,34 @@
     def _():
         lax.fori_loop(0, groups, deal_at_helper, 0)
 
-
-def assign(me, table):
+    pieces, count, rows, _ = ready.shape
+    for i in range(count):
+        for piece in range(pieces):
+            half, part = divmod(piece, factors.shape[2] // LANES)
+            ready[piece, i] = factors[send[i], half * rows : (half + 1) * rows, part * LANES : (part + 1) * LANES]
+
+
+def assign(me, table, factors):
     groups = table.shape[0]
-    smem = pl.BlockSpec(memory_space=pltpu.SMEM)
+    smem, vmem = pl.BlockSpec(memory_space=pltpu.SMEM), pl.BlockSpec(memory_space=pltpu.VMEM)
+    _, rows, width = factors.shape
     one = lambda n: pltpu.SMEM((n,), jnp.int32)
     tasks = groups * TASKS
     return pl.pallas_call(
         assign_kernel,
-        in_specs=[smem, smem],
-        out_specs=[smem] * 4,
+        in_specs=[smem, smem, vmem],
+        out_specs=[smem] * 4 + [vmem],
         out_shape=[
             jax.ShapeDtypeStruct((2 * FPG,), jnp.int32),
             jax.ShapeDtypeStruct(((groups + 1) * FPG,), jnp.int32),
             jax.ShapeDtypeStruct((2 * FAST, 4), jnp.int32),
             jax.ShapeDtypeStruct((1,), jnp.int32),
+            jax.ShapeDtypeStruct((groups, FAST, rows * width // LANES // groups, LANES), factors.dtype),
         ],
         scratch_shapes=[one(tasks)] * 4 + [one(groups)] * 2 + [one(groups * FPG)] + [one(groups)] * 2 + [one(groups * FPG)],
+        compiler_params=pltpu.CompilerParams(vmem_limit_bytes=12 << 20),
         name="assign",
-    )(me, table)
+    )(me, table, factors)
 
 
 def leave_kernel(send, factors, out, held, arrive):
@@ -467,10 +476,12 @@
     return held.reshape(groups * (tiles + 1), *held.shape[2:]), held[:, tiles, 0].astype(jnp.int32)
 
 
-def contributions(blocks_sent, slots, factors, amp_rows, send, pick, plan):
+def contributions(blocks_sent, slots, factors, ready, amp_rows, send, pick, plan):
     groups = lax.axis_size("group")
     width = factors.shape[2]
-    leaving = leaving_pieces(send, factors, blocks_sent, groups)
+    leaving = ready
+    if blocks_sent > FAST:
+        leaving = leaving_pieces(send, factors, blocks_sent, groups)
     held = lax.all_to_all(leaving, "group", split_axis=0, concat_axis=0, tiled=True)
     chosen = amp_rows.at[plan[:FAST, 2]].get(mode="promise_in_bounds")
     amps = spread(chosen[None], "shard", (1, 2, 4))
@@ -486,8 +497,8 @@
     groups = lax.axis_size("group")
     amp_rows, table = group_facts(amplitudes, factor_route, amp_route, task_list, target_tile)
     me = lax.axis_index("group").astype(jnp.int32).reshape(1)
-    send, pick, plan, balanced = assign(me, table)
-    operands = (factors, amp_rows, send, pick, plan)
+    send, pick, plan, balanced, ready = assign(me, table, factors)
+    operands = (factors, ready, amp_rows, send, pick, plan)
     parts = lax.cond(
         balanced[0] == 1,
         functools.partial(contributions, FAST, FAST),

time: 185 us -> 182 us (0.984)
  blocking collectives: 47 us -> 39.4 us
  Pallas kernels: 29 us -> 34.9 us
    all_to_all x1, blocking collectives: 22.9 us -> 15.3 us  [body(): lax.all_to_all(returns, 'group', split_axis=0, concat_axis=0, tiled=True)]
    pallas_call x1, Pallas kernels: 10.8 us -> 17.9 us  [ladder(): pl.pallas_call(ladder_kernel, grid_spec=pltpu.PrefetchScalarGridSpec(num_...]
    pallas_call x2 -> x1, Pallas kernels: 11.4 us -> 10.1 us  [assign(): pl.pallas_call(assign_kernel, in_specs=[smem, smem, vmem], out_specs=[sme...]
where the time goes in v8:
time: 182 us
  waiting for transfers between devices  57.7 us (32%)
  starting transfers between devices  45.4 us (25%)
  blocking collectives  39.4 us (22%)
  Pallas kernels  34.9 us (19%)
  other arithmetic  2.43 us (1%)
    ppermute x5, starting transfers between devices, spread(): other = lax.ppermute(held, axis, [(i, i ^ bit) for i in range(members)])  26 us
    all_to_all x1, blocking collectives, body(): lax.all_to_all(parts, 'shard', split_axis=0, concat_axis=0, tiled=True)  24.1 us
    all_to_all x1, waiting for transfers between devices, contributions(): lax.all_to_all(leaving, 'group', split_axis=0, concat_axis=0, tiled=True)  20.4 us
    pallas_call x1, Pallas kernels, ladder(): pl.pallas_call(ladder_kernel, grid_spec=pltpu.PrefetchScalarGridSpec(num_...  17.9 us
    ppermute x5, waiting for transfers between devices, spread(): other = lax.ppermute(held, axis, [(i, i ^ bit) for i in range(members)])  17.2 us
    all_to_all x1, blocking collectives, body(): lax.all_to_all(returns, 'group', split_axis=0, concat_axis=0, tiled=True)  15.3 us
    pallas_call x1, Pallas kernels, assign(): pl.pallas_call(assign_kernel, in_specs=[smem, smem, vmem], out_specs=[sme...  10.1 us
    all_to_all x1, waiting for transfers between devices, group_facts(): lax.all_to_all(facts, 'group', split_axis=0, concat_axis=0, tiled=True)  10.1 us
  transfers between devices with their start and end apart: 8, of which 8 were waited for; matrix products, arithmetic and copies ran while one was open for 2% of the time, Pallas kernels for 0%

profile of v8, /device:TPU:8, one launch (start us, length us, event | category | flops | bytes accessed | tf_op | source)
XLA Modules:
  0.0 182.3 jit_solution(12010172900096154073)
XLA Ops:
  0.0 1.7 facts.1
  1.7 10.0 %all-to-all-start.4 = ((bf16[16,5,8,128]{3,2,1,0:T(8,128)(2,1)}), bf16[16,5,8,128]{3,2,1,0:T(8,128)(2,1)S(1)}, u32[]{:S(2)}, u32[]{:S(2)}) async-start(bf16[16,5,8,128]{3,2,1,0:T(8,128)(2,1)} %facts.1), calls=%async_computation.4 | async-start | bytes 327680 | tf_op jit(solution)/shard_map/all_to_all | solution.py:475
  11.8 10.1 %all-to-all-done.4 = bf16[16,5,8,128]{3,2,1,0:T(8,128)(2,1)S(1)} async-done(((bf16[16,5,8,128]{3,2,1,0:T(8,128)(2,1)}), bf16[16,5,8,128]{3,2,1,0:T(8,128)(2,1)S(1)}, u32[]{:S(2)}, u32[]{:S(2)}) %all-to-all-start.4) | async-done | bytes 163872 | tf_op jit(solution)/shard_map/all_to_all | solution.py:475
  21.9 10.1 %assign.1 = (s32[16]{0:T(128)S(1)}, s32[136]{0:T(256)S(1)}, s32[8,4]{1,0:T(8,128)S(1)}, s32[1]{0:T(128)}, bf16[16,4,96,128]{3,2,1,0:T(8,128)(2,1)}) custom-call(s32[1]{0:T(128)} %bitcast.10.me, s32[16,128]{1,0:T(8,128)S(1)} %fusion.16.table, bf16[8,192,1024]{2,1,0:T(8,128)(2,1)} %factors.1), custom_call_target="tpu_custom_call" | custom-call | tf_op jit(solution)/shard_map/assign/pallas_call | solution.py:367
  32.7 106.9 %conditional.1 = (bf16[32,4,8,128]{3,2,1,0:T(8,128)(2,1)S(1)}) conditional(s32[]{:T(128)} %bitcast.14, (s32[16]{0:T(128)S(1)}, bf16[8,192,1024]{2,1,0:T(8,128)(2,1)}, s32[8,4]{1,0:T(8,128)S(1)}, bf16[80,8,128]{2,1,0:T(8,128)(2,1)S(1)}, s32[136]{0:T(256)S(1)}) %tuple.17, (bf16[16,4,96,128]{3,2,1,0:T(8,128)(2,1)}, s32[8,4]{1,0:T(8,128)S(1)}, ...), branch_computations={%region_0.1_spmd, %region_1.2_spmd} | conditional | flops 2279192 | bytes 54352412 | solution.py:502
  32.7 4.0 %all-to-all-start.2 = ((bf16[16,4,96,128]{3,2,1,0:T(8,128)(2,1)}), bf16[16,4,96,128]{3,2,1,0:T(8,128)(2,1)S(1)}, u32[]{:S(2)}, u32[]{:S(2)}) async-start(bf16[16,4,96,128]{3,2,1,0:T(8,128)(2,1)} %get-tuple-element.38), calls=%async_computation.2 | async-start | bytes 3145728 | tf_op jit(solution)/shard_map/cond/branch_1_fun/all_to_all | solution.py:485
  36.6 0.2 fusion.10
  36.8 0.6 gather_fusion.1
  37.4 1.9 %collective-permute-start.5 = (bf16[1,4,8,128]{3,2,1,0:T(8,128)(2,1)S(1)}, bf16[1,4,8,128]{3,2,1,0:T(8,128)(2,1)S(1)}, u32[]{:S(2)}, u32[]{:S(2)}) collective-permute-start(bf16[1,4,8,128]{3,2,1,0:T(8,128)(2,1)S(1)} %bitcast.46), channel_id=1, source_target_pairs={{0,1},{1,0},{2,3},{3,2},{4,5},{5,4},{6,7},{7,6},{8,9},{9,8},{10,11... | collective-permute-start | bytes 24584 | tf_op jit(solution)/shard_map/cond/branch_1_fun/ppermute | solution.py:436
  39.3 1.1 collective-permute-done.5
  40.5 4.3 %collective-permute-start.6 = (bf16[2,4,8,128]{3,2,1,0:T(8,128)(2,1)S(1)}, bf16[2,4,8,128]{3,2,1,0:T(8,128)(2,1)S(1)}, u32[]{:S(2)}, u32[]{:S(2)}) collective-permute-start(bf16[2,4,8,128]{3,2,1,0:T(8,128)(2,1)S(1)} %maximum_select_fusion.11), channel_id=1, source_target_pairs={{0,2},{1,3},{2,0},{3,1},{4,6},{5,7},{6,4},{7,5},{8,10},{9,11},{10,... | collective-permute-start | bytes 49160 | tf_op jit(solution)/shard_map/cond/branch_1_fun/ppermute | solution.py:436
  44.7 1.7 collective-permute-done.6
  46.5 6.1 %collective-permute-start.7 = (bf16[4,4,8,128]{3,2,1,0:T(8,128)(2,1)S(1)}, bf16[4,4,8,128]{3,2,1,0:T(8,128)(2,1)S(1)}, u32[]{:S(2)}, u32[]{:S(2)}) collective-permute-start(bf16[4,4,8,128]{3,2,1,0:T(8,128)(2,1)S(1)} %maximum_select_fusion.10), channel_id=1, source_target_pairs={{0,4},{1,5},{2,6},{3,7},{4,0},{5,1},{6,2},{7,3},{8,12},{9,13},{10,... | collective-permute-start | bytes 98312 | tf_op jit(solution)/shard_map/cond/branch_1_fun/ppermute | solution.py:436
  52.6 2.2 %collective-permute-done.7 = bf16[4,4,8,128]{3,2,1,0:T(8,128)(2,1)S(1)} collective-permute-done((bf16[4,4,8,128]{3,2,1,0:T(8,128)(2,1)S(1)}, bf16[4,4,8,128]{3,2,1,0:T(8,128)(2,1)S(1)}, u32[]{:S(2)}, u32[]{:S(2)}) %collective-permute-start.7) | collective-permute-done | bytes 32800 | tf_op jit(solution)/shard_map/cond/branch_1_fun/ppermute | solution.py:436
  54.8 20.4 %all-to-all-done.2 = bf16[16,4,96,128]{3,2,1,0:T(8,128)(2,1)S(1)} async-done(((bf16[16,4,96,128]{3,2,1,0:T(8,128)(2,1)}), bf16[16,4,96,128]{3,2,1,0:T(8,128)(2,1)S(1)}, u32[]{:S(2)}, u32[]{:S(2)}) %all-to-all-start.2) | async-done | bytes 1572896 | tf_op jit(solution)/shard_map/cond/branch_1_fun/all_to_all | solution.py:485
  75.2 1.8 dealt_pieces.3
  77.0 0.0 copy-start.3
  77.0 5.4 %all-to-all-start.3 = ((bf16[16,4,96,128]{3,2,1,0:T(8,128)(2,1)}), bf16[16,4,96,128]{3,2,1,0:T(8,128)(2,1)}, u32[]{:S(2)}, u32[]{:S(2)}) async-start(bf16[16,4,96,128]{3,2,1,0:T(8,128)(2,1)} %dealt_pieces.3), calls=%async_computation.3 | async-start | bytes 3145728 | tf_op jit(solution)/shard_map/cond/branch_1_fun/all_to_all | solution.py:490
  82.4 10.9 %collective-permute-start.8 = (bf16[8,4,8,128]{3,2,1,0:T(8,128)(2,1)S(1)}, bf16[8,4,8,128]{3,2,1,0:T(8,128)(2,1)S(1)}, u32[]{:S(2)}, u32[]{:S(2)}) collective-permute-start(bf16[8,4,8,128]{3,2,1,0:T(8,128)(2,1)S(1)} %maximum_select_fusion.9), channel_id=1, source_target_pairs={{0,8},{1,9},{2,10},{3,11},{4,12},{5,13},{6,14},{7,15},{8,0},{9,1},... | collective-permute-start | bytes 196616 | tf_op jit(solution)/shard_map/cond/branch_1_fun/ppermute | solution.py:436
  93.3 2.5 %collective-permute-done.8 = bf16[8,4,8,128]{3,2,1,0:T(8,128)(2,1)S(1)} collective-permute-done((bf16[8,4,8,128]{3,2,1,0:T(8,128)(2,1)S(1)}, bf16[8,4,8,128]{3,2,1,0:T(8,128)(2,1)S(1)}, u32[]{:S(2)}, u32[]{:S(2)}) %collective-permute-start.8) | collective-permute-done | bytes 65568 | tf_op jit(solution)/shard_map/cond/branch_1_fun/ppermute | solution.py:436
  95.9 0.7 maximum_select_fusion.8
  96.5 2.9 %collective-permute-start.9 = (bf16[16,4,8,128]{3,2,1,0:T(8,128)(2,1)}, bf16[16,4,8,128]{3,2,1,0:T(8,128)(2,1)}, u32[]{:S(2)}, u32[]{:S(2)}) collective-permute-start(bf16[16,4,8,128]{3,2,1,0:T(8,128)(2,1)} %maximum_select_fusion.8), channel_id=1, source_target_pairs={{0,16},{1,17},{2,18},{3,19},{4,20},{5,21},{6,22},{7,23},{8,24},{9,... | collective-permute-start | bytes 393224 | tf_op jit(solution)/shard_map/cond/branch_1_fun/ppermute | solution.py:436
  99.4 0.8 fusion.9.swap
  100.3 9.6 %collective-permute-done.9 = bf16[16,4,8,128]{3,2,1,0:T(8,128)(2,1)} collective-permute-done((bf16[16,4,8,128]{3,2,1,0:T(8,128)(2,1)}, bf16[16,4,8,128]{3,2,1,0:T(8,128)(2,1)}, u32[]{:S(2)}, u32[]{:S(2)}) %collective-permute-start.9) | collective-permute-done | bytes 131104 | tf_op jit(solution)/shard_map/cond/branch_1_fun/ppermute | solution.py:436
  109.9 0.9 reshape.165
  110.9 0.8 fusion.8.amp
  111.7 10.0 %all-to-all-done.3.left_cut.right_cut = bf16[16,4,96,128]{3,2,1,0:T(8,128)(2,1)} async-done(((bf16[16,4,96,128]{3,2,1,0:T(8,128)(2,1)}), bf16[16,4,96,128]{3,2,1,0:T(8,128)(2,1)}, u32[]{:S(2)}, u32[]{:S(2)}) %all-to-all-start.3) | async-done | bytes 1572896 | tf_op jit(solution)/shard_map/cond/branch_1_fun/all_to_all | solution.py:490
  121.7 0.0 copy-done.3
  121.7 17.9 %ladder.3 = bf16[32,4,8,128]{3,2,1,0:T(8,128)(2,1)S(1)} custom-call(s32[8,4]{1,0:T(8,128)S(1)} %get-tuple-element.35.plan, bf16[8,192,1024]{2,1,0:T(8,128)(2,1)S(1)} %copy-done.3, bf16[16,4,96,128]{3,2,1,0:T(8,128)(2,1)} %all-to-all-done.3.left_cut.right_cut, bf16[8,192,1024]{2,1,0:T(8,128)(2,1)S(1)} %copy-done.3, ...), custom_call_target="tpu_custom_call" | custom-call | tf_op jit(solution)/shard_map/cond/branch_1_fun/ladder/pallas_call | solution.py:146
  139.6 24.1 %all_to_all.31.pieces = bf16[32,4,8,128]{3,2,1,0:T(8,128)(2,1)} all-to-all(bf16[32,4,8,128]{3,2,1,0:T(8,128)(2,1)S(1)} %get-tuple-element.52), channel_id=1, replica_groups=mesh['group'=16,'shard'=32] {'shard'}, dimensions={0} | all-to-all | bytes 524288 | tf_op jit(solution)/shard_map/all_to_all | solution.py:508
  163.7 1.7 combine.1
  165.4 15.3 %all_to_all.32 = f32[32,8,128]{2,1,0:T(8,128)} all-to-all(f32[32,8,128]{2,1,0:T(8,128)} %combine.1), channel_id=1, replica_groups=mesh['group'=16,'shard'=32] {'group'}, dimensions={0} | all-to-all | bytes 262144 | tf_op jit(solution)/shard_map/all_to_all | solution.py:510
  180.7 1.6 owned.1
  (11 shorter events, 0.2 us)
Async XLA Ops:
  1.7 20.1 %all-to-all-start.4 = ((bf16[16,5,8,128]{3,2,1,0:T(8,128)(2,1)}), bf16[16,5,8,128]{3,2,1,0:T(8,128)(2,1)S(1)}, u32[]{:S(2)}, u32[]{:S(2)}) async-start(bf16[16,5,8,128]{3,2,1,0:T(8,128)(2,1)} %facts.1), calls=%async_computation.4 | async-start | bytes 327680 | tf_op jit(solution)/shard_map/all_to_all | solution.py:475
  32.7 42.5 %all-to-all-start.2 = ((bf16[16,4,96,128]{3,2,1,0:T(8,128)(2,1)}), bf16[16,4,96,128]{3,2,1,0:T(8,128)(2,1)S(1)}, u32[]{:S(2)}, u32[]{:S(2)}) async-start(bf16[16,4,96,128]{3,2,1,0:T(8,128)(2,1)} %get-tuple-element.38), calls=%async_computation.2 | async-start | bytes 3145728 | tf_op jit(solution)/shard_map/cond/branch_1_fun/all_to_all | solution.py:485
  37.4 3.1 %collective-permute-start.5 = (bf16[1,4,8,128]{3,2,1,0:T(8,128)(2,1)S(1)}, bf16[1,4,8,128]{3,2,1,0:T(8,128)(2,1)S(1)}, u32[]{:S(2)}, u32[]{:S(2)}) collective-permute-start(bf16[1,4,8,128]{3,2,1,0:T(8,128)(2,1)S(1)} %bitcast.46), channel_id=1, source_target_pairs={{0,1},{1,0},{2,3},{3,2},{4,5},{5,4},{6,7},{7,6},{8,9},{9,8},{10,11... | collective-permute-start | bytes 24584 | tf_op jit(solution)/shard_map/cond/branch_1_fun/ppermute | solution.py:436
  40.5 6.0 %collective-permute-start.6 = (bf16[2,4,8,128]{3,2,1,0:T(8,128)(2,1)S(1)}, bf16[2,4,8,128]{3,2,1,0:T(8,128)(2,1)S(1)}, u32[]{:S(2)}, u32[]{:S(2)}) collective-permute-start(bf16[2,4,8,128]{3,2,1,0:T(8,128)(2,1)S(1)} %maximum_select_fusion.11), channel_id=1, source_target_pairs={{0,2},{1,3},{2,0},{3,1},{4,6},{5,7},{6,4},{7,5},{8,10},{9,11},{10,... | collective-permute-start | bytes 49160 | tf_op jit(solution)/shard_map/cond/branch_1_fun/ppermute | solution.py:436
  46.5 8.3 %collective-permute-start.7 = (bf16[4,4,8,128]{3,2,1,0:T(8,128)(2,1)S(1)}, bf16[4,4,8,128]{3,2,1,0:T(8,128)(2,1)S(1)}, u32[]{:S(2)}, u32[]{:S(2)}) collective-permute-start(bf16[4,4,8,128]{3,2,1,0:T(8,128)(2,1)S(1)} %maximum_select_fusion.10), channel_id=1, source_target_pairs={{0,4},{1,5},{2,6},{3,7},{4,0},{5,1},{6,2},{7,3},{8,12},{9,13},{10,... | collective-permute-start | bytes 98312 | tf_op jit(solution)/shard_map/cond/branch_1_fun/ppermute | solution.py:436
  77.0 44.7 %copy-start.3 = (bf16[8,192,1024]{2,1,0:T(8,128)(2,1)S(1)}, bf16[8,192,1024]{2,1,0:T(8,128)(2,1)}, u32[]{:S(2)}) copy-start(bf16[8,192,1024]{2,1,0:T(8,128)(2,1)} %get-tuple-element.36.left_whole.right_whole) | copy-start | bytes 9437188 | tf_op jit(solution)/shard_map/cond
  77.0 44.7 %all-to-all-start.3 = ((bf16[16,4,96,128]{3,2,1,0:T(8,128)(2,1)}), bf16[16,4,96,128]{3,2,1,0:T(8,128)(2,1)}, u32[]{:S(2)}, u32[]{:S(2)}) async-start(bf16[16,4,96,128]{3,2,1,0:T(8,128)(2,1)} %dealt_pieces.3), calls=%async_computation.3 | async-start | bytes 3145728 | tf_op jit(solution)/shard_map/cond/branch_1_fun/all_to_all | solution.py:490
  82.4 13.5 %collective-permute-start.8 = (bf16[8,4,8,128]{3,2,1,0:T(8,128)(2,1)S(1)}, bf16[8,4,8,128]{3,2,1,0:T(8,128)(2,1)S(1)}, u32[]{:S(2)}, u32[]{:S(2)}) collective-permute-start(bf16[8,4,8,128]{3,2,1,0:T(8,128)(2,1)S(1)} %maximum_select_fusion.9), channel_id=1, source_target_pairs={{0,8},{1,9},{2,10},{3,11},{4,12},{5,13},{6,14},{7,15},{8,0},{9,1},... | collective-permute-start | bytes 196616 | tf_op jit(solution)/shard_map/cond/branch_1_fun/ppermute | solution.py:436
  96.5 13.4 %collective-permute-start.9 = (bf16[16,4,8,128]{3,2,1,0:T(8,128)(2,1)}, bf16[16,4,8,128]{3,2,1,0:T(8,128)(2,1)}, u32[]{:S(2)}, u32[]{:S(2)}) collective-permute-start(bf16[16,4,8,128]{3,2,1,0:T(8,128)(2,1)} %maximum_select_fusion.8), channel_id=1, source_target_pairs={{0,16},{1,17},{2,18},{3,19},{4,20},{5,21},{6,22},{7,23},{8,24},{9,... | collective-permute-start | bytes 393224 | tf_op jit(solution)/shard_map/cond/branch_1_fun/ppermute | solution.py:436
